TPU v7x, 256 devices: a whole 4x4x8 slice. The times are simulated.
256 devices in a mesh: ga: 64 (over z, y, x_hi), gp: 4 (over x_lo, core).
Axes of the slice: x: 4 (x_hi: 2, x_lo: 2; x = x_hi * 2 + x_lo), y: 4, z: 8, core: 2. Of those that a mesh axis runs over, the one named last changes fastest.
Arguments:
- screened: bfloat16 [16384, 65536], P('ga', 'gp'), may hold values from -0.0234375 to 0.0234375
- valence: bfloat16 [64, 32, 65536], P('ga', None, 'gp'), may hold values from -6 to 6
- conduction: bfloat16 [1024, 16384], P(None, 'ga'), may hold values from -0.125 to 0.125
- owner: int32 [6], replicated, may hold values from 0 to 63
Outputs:
- kernel: float32 [1024, 192], P('ga', 'gp')
Inputs may be any that keep to these rules, and one draw needn't show every extreme that they name: owner[b] is the slot of valence, along its first dimension, that holds batch b.
All inputs are finite; a program needn't handle non-finite values.
Results may differ from a plain program's by a relative error of at most 0.0003.
Values may be sent and summed in bfloat16 or wider, within the bound.
No kernel may reach another device: no remote copies, remote signals or barrier semaphores. Data moves between devices by JAX's collectives and lax.ppermute only.
A program may use at most 64 MiB of HBM per device.

v0:
```python
import jax
import jax.numpy as jnp
from jax import lax
from jax.sharding import PartitionSpec as P


def spread(block, axis, source):
    block = jnp.where(lax.axis_index(axis) == source, block, jnp.zeros_like(block))
    return lax.psum(block, axis)


def body(screened, valence, conduction, owner):
    own_slot = valence[0]
    dims = (((1,), (1,)), ((), ()))
    pieces = []
    for batch in range(owner.shape[0]):
        chosen = spread(own_slot, "ga", owner[batch])
        pieces.append(lax.dot_general(screened, chosen, dims, preferred_element_type=jnp.float32))
    partial_value = jnp.concatenate(pieces, axis=1)
    cond_full = conduction.astype(jnp.float32)
    term = jnp.dot(cond_full, partial_value, precision=lax.Precision.HIGHEST)
    columns = lax.psum_scatter(term, "gp", scatter_dimension=1, tiled=True)
    kernel = lax.psum_scatter(columns, "ga", scatter_dimension=0, tiled=True)
    return kernel


def solution(mesh):
    placed = (P("ga", "gp"), P("ga", None, "gp"), P(None, "ga"), P())
    return jax.shard_map(body, mesh=mesh, in_specs=placed, out_specs=P("ga", "gp"), check_vma=False)
```

profile of v0, /device:TPU:2, one launch (start us, length us, event | category | flops | bytes accessed | tf_op | source)
XLA Modules:
  0.0 1154.6 jit_solution(2355596265020691896)
XLA Ops:
  6.5 0.0 copy-start
  6.5 0.0 all-reduce.3.cloned.1.call-start
  6.5 1.6 fusion.6
  11.9 4.0 select_bitcast_fusion
  15.8 0.0 all-reduce.3.cloned.1.call-update
  15.9 0.0 reduce-scatter.5.cloned.1.call-start
  15.9 722.8 %all-reduce.3.cloned.1.call-done = (bf16[32,16384]{1,0:T(8,128)(2,1)}, bf16[32,16384]{1,0:T(8,128)(2,1)}, bf16[32,16384]{1,0:T(8,128)(2,1)}, bf16[32,16384]{1,0:...) async-done(((bf16[32,16384]{1,0:T(8,128)(2,1)}, bf16[32,16384]{1,0:T(8,128)(2,1)}, bf16[32,16384]{1,0:T(8,128)(2,1)}, bf16[32,16384]{1,0:T(8,128)(2,1)}, ...) | async-done | bytes 6291472 | tf_op jit(solution)/shard_map/psum | solution.py:9
  738.7 0.0 copy-start.5
  738.7 0.0 slice-start
  738.7 0.0 copy-start.4
  738.7 6.5 fusion.5
  745.2 0.0 copy-done.5
  745.2 0.0 slice-start.1
  745.2 0.0 copy-start.3
  745.2 6.2 fusion.4
  751.4 0.0 slice-done
  751.4 0.0 copy-done.4
  751.4 0.0 slice-done.1
  751.4 0.0 copy-start.2
  751.4 2.6 fusion.3
  754.0 0.0 copy-done.3
  754.1 0.0 copy-start.1
  754.1 2.6 fusion.2
  756.7 0.0 copy-done.2
  756.7 2.6 fusion.1
  759.3 0.0 copy-done.1
  759.3 2.6 fusion
  761.9 0.0 copy-done
  761.9 1.6 convolution_bitcast_fusion
  763.5 0.0 reduce-scatter.5.cloned.1.call-update
  763.6 0.0 reduce-scatter.7.cloned.1.call-start
  763.6 17.5 %reduce-scatter.5.cloned.1.call-done = f32[1024,48]{0,1:T(8,128)} async-done(((f32[1024,192]{0,1:T(8,128)}), f32[1024,48]{0,1:T(8,128)}) %reduce-scatter.5.cloned.1.call-update) | async-done | bytes 196624 | tf_op jit(solution)/shard_map/reduce_scatter | solution.py:22
  781.1 1.9 copy.7
  783.0 0.0 reduce-scatter.7.cloned.1.call-update
  783.0 365.1 %reduce-scatter.7.cloned.1.call-done = f32[16,48]{1,0:T(8,128)} async-done(((f32[1024,48]{1,0:T(8,128)}), f32[16,48]{1,0:T(8,128)}) %reduce-scatter.7.cloned.1.call-update) | async-done | bytes 3088 | tf_op jit(solution)/shard_map/reduce_scatter | solution.py:23
  (1 shorter events, 0.0 us)
Async XLA Ops:
  6.5 755.4 %copy-start = (bf16[1024,256]{1,0:T(8,128)(2,1)S(1)}, bf16[1024,256]{1,0:T(8,128)(2,1)}, u32[]{:S(2)}) copy-start(bf16[1024,256]{1,0:T(8,128)(2,1)} %param.6) | copy-start | bytes 1572868
  6.5 732.2 %all-reduce.3.cloned.1.call-start = ((), (), s32[]{:S(2)}) async-start(), calls=%async_computation.4 | async-start | bytes 12582912 | tf_op jit(solution)/shard_map/psum | solution.py:9
  15.9 765.2 %reduce-scatter.5.cloned.1.call-start = ((), (), s32[]{:S(2)}) async-start(), calls=%async_computation.2 | async-start | bytes 983040 | tf_op jit(solution)/shard_map/reduce_scatter | solution.py:22
  738.7 6.5 copy-start.5
  738.7 12.7 %slice-start = ((s8[8388608]{0:T(1024)(128)(4,1)}), s8[4194304]{0:T(1024)(128)(4,1)S(1)}, s32[]{:S(2)}) async-start(s8[8388608]{0:T(1024)(128)(4,1)} %bitcast.59), calls=%async_computation.5 | async-start | bytes 8388608
  738.7 12.7 %copy-start.4 = (bf16[32,16384]{1,0:T(8,128)(2,1)S(1)}, bf16[32,16384]{1,0:T(8,128)(2,1)}, u32[]{:S(2)}) copy-start(bf16[32,16384]{1,0:T(8,128)(2,1)} %get-tuple-element.7) | copy-start | bytes 3145732
  745.2 6.2 slice-start.1
  745.2 8.8 copy-start.3
  751.4 5.3 copy-start.2
  754.1 5.2 copy-start.1
  763.6 384.5 %reduce-scatter.7.cloned.1.call-start = ((), (), s32[]{:S(2)}) async-start(), calls=%async_computation.3 | async-start | bytes 532480 | tf_op jit(solution)/shard_map/reduce_scatter | solution.py:23
Sparse Core Ops, SparseCore 0:
  16.0 722.6 all-reduce.2
  763.7 17.3 reduce-scatter.4
  783.7 364.3 reduce-scatter.6
where the time goes:
time: 1150 us
  waiting for transfers between devices  1110 us (97%)
  matrix products  24.6 us (2%)
  between operations  17 us (1%)
    psum x1, waiting for transfers between devices, spread(): return lax.psum(block, axis)  723 us
    reduce_scatter x1, waiting for transfers between devices, body(): kernel = lax.psum_scatter(columns, 'ga', scatter_dimension=0, tiled=True)  365 us
    dot_general x6, matrix products, body(): lax.dot_general(screened, chosen, dims, preferred_element_type=jnp.float32)  23 us
  transfers between devices with their start and end apart: 3, of which 3 were waited for; matrix products, arithmetic and copies ran while one was open for 0% of the time, Pallas kernels for 0%

commit v1 on v0

v1 whole, which is shorter than its diff:
```python
import functools

import jax
import jax.numpy as jnp
from jax import lax
from jax.experimental import pallas as pl
from jax.experimental.pallas import tpu as pltpu
from jax.sharding import Mesh, PartitionSpec as P

NZ, NY, NX, NGP = 8, 4, 2, 4
K = 256
F32, BF16 = jnp.float32, jnp.bfloat16


def shift(x, axis, n, d):
    return lax.ppermute(x, axis, [(i, (i + d) % n) for i in range(n)])


def accumulate(offs_ref, w_ref, blocks, wbuf, sems, acc):
    flat = [(ref, i) for ref in blocks for i in range(ref.shape[0])]
    copies = []
    for n in range(len(flat)):
        column = pl.multiple_of(offs_ref[n], K)
        copy = pltpu.make_async_copy(w_ref.at[:, pl.ds(column, K)], wbuf.at[n], sems.at[n])
        copy.start()
        copies.append(copy)
    for n, (ref, i) in enumerate(flat):
        copies[n].wait()
        acc = acc + lax.dot_general(ref[i], wbuf[n], (((1,), (1,)), ((), ())), preferred_element_type=F32)
    return acc


def pair_kernel(n_blocks, first, offs_ref, w_ref, *refs):
    blocks, rest = refs[:n_blocks], refs[n_blocks:]
    if first:
        out_ref, wbuf, sems = rest
        acc = jnp.zeros(out_ref.shape, F32)
    else:
        acc_ref, out_ref, wbuf, sems = rest
        acc = acc_ref[...]
    out_ref[...] = accumulate(offs_ref, w_ref, blocks, wbuf, sems, acc)


def pair_call(w, blocks, offs, acc=None):
    n = sum(b.shape[0] for b in blocks)
    rows, g = blocks[0].shape[1], w.shape[0]
    vm = pl.BlockSpec(memory_space=pltpu.VMEM)
    args = [jnp.stack(offs).astype(jnp.int32), w, *blocks] + ([] if acc is None else [acc])
    return pl.pallas_call(
        functools.partial(pair_kernel, len(blocks), acc is None),
        out_shape=jax.ShapeDtypeStruct((rows, g), F32),
        in_specs=[pl.BlockSpec(memory_space=pltpu.SMEM), pl.BlockSpec(memory_space=pl.ANY)] + [vm] * (len(args) - 2),
        out_specs=vm,
        scratch_shapes=[pltpu.VMEM((n, g, K), BF16), pltpu.SemaphoreType.DMA((n,))],
        compiler_params=pltpu.CompilerParams(vmem_limit_bytes=32 << 20),
        cost_estimate=pl.CostEstimate(flops=2 * n * rows * g * K, bytes_accessed=n * (rows + g) * K * 2, transcendentals=0),
    )(*args)


def term_kernel(a_ref, b_ref, c_ref, d_ref, cond_ref, out_ref):
    total = (a_ref[...] + b_ref[...]) + (c_ref[...] + d_ref[...])
    rows = total.shape[0]
    hi = total.astype(BF16)
    rest = total - hi.astype(F32)
    mid = rest.astype(BF16)
    low = (rest - mid.astype(F32)).astype(BF16)
    stacked = jnp.concatenate([hi, mid, low], axis=0)
    prod = lax.dot_general(stacked, cond_ref[...], (((1,), (1,)), ((), ())), preferred_element_type=F32)
    term = prod[:rows] + (prod[rows:2 * rows] + prod[2 * rows:])
    width = out_ref.shape[2]
    for z in range(out_ref.shape[0]):
        out_ref[z] = term[:, z * width:(z + 1) * width]


def term_call(parts, cond):
    rows, nc = parts[0].shape[0], cond.shape[0]
    vm = pl.BlockSpec(memory_space=pltpu.VMEM)
    return pl.pallas_call(
        term_kernel,
        out_shape=jax.ShapeDtypeStruct((NZ, rows, nc // NZ), F32),
        in_specs=[vm] * 5,
        out_specs=vm,
        cost_estimate=pl.CostEstimate(flops=6 * rows * nc * cond.shape[1], bytes_accessed=nc * cond.shape[1] * 2, transcendentals=0),
    )(*parts, cond)


def body(screened, valence, conduction, owner):
    nb = owner.shape[0]
    _, nv, ncol = valence.shape
    half = ncol // 2
    z, y, xh = lax.axis_index("z"), lax.axis_index("y"), lax.axis_index("xh")
    gp = lax.axis_index("xl") * 2 + lax.axis_index("c")
    lane = half // (NZ * NY * NX)

    own = valence[0]
    part_a = own[:, :half].reshape(nv, NZ, NY, NX, lane).transpose(1, 2, 3, 0, 4)
    part_b = own[:, half:].reshape(nv, NY, NZ, NX, lane).transpose(2, 1, 3, 0, 4)
    pieces = jnp.concatenate([part_a, part_b], axis=-1).reshape(NZ * NY * NX, nv, 2 * lane)
    recv = lax.all_to_all(pieces, ("z", "y", "xh"), 0, 0, tiled=True)
    mine = jnp.concatenate([lax.dynamic_index_in_dim(recv, owner[b], 0, keepdims=False) for b in range(nb)], axis=0)

    other = shift(mine, "xh", NX, 1)
    lo, hi = jnp.where(xh == 0, mine, other), jnp.where(xh == 0, other, mine)
    a = jnp.concatenate([lo[:, :lane], hi[:, :lane]], axis=1)
    b = jnp.concatenate([lo[:, lane:], hi[:, lane:]], axis=1)

    def col_a(dz, dy):
        return (((z + dz) % NZ) * NY + (y + dy) % NY) * K

    def col_b(dz, dy):
        return half + (((y + dy) % NY) * NZ + (z + dz) % NZ) * K

    ya = [a, shift(a, "y", NY, 1), shift(a, "y", NY, -1), shift(a, "y", NY, 2)]
    dys = [0, -1, 1, -2]
    zr = zl = b
    zb, dzs = [b], [0]
    hb = b.shape[0] // 2
    for s in (1, 2, 3):
        zr, zl = shift(zr, "z", NZ, 1), shift(zl, "z", NZ, -1)
        zb += [zr, zl]
        dzs += [-s, s]
    zb.append(jnp.concatenate([shift(zr[:hb], "z", NZ, 1), shift(zl[hb:], "z", NZ, -1)], axis=0))
    dzs.append(4)
    sa = jnp.stack(ya)
    sb = jnp.stack(zb)

    blocks1, offs1 = [sa, sb], [col_a(0, d) for d in dys] + [col_b(d, 0) for d in dzs]
    ar = al = sa
    for s in (1, 2):
        ar, al = shift(ar, "z", NZ, 1), shift(al, "z", NZ, -1)
        blocks1 += [ar, al]
        offs1 += [col_a(-s, d) for d in dys] + [col_a(s, d) for d in dys]
    br, bl = shift(sb, "y", NY, 1), shift(sb, "y", NY, -1)
    ar, al = shift(ar, "z", NZ, 1), shift(al, "z", NZ, -1)
    blocks2 = [ar, al, br, bl]
    offs2 = [col_a(-3, d) for d in dys] + [col_a(3, d) for d in dys] + [col_b(d, -1) for d in dzs] + [col_b(d, 1) for d in dzs]
    a4r, a4l = shift(ar[:2], "z", NZ, 1), shift(al[2:], "z", NZ, -1)
    b2r, b2l = shift(br[:4], "y", NY, 1), shift(bl[4:], "y", NY, -1)
    blocks3 = [a4r, a4l, b2r, b2l]
    offs3 = [col_a(4, d) for d in dys] + [col_b(d, 2) for d in dzs]

    acc = pair_call(screened, blocks1, offs1)
    acc = pair_call(screened, blocks2, offs2, acc)
    acc = pair_call(screened, blocks3, offs3, acc)

    wide = acc.reshape(NGP, acc.shape[0] // NGP, acc.shape[1])
    parts = [lax.dynamic_index_in_dim(wide, gp, 0, keepdims=False)]
    for k in (1, 2, 3):
        out = lax.dynamic_index_in_dim(wide, gp ^ k, 0, keepdims=False)
        parts.append(lax.ppermute(out, ("xl", "c"), [(i, i ^ k) for i in range(NGP)]))
    term = term_call(parts, conduction)

    zsum = jnp.sum(lax.all_to_all(term, "z", 0, 0, tiled=True), axis=0)
    rows = zsum.T.reshape(NY * NX, zsum.shape[1] // (NY * NX), zsum.shape[0])
    return jnp.sum(lax.all_to_all(rows, ("y", "xh"), 0, 0, tiled=True), axis=0)


def solution(mesh):
    fine = Mesh(mesh.devices.reshape(NZ, NY, NX, 2, 2), ("z", "y", "xh", "xl", "c"))
    ga, gp = ("z", "y", "xh"), ("xl", "c")
    placed = (P(ga, gp), P(ga, None, gp), P(None, ga), P())
    return jax.shard_map(body, mesh=fine, in_specs=placed, out_specs=P(ga, gp), check_vma=False)
```

time: 1150 us -> 182 us (0.16)
  waiting for transfers between devices: 1110 us -> 47.4 us
  starting transfers between devices: 0.09 us -> 54.1 us
  blocking collectives: 0 us -> 27.3 us
  matrix products: 24.6 us -> 0 us
  local copies, waits for them, and re-layouts: 3.57 us -> 22.6 us
  Pallas kernels: 0 us -> 14.8 us
    psum x1 -> x0, waiting for transfers between devices: 723 us -> none  [spread(): return lax.psum(block, axis)]
    reduce_scatter x2 -> x0, waiting for transfers between devices: 383 us -> none  [the longest x1 365 us: body(): kernel = lax.psum_scatter(columns, 'ga', scatter_dimension=0, tiled=True)]
    ppermute x0 -> x27, starting transfers between devices: none -> 40.5 us  [the longest x24 38.6 us: shift(): return lax.ppermute(x, axis, [(i, (i + d) % n) for i in range(n)])]
    ppermute x0 -> x27, waiting for transfers between devices: none -> 29 us  [the longest x24 25.7 us: shift(): return lax.ppermute(x, axis, [(i, (i + d) % n) for i in range(n)])]
    all_to_all x0 -> x2, blocking collectives: none -> 27.3 us  [the longest x1 17.2 us: body(): zsum = jnp.sum(lax.all_to_all(term, 'z', 0, 0, tiled=True), axis=0)]
    dot_general x7 -> x0, matrix products: 24.6 us -> none  [the longest x6 23 us: body(): lax.dot_general(screened, chosen, dims, preferred_element_type=jnp.float32)]
    all_to_all x0 -> x1, waiting for transfers between devices: none -> 18.4 us  [body(): recv = lax.all_to_all(pieces, ('z', 'y', 'xh'), 0, 0, tiled=True)]
    pallas_call x0 -> x4, Pallas kernels: none -> 14.8 us  [the longest x3 12.6 us: pair_call(): pl.pallas_call(functools.partial(pair_kernel, len(blocks), acc is None),...]
  transfers between devices with their start and end apart: 3 -> 28, of which waited for: 3 -> 15; matrix products, arithmetic and copies ran while one was open for 0% -> 2% of each run, Pallas kernels for 0% -> 5%
where the time goes in v1:
time: 182 us; the launch traced here: 181 us
  starting transfers between devices  54.1 us (30%)
  waiting for transfers between devices  47.4 us (26%)
  blocking collectives  27.3 us (15%)
  local copies, waits for them, and re-layouts  22.6 us (12%)
  Pallas kernels  14.8 us (8%)
  between operations  11.7 us (6%)
  other arithmetic  2.96 us (2%)
    ppermute x24, starting transfers between devices, shift(): return lax.ppermute(x, axis, [(i, (i + d) % n) for i in range(n)])  38.6 us
    ppermute x24, waiting for transfers between devices, shift(): return lax.ppermute(x, axis, [(i, (i + d) % n) for i in range(n)])  25.7 us
    all_to_all x1, waiting for transfers between devices, body(): recv = lax.all_to_all(pieces, ('z', 'y', 'xh'), 0, 0, tiled=True)  18.4 us
    all_to_all x1, blocking collectives, body(): zsum = jnp.sum(lax.all_to_all(term, 'z', 0, 0, tiled=True), axis=0)  17.2 us
    all_to_all x1, starting transfers between devices, body(): recv = lax.all_to_all(pieces, ('z', 'y', 'xh'), 0, 0, tiled=True)  13.7 us
    unnamed x41, local copies, waits for them, and re-layouts  13.1 us
    pallas_call x3, Pallas kernels, pair_call(): pl.pallas_call(functools.partial(pair_kernel, len(blocks), acc is None),...  12.6 us
    all_to_all x1, blocking collectives, body(): return jnp.sum(lax.all_to_all(rows, ('y', 'xh'), 0, 0, tiled=True), axis=0)  10.1 us
  transfers between devices with their start and end apart: 28, of which 15 were waited for; matrix products, arithmetic and copies ran while one was open for 2% of the time, Pallas kernels for 5%

profile of v1, /device:TPU:2, one launch (start us, length us, event | category | flops | bytes accessed | tf_op | source)
XLA Modules:
  0.0 180.9 jit_solution(11945749610846246311)
XLA Ops:
  0.0 1.3 fusion.2
  2.4 1.5 pad_maximum_fusion
  4.0 1.8 %copy.10 = bf16[8,4,2,32,256]{4,3,2,1,0:T(8,128)(2,1)} copy(bf16[8,4,2,32,256]{4,2,0,1,3:T(2,128)(2,1)S(1)} %pad_maximum_fusion) | data formatting | bytes 2097152 | tf_op jit(solution)/shard_map/concatenate | solution.py:98
  5.8 13.7 %all-to-all-start = ((bf16[64,32,256]{2,1,0:T(8,128)(2,1)}), bf16[64,32,256]{2,1,0:T(8,128)(2,1)S(1)}, u32[]{:S(2)}, u32[]{:S(2)}) async-start(bf16[64,32,256]{2,1,0:T(8,128)(2,1)} %bitcast.15), calls=%async_computation | async-start | bytes 2097152 | tf_op jit(solution)/shard_map/all_to_all | solution.py:99
  19.5 0.7 fusion.5
  31.5 18.4 %all-to-all-done = bf16[64,32,256]{2,1,0:T(8,128)(2,1)S(1)} async-done(((bf16[64,32,256]{2,1,0:T(8,128)(2,1)}), bf16[64,32,256]{2,1,0:T(8,128)(2,1)S(1)}, u32[]{:S(2)}, u32[]{:S(2)}) %all-to-all-start) | async-done | bytes 1048608 | tf_op jit(solution)/shard_map/all_to_all | solution.py:99
  50.6 5.6 %collective-permute-done = bf16[192,256]{1,0:T(8,128)(2,1)S(1)} collective-permute-done((bf16[192,256]{1,0:T(8,128)(2,1)S(1)}, bf16[192,256]{1,0:T(8,128)(2,1)S(1)}, u32[]{:S(2)}, u32[]{:S(2)}) %collective-permute-start) | collective-permute-done | bytes 98336 | tf_op jit(solution)/shard_map/ppermute | solution.py:16
  56.3 1.5 collective-permute-start.12
  57.8 1.9 %collective-permute-start.13 = (bf16[192,256]{1,0:T(8,128)(2,1)S(1)}, bf16[192,256]{1,0:T(8,128)(2,1)S(1)}, u32[]{:S(2)}, u32[]{:S(2)}) collective-permute-start(bf16[192,256]{1,0:T(8,128)(2,1)S(1)} %pad_maximum_fusion.3), channel_id=1, source_target_pairs={{0,224},{32,0},{64,32},{96,64},{128,96},{160,128},{192,160},{224,1... | collective-permute-start | bytes 294920 | tf_op jit(solution)/shard_map/ppermute | solution.py:16
  59.9 3.1 %collective-permute-start.2 = (bf16[192,256]{1,0:T(8,128)(2,1)S(1)}, bf16[192,256]{1,0:T(8,128)(2,1)S(1)}, u32[]{:S(2)}, u32[]{:S(2)}) collective-permute-start(bf16[192,256]{1,0:T(8,128)(2,1)S(1)} %get-tuple-element.18), channel_id=1, source_target_pairs={{0,24},{8,0},{16,8},{24,16},{1,25},{9,1},{17,9},{25,17},{2,26},{10... | collective-permute-start | bytes 294920 | tf_op jit(solution)/shard_map/ppermute | solution.py:16
  63.0 2.6 %collective-permute-done.1 = bf16[192,256]{1,0:T(8,128)(2,1)S(1)} collective-permute-done((bf16[192,256]{1,0:T(8,128)(2,1)S(1)}, bf16[192,256]{1,0:T(8,128)(2,1)S(1)}, u32[]{:S(2)}, u32[]{:S(2)}) %collective-permute-start.1) | collective-permute-done | bytes 98336 | tf_op jit(solution)/shard_map/ppermute | solution.py:16
  66.2 2.9 %collective-permute-done.3 = bf16[192,256]{1,0:T(8,128)(2,1)S(1)} collective-permute-done((bf16[192,256]{1,0:T(8,128)(2,1)S(1)}, bf16[192,256]{1,0:T(8,128)(2,1)S(1)}, u32[]{:S(2)}, u32[]{:S(2)}) %collective-permute-start.3) | collective-permute-done | bytes 98336 | tf_op jit(solution)/shard_map/ppermute | solution.py:16
  69.4 3.1 %collective-permute-start.8 = (bf16[4,192,256]{2,1,0:T(8,128)(2,1)S(1)}, bf16[4,192,256]{2,1,0:T(8,128)(2,1)S(1)}, u32[]{:S(2)}, u32[]{:S(2)}) collective-permute-start(bf16[4,192,256]{2,1,0:T(8,128)(2,1)S(1)} %pad_maximum_fusion.1.refs_0_), channel_id=1, source_target_pairs={{0,224},{32,0},{64,32},{96,64},{128,96},{160,128},{192,160},{224,1... | collective-permute-start | bytes 1179656 | tf_op jit(solution)/shard_map/ppermute | solution.py:16
  72.5 3.5 %collective-permute-start.15 = (bf16[192,256]{1,0:T(8,128)(2,1)S(1)}, bf16[192,256]{1,0:T(8,128)(2,1)S(1)}, u32[]{:S(2)}, u32[]{:S(2)}) collective-permute-start(bf16[192,256]{1,0:T(8,128)(2,1)S(1)} %collective-permute-done.13), channel_id=1, source_target_pairs={{0,224},{32,0},{64,32},{96,64},{128,96},{160,128},{192,160},{224,1... | collective-permute-start | bytes 294920 | tf_op jit(solution)/shard_map/ppermute | solution.py:16
  76.0 4.3 %collective-permute-done.14 = bf16[192,256]{1,0:T(8,128)(2,1)S(1)} collective-permute-done((bf16[192,256]{1,0:T(8,128)(2,1)S(1)}, bf16[192,256]{1,0:T(8,128)(2,1)S(1)}, u32[]{:S(2)}, u32[]{:S(2)}) %collective-permute-start.14) | collective-permute-done | bytes 98336 | tf_op jit(solution)/shard_map/ppermute | solution.py:16
  80.4 3.3 %collective-permute-start.17 = (bf16[192,256]{1,0:T(8,128)(2,1)S(1)}, bf16[192,256]{1,0:T(8,128)(2,1)S(1)}, u32[]{:S(2)}, u32[]{:S(2)}) collective-permute-start(bf16[192,256]{1,0:T(8,128)(2,1)S(1)} %collective-permute-done.15), channel_id=1, source_target_pairs={{0,224},{32,0},{64,32},{96,64},{128,96},{160,128},{192,160},{224,1... | collective-permute-start | bytes 294920 | tf_op jit(solution)/shard_map/ppermute | solution.py:16
  83.7 2.5 %collective-permute-done.16 = bf16[192,256]{1,0:T(8,128)(2,1)S(1)} collective-permute-done((bf16[192,256]{1,0:T(8,128)(2,1)S(1)}, bf16[192,256]{1,0:T(8,128)(2,1)S(1)}, u32[]{:S(2)}, u32[]{:S(2)}) %collective-permute-start.16) | collective-permute-done | bytes 98336 | tf_op jit(solution)/shard_map/ppermute | solution.py:16
  86.2 3.3 %collective-permute-start.19 = (bf16[96,256]{1,0:T(8,128)(2,1)S(1)}, bf16[96,256]{1,0:T(8,128)(2,1)S(1)}, u32[]{:S(2)}, u32[]{:S(2)}) collective-permute-start(bf16[96,256]{1,0:T(8,128)(2,1)S(1)} %slice.81), channel_id=1, source_target_pairs={{0,224},{32,0},{64,32},{96,64},{128,96},{160,128},{192,160},{224,1... | collective-permute-start | bytes 147464 | tf_op jit(solution)/shard_map/ppermute | solution.py:16
  89.5 2.0 %collective-permute-done.18 = bf16[96,256]{1,0:T(8,128)(2,1)S(1)} collective-permute-done((bf16[96,256]{1,0:T(8,128)(2,1)S(1)}, bf16[96,256]{1,0:T(8,128)(2,1)S(1)}, u32[]{:S(2)}, u32[]{:S(2)}) %collective-permute-start.18) | collective-permute-done | bytes 49184 | tf_op jit(solution)/shard_map/ppermute | solution.py:16
  91.7 3.2 %collective-permute-start.22 = (bf16[8,192,256]{2,1,0:T(8,128)(2,1)S(1)}, bf16[8,192,256]{2,1,0:T(8,128)(2,1)S(1)}, u32[]{:S(2)}, u32[]{:S(2)}) collective-permute-start(bf16[8,192,256]{2,1,0:T(8,128)(2,1)S(1)} %fusion.refs_1_), channel_id=1, source_target_pairs={{0,24},{8,0},{16,8},{24,16},{1,25},{9,1},{17,9},{25,17},{2,26},{10... | collective-permute-start | bytes 2359304 | tf_op jit(solution)/shard_map/ppermute | solution.py:16
  95.0 3.8 %collective-permute-start.9 = (bf16[4,192,256]{2,1,0:T(8,128)(2,1)S(1)}, bf16[4,192,256]{2,1,0:T(8,128)(2,1)S(1)}, u32[]{:S(2)}, u32[]{:S(2)}) collective-permute-start(bf16[4,192,256]{2,1,0:T(8,128)(2,1)S(1)} %collective-permute-done.8.refs_3_), channel_id=1, source_target_pairs={{0,224},{32,0},{64,32},{96,64},{128,96},{160,128},{192,160},{224,1... | collective-permute-start | bytes 1179656 | tf_op jit(solution)/shard_map/ppermute | solution.py:16
  98.7 0.8 copy-done.4
  99.5 0.8 copy-done.2
  100.2 4.4 %collective-permute-done.9.refs_5_ = bf16[4,192,256]{2,1,0:T(8,128)(2,1)S(1)} collective-permute-done((bf16[4,192,256]{2,1,0:T(8,128)(2,1)S(1)}, bf16[4,192,256]{2,1,0:T(8,128)(2,1)S(1)}, u32[]{:S(2)}, u32[]{:S(2)}) %collective-permute-start.9) | collective-permute-done | bytes 393248 | tf_op jit(solution)/shard_map/ppermute | solution.py:16
  104.7 3.7 %collective-permute-start.10 = (bf16[4,192,256]{2,1,0:T(8,128)(2,1)S(1)}, bf16[4,192,256]{2,1,0:T(8,128)(2,1)S(1)}, u32[]{:S(2)}, u32[]{:S(2)}) collective-permute-start(bf16[4,192,256]{2,1,0:T(8,128)(2,1)S(1)} %collective-permute-done.9.refs_5_), channel_id=1, source_target_pairs={{0,224},{32,0},{64,32},{96,64},{128,96},{160,128},{192,160},{224,1... | collective-permute-start | bytes 1179656 | tf_op jit(solution)/shard_map/ppermute | solution.py:16
  108.8 0.8 slice.82
  109.6 0.8 slice.83
  110.4 3.2 %collective-permute-start.23 = (bf16[4,192,256]{2,1,0:T(8,128)(2,1)}, bf16[4,192,256]{2,1,0:T(8,128)(2,1)}, u32[]{:S(2)}, u32[]{:S(2)}) collective-permute-start(bf16[4,192,256]{2,1,0:T(8,128)(2,1)} %slice.83), channel_id=1, source_target_pairs={{0,24},{8,0},{16,8},{24,16},{1,25},{9,1},{17,9},{25,17},{2,26},{10... | collective-permute-start | bytes 1179656 | tf_op jit(solution)/shard_map/ppermute | solution.py:16
  113.7 0.7 slice.77
  114.3 4.0 %collective-permute-start.11 = (bf16[2,192,256]{2,1,0:T(8,128)(2,1)}, bf16[2,192,256]{2,1,0:T(8,128)(2,1)}, u32[]{:S(2)}, u32[]{:S(2)}) collective-permute-start(bf16[2,192,256]{2,1,0:T(8,128)(2,1)} %slice.77), channel_id=1, source_target_pairs={{0,224},{32,0},{64,32},{96,64},{128,96},{160,128},{192,160},{224,1... | collective-permute-start | bytes 589832 | tf_op jit(solution)/shard_map/ppermute | solution.py:16
  118.4 0.7 slice.76
  119.4 3.4 %copy-done = bf16[256,16384]{1,0:T(8,128)(2,1)S(1)} copy-done((bf16[256,16384]{1,0:T(8,128)(2,1)S(1)}, bf16[256,16384]{1,0:T(8,128)(2,1)}, u32[]{:S(2)}) %copy-start) | copy-done | bytes 8388632
  122.8 1.0 copy-done.3
  123.8 1.0 copy-done.5
  124.8 1.0 copy-done.7
  125.8 1.0 copy-done.9
  126.8 4.9 %shard_map.46.refs_4_ = f32[192,256]{1,0:T(8,128)S(1)} custom-call(s32[28]{0:T(128)S(1)} %stack.323.offs_ref, bf16[256,16384]{1,0:T(8,128)(2,1)S(1)} %copy-done, bf16[4,192,256]{2,1,0:T(8,128)(2,1)S(1)} %pad_maximum_fusion.1.refs_0_, bf16[8,192,256]{2,1,0:T(8,128)(2,1)S(1)} %fusion.refs_1_, bf16[4,192,256]{2,1,0:T(8,128)(2,1)S(1)} %copy-done.3, ...), custom_call_target="tpu_custom_call" | custom-call | flops 704643072 | bytes 6422528 | tf_op jit(solution)/shard_map/pallas_call | solution.py:49
  131.7 3.4 %copy-done.1 = bf16[256,16384]{1,0:T(8,128)(2,1)S(1)} copy-done((bf16[256,16384]{1,0:T(8,128)(2,1)S(1)}, bf16[256,16384]{1,0:T(8,128)(2,1)}, u32[]{:S(2)}) %copy-start.1) | copy-done | bytes 8388632
  135.1 4.4 %shard_map.47.refs_4_ = f32[192,256]{1,0:T(8,128)S(1)} custom-call(s32[24]{0:T(128)S(1)} %stack.294.offs_ref, bf16[256,16384]{1,0:T(8,128)(2,1)S(1)} %copy-done.1, bf16[4,192,256]{2,1,0:T(8,128)(2,1)S(1)} %collective-permute-done.6.refs_0_, bf16[4,192,256]{2,1,0:T(8,128)(2,1)S(1)} %collective-permute-done.10.refs_1_, ...), custom_call_target="tpu_custom_call" | custom-call | flops 603979776 | bytes 5505024 | tf_op jit(solution)/shard_map/pallas_call | solution.py:49
  139.5 3.4 %shard_map.48 = f32[192,256]{1,0:T(8,128)S(1)} custom-call(s32[12]{0:T(128)S(1)} %stack.255.offs_ref, bf16[256,16384]{1,0:T(8,128)(2,1)S(1)} %copy-done.1, bf16[2,192,256]{2,1,0:T(8,128)(2,1)} %collective-permute-done.7.refs_0_, bf16[2,192,256]{2,1,0:T(8,128)(2,1)} %collective-permute-done.11.refs_1_, bf16[4,192,256]{2,1,0:T(8,128)(2,1)} %collective-permute-done.21.refs_2_, ...), custom_call_target="tpu_custom_call" | custom-call | flops 301989888 | bytes 2752512 | tf_op jit(solution)/shard_map/pallas_call | solution.py:49
  142.9 0.6 dynamic-slice_bitcast_fusion
  143.5 1.4 collective-permute-start.25
  145.4 2.3 %collective-permute-done.25.c_ref = f32[48,256]{1,0:T(8,128)S(1)} collective-permute-done((f32[48,256]{1,0:T(8,128)S(1)}, f32[48,256]{1,0:T(8,128)S(1)}, u32[]{:S(2)}, u32[]{:S(2)}) %collective-permute-start.25) | collective-permute-done | bytes 49184 | tf_op jit(solution)/shard_map/ppermute | solution.py:150
  147.7 1.0 collective-permute-done.26.d_ref
  149.3 2.2 %shard_map.49 = f32[8,48,128]{2,1,0:T(8,128)} custom-call(f32[48,256]{1,0:T(8,128)} %get-tuple-element.10.a_ref, f32[48,256]{1,0:T(8,128)} %copy-done.10, f32[48,256]{1,0:T(8,128)} %copy-done.11, f32[48,256]{1,0:T(8,128)} %copy-done.12, bf16[1024,256]{1,0:T(8,128)(2,1)} %cond_ref.1), custom_call_target="tpu_custom_call" | custom-call | flops 75497472 | bytes 524288 | tf_op jit(solution)/shard_map/pallas_call | solution.py:78
  151.4 17.2 %all_to_all.15 = f32[8,48,128]{2,1,0:T(8,128)S(1)} all-to-all(f32[8,48,128]{2,1,0:T(8,128)} %shard_map.49), channel_id=1, replica_groups=mesh['z'=8,'y'=4,'xh'=2,'xl'=2,'c'=2] {'z'}, dimensions={0} | all-to-all | bytes 393216 | tf_op jit(solution)/shard_map/all_to_all | solution.py:153
  168.8 10.1 %all_to_all.16 = f32[8,1,768]{2,1,0:T(1,128)S(1)} all-to-all(f32[8,1,768]{2,1,0:T(1,128)S(1)} %reshape.20), channel_id=1, replica_groups=mesh['z'=8,'y'=4,'xh'=2,'xl'=2,'c'=2] {'y','xh'}, dimensions={0} | all-to-all | bytes 49152 | tf_op jit(solution)/shard_map/all_to_all | solution.py:155
  179.5 0.7 reduce
  (85 shorter events, 6.7 us)
Async XLA Ops:
  4.0 15.5 %copy-start.13 = (s32[6]{0:T(128)S(1)}, s32[6]{0:T(128)}, u32[]{:S(2)}) copy-start(s32[6]{0:T(128)} %param.7) | copy-start | bytes 76
  5.8 44.2 %all-to-all-start = ((bf16[64,32,256]{2,1,0:T(8,128)(2,1)}), bf16[64,32,256]{2,1,0:T(8,128)(2,1)S(1)}, u32[]{:S(2)}, u32[]{:S(2)}) async-start(bf16[64,32,256]{2,1,0:T(8,128)(2,1)} %bitcast.15), calls=%async_computation | async-start | bytes 2097152 | tf_op jit(solution)/shard_map/all_to_all | solution.py:99
  50.0 6.2 %collective-permute-start = (bf16[192,256]{1,0:T(8,128)(2,1)S(1)}, bf16[192,256]{1,0:T(8,128)(2,1)S(1)}, u32[]{:S(2)}, u32[]{:S(2)}) collective-permute-start(bf16[192,256]{1,0:T(8,128)(2,1)S(1)} %constant_dynamic-update-slice_fusion), channel_id=1, source_target_pairs={{0,4},{4,0},{1,5},{5,1},{2,6},{6,2},{3,7},{7,3},{8,12},{12,8},{9,1... | collective-permute-start | bytes 294920 | tf_op jit(solution)/shard_map/ppermute | solution.py:16
  56.3 16.1 %collective-permute-start.12 = (bf16[192,256]{1,0:T(8,128)(2,1)S(1)}, bf16[192,256]{1,0:T(8,128)(2,1)S(1)}, u32[]{:S(2)}, u32[]{:S(2)}) collective-permute-start(bf16[192,256]{1,0:T(8,128)(2,1)S(1)} %pad_maximum_fusion.3), channel_id=1, source_target_pairs={{0,32},{32,64},{64,96},{96,128},{128,160},{160,192},{192,224},{224... | collective-permute-start | bytes 294920 | tf_op jit(solution)/shard_map/ppermute | solution.py:16
  57.8 14.7 %collective-permute-start.13 = (bf16[192,256]{1,0:T(8,128)(2,1)S(1)}, bf16[192,256]{1,0:T(8,128)(2,1)S(1)}, u32[]{:S(2)}, u32[]{:S(2)}) collective-permute-start(bf16[192,256]{1,0:T(8,128)(2,1)S(1)} %pad_maximum_fusion.3), channel_id=1, source_target_pairs={{0,224},{32,0},{64,32},{96,64},{128,96},{160,128},{192,160},{224,1... | collective-permute-start | bytes 294920 | tf_op jit(solution)/shard_map/ppermute | solution.py:16
  59.7 5.9 %collective-permute-start.1 = (bf16[192,256]{1,0:T(8,128)(2,1)S(1)}, bf16[192,256]{1,0:T(8,128)(2,1)S(1)}, u32[]{:S(2)}, u32[]{:S(2)}) collective-permute-start(bf16[192,256]{1,0:T(8,128)(2,1)S(1)} %get-tuple-element.18), channel_id=1, source_target_pairs={{0,8},{8,16},{16,24},{24,0},{1,9},{9,17},{17,25},{25,1},{2,10},{10... | collective-permute-start | bytes 294920 | tf_op jit(solution)/shard_map/ppermute | solution.py:16
  59.9 6.3 %collective-permute-start.2 = (bf16[192,256]{1,0:T(8,128)(2,1)S(1)}, bf16[192,256]{1,0:T(8,128)(2,1)S(1)}, u32[]{:S(2)}, u32[]{:S(2)}) collective-permute-start(bf16[192,256]{1,0:T(8,128)(2,1)S(1)} %get-tuple-element.18), channel_id=1, source_target_pairs={{0,24},{8,0},{16,8},{24,16},{1,25},{9,1},{17,9},{25,17},{2,26},{10... | collective-permute-start | bytes 294920 | tf_op jit(solution)/shard_map/ppermute | solution.py:16
  63.0 6.1 %collective-permute-start.3 = (bf16[192,256]{1,0:T(8,128)(2,1)S(1)}, bf16[192,256]{1,0:T(8,128)(2,1)S(1)}, u32[]{:S(2)}, u32[]{:S(2)}) collective-permute-start(bf16[192,256]{1,0:T(8,128)(2,1)S(1)} %get-tuple-element.18), channel_id=1, source_target_pairs={{0,16},{8,24},{16,0},{24,8},{1,17},{9,25},{17,1},{25,9},{2,18},{10... | collective-permute-start | bytes 294920 | tf_op jit(solution)/shard_map/ppermute | solution.py:16
  69.2 30.3 %collective-permute-start.4 = (bf16[4,192,256]{2,1,0:T(8,128)(2,1)S(1)}, bf16[4,192,256]{2,1,0:T(8,128)(2,1)S(1)}, u32[]{:S(2)}, u32[]{:S(2)}) collective-permute-start(bf16[4,192,256]{2,1,0:T(8,128)(2,1)S(1)} %pad_maximum_fusion.1.refs_0_), channel_id=1, source_target_pairs={{0,32},{32,64},{64,96},{96,128},{128,160},{160,192},{192,224},{224... | collective-permute-start | bytes 1179656 | tf_op jit(solution)/shard_map/ppermute | solution.py:16
  69.4 25.5 %collective-permute-start.8 = (bf16[4,192,256]{2,1,0:T(8,128)(2,1)S(1)}, bf16[4,192,256]{2,1,0:T(8,128)(2,1)S(1)}, u32[]{:S(2)}, u32[]{:S(2)}) collective-permute-start(bf16[4,192,256]{2,1,0:T(8,128)(2,1)S(1)} %pad_maximum_fusion.1.refs_0_), channel_id=1, source_target_pairs={{0,224},{32,0},{64,32},{96,64},{128,96},{160,128},{192,160},{224,1... | collective-permute-start | bytes 1179656 | tf_op jit(solution)/shard_map/ppermute | solution.py:16
  72.5 7.9 %collective-permute-start.14 = (bf16[192,256]{1,0:T(8,128)(2,1)S(1)}, bf16[192,256]{1,0:T(8,128)(2,1)S(1)}, u32[]{:S(2)}, u32[]{:S(2)}) collective-permute-start(bf16[192,256]{1,0:T(8,128)(2,1)S(1)} %collective-permute-done.12), channel_id=1, source_target_pairs={{0,32},{32,64},{64,96},{96,128},{128,160},{160,192},{192,224},{224... | collective-permute-start | bytes 294920 | tf_op jit(solution)/shard_map/ppermute | solution.py:16
  72.5 7.8 %collective-permute-start.15 = (bf16[192,256]{1,0:T(8,128)(2,1)S(1)}, bf16[192,256]{1,0:T(8,128)(2,1)S(1)}, u32[]{:S(2)}, u32[]{:S(2)}) collective-permute-start(bf16[192,256]{1,0:T(8,128)(2,1)S(1)} %collective-permute-done.13), channel_id=1, source_target_pairs={{0,224},{32,0},{64,32},{96,64},{128,96},{160,128},{192,160},{224,1... | collective-permute-start | bytes 294920 | tf_op jit(solution)/shard_map/ppermute | solution.py:16
  80.3 5.8 %collective-permute-start.16 = (bf16[192,256]{1,0:T(8,128)(2,1)S(1)}, bf16[192,256]{1,0:T(8,128)(2,1)S(1)}, u32[]{:S(2)}, u32[]{:S(2)}) collective-permute-start(bf16[192,256]{1,0:T(8,128)(2,1)S(1)} %collective-permute-done.14), channel_id=1, source_target_pairs={{0,32},{32,64},{64,96},{96,128},{128,160},{160,192},{192,224},{224... | collective-permute-start | bytes 294920 | tf_op jit(solution)/shard_map/ppermute | solution.py:16
  80.4 5.8 %collective-permute-start.17 = (bf16[192,256]{1,0:T(8,128)(2,1)S(1)}, bf16[192,256]{1,0:T(8,128)(2,1)S(1)}, u32[]{:S(2)}, u32[]{:S(2)}) collective-permute-start(bf16[192,256]{1,0:T(8,128)(2,1)S(1)} %collective-permute-done.15), channel_id=1, source_target_pairs={{0,224},{32,0},{64,32},{96,64},{128,96},{160,128},{192,160},{224,1... | collective-permute-start | bytes 294920 | tf_op jit(solution)/shard_map/ppermute | solution.py:16
  86.2 5.3 %collective-permute-start.18 = (bf16[96,256]{1,0:T(8,128)(2,1)S(1)}, bf16[96,256]{1,0:T(8,128)(2,1)S(1)}, u32[]{:S(2)}, u32[]{:S(2)}) collective-permute-start(bf16[96,256]{1,0:T(8,128)(2,1)S(1)} %slice.80), channel_id=1, source_target_pairs={{0,32},{32,64},{64,96},{96,128},{128,160},{160,192},{192,224},{224... | collective-permute-start | bytes 147464 | tf_op jit(solution)/shard_map/ppermute | solution.py:16
  86.2 5.5 %collective-permute-start.19 = (bf16[96,256]{1,0:T(8,128)(2,1)S(1)}, bf16[96,256]{1,0:T(8,128)(2,1)S(1)}, u32[]{:S(2)}, u32[]{:S(2)}) collective-permute-start(bf16[96,256]{1,0:T(8,128)(2,1)S(1)} %slice.81), channel_id=1, source_target_pairs={{0,224},{32,0},{64,32},{96,64},{128,96},{160,128},{192,160},{224,1... | collective-permute-start | bytes 147464 | tf_op jit(solution)/shard_map/ppermute | solution.py:16
  91.7 17.1 %collective-permute-start.20 = (bf16[8,192,256]{2,1,0:T(8,128)(2,1)S(1)}, bf16[8,192,256]{2,1,0:T(8,128)(2,1)S(1)}, u32[]{:S(2)}, u32[]{:S(2)}) collective-permute-start(bf16[8,192,256]{2,1,0:T(8,128)(2,1)S(1)} %fusion.refs_1_), channel_id=1, source_target_pairs={{0,8},{8,16},{16,24},{24,0},{1,9},{9,17},{17,25},{25,1},{2,10},{10... | collective-permute-start | bytes 2359304 | tf_op jit(solution)/shard_map/ppermute | solution.py:16
  91.7 17.9 %collective-permute-start.22 = (bf16[8,192,256]{2,1,0:T(8,128)(2,1)S(1)}, bf16[8,192,256]{2,1,0:T(8,128)(2,1)S(1)}, u32[]{:S(2)}, u32[]{:S(2)}) collective-permute-start(bf16[8,192,256]{2,1,0:T(8,128)(2,1)S(1)} %fusion.refs_1_), channel_id=1, source_target_pairs={{0,24},{8,0},{16,8},{24,16},{1,25},{9,1},{17,9},{25,17},{2,26},{10... | collective-permute-start | bytes 2359304 | tf_op jit(solution)/shard_map/ppermute | solution.py:16
  95.0 9.7 %collective-permute-start.9 = (bf16[4,192,256]{2,1,0:T(8,128)(2,1)S(1)}, bf16[4,192,256]{2,1,0:T(8,128)(2,1)S(1)}, u32[]{:S(2)}, u32[]{:S(2)}) collective-permute-start(bf16[4,192,256]{2,1,0:T(8,128)(2,1)S(1)} %collective-permute-done.8.refs_3_), channel_id=1, source_target_pairs={{0,224},{32,0},{64,32},{96,64},{128,96},{160,128},{192,160},{224,1... | collective-permute-start | bytes 1179656 | tf_op jit(solution)/shard_map/ppermute | solution.py:16
  98.7 0.8 copy-start.4
  99.5 9.0 %collective-permute-start.5 = (bf16[4,192,256]{2,1,0:T(8,128)(2,1)S(1)}, bf16[4,192,256]{2,1,0:T(8,128)(2,1)S(1)}, u32[]{:S(2)}, u32[]{:S(2)}) collective-permute-start(bf16[4,192,256]{2,1,0:T(8,128)(2,1)S(1)} %collective-permute-done.4.refs_2_), channel_id=1, source_target_pairs={{0,32},{32,64},{64,96},{96,128},{128,160},{160,192},{192,224},{224... | collective-permute-start | bytes 1179656 | tf_op jit(solution)/shard_map/ppermute | solution.py:16
  99.5 0.8 copy-start.2
  104.7 13.7 %copy-start.6 = (bf16[4,192,256]{2,1,0:T(8,128)(2,1)}, bf16[4,192,256]{2,1,0:T(8,128)(2,1)S(1)}, u32[]{:S(2)}) copy-start(bf16[4,192,256]{2,1,0:T(8,128)(2,1)S(1)} %collective-permute-done.9.refs_5_) | copy-start | bytes 1179652
  104.7 9.0 %collective-permute-start.10 = (bf16[4,192,256]{2,1,0:T(8,128)(2,1)S(1)}, bf16[4,192,256]{2,1,0:T(8,128)(2,1)S(1)}, u32[]{:S(2)}, u32[]{:S(2)}) collective-permute-start(bf16[4,192,256]{2,1,0:T(8,128)(2,1)S(1)} %collective-permute-done.9.refs_5_), channel_id=1, source_target_pairs={{0,224},{32,0},{64,32},{96,64},{128,96},{160,128},{192,160},{224,1... | collective-permute-start | bytes 1179656 | tf_op jit(solution)/shard_map/ppermute | solution.py:16
  108.5 10.6 %copy-start.8 = (bf16[4,192,256]{2,1,0:T(8,128)(2,1)}, bf16[4,192,256]{2,1,0:T(8,128)(2,1)S(1)}, u32[]{:S(2)}) copy-start(bf16[4,192,256]{2,1,0:T(8,128)(2,1)S(1)} %collective-permute-done.5.refs_4_) | copy-start | bytes 1179652
  108.5 9.9 %collective-permute-start.6 = (bf16[4,192,256]{2,1,0:T(8,128)(2,1)S(1)}, bf16[4,192,256]{2,1,0:T(8,128)(2,1)S(1)}, u32[]{:S(2)}, u32[]{:S(2)}) collective-permute-start(bf16[4,192,256]{2,1,0:T(8,128)(2,1)S(1)} %collective-permute-done.5.refs_4_), channel_id=1, source_target_pairs={{0,32},{32,64},{64,96},{96,128},{128,160},{160,192},{192,224},{224... | collective-permute-start | bytes 1179656 | tf_op jit(solution)/shard_map/ppermute | solution.py:16
  109.6 29.9 %collective-permute-start.21 = (bf16[4,192,256]{2,1,0:T(8,128)(2,1)}, bf16[4,192,256]{2,1,0:T(8,128)(2,1)}, u32[]{:S(2)}, u32[]{:S(2)}) collective-permute-start(bf16[4,192,256]{2,1,0:T(8,128)(2,1)} %slice.82), channel_id=1, source_target_pairs={{0,8},{8,16},{16,24},{24,0},{1,9},{9,17},{17,25},{25,1},{2,10},{10... | collective-permute-start | bytes 1179656 | tf_op jit(solution)/shard_map/ppermute | solution.py:16
  110.4 29.1 %collective-permute-start.23 = (bf16[4,192,256]{2,1,0:T(8,128)(2,1)}, bf16[4,192,256]{2,1,0:T(8,128)(2,1)}, u32[]{:S(2)}, u32[]{:S(2)}) collective-permute-start(bf16[4,192,256]{2,1,0:T(8,128)(2,1)} %slice.83), channel_id=1, source_target_pairs={{0,24},{8,0},{16,8},{24,16},{1,25},{9,1},{17,9},{25,17},{2,26},{10... | collective-permute-start | bytes 1179656 | tf_op jit(solution)/shard_map/ppermute | solution.py:16
  114.3 25.1 %collective-permute-start.11 = (bf16[2,192,256]{2,1,0:T(8,128)(2,1)}, bf16[2,192,256]{2,1,0:T(8,128)(2,1)}, u32[]{:S(2)}, u32[]{:S(2)}) collective-permute-start(bf16[2,192,256]{2,1,0:T(8,128)(2,1)} %slice.77), channel_id=1, source_target_pairs={{0,224},{32,0},{64,32},{96,64},{128,96},{160,128},{192,160},{224,1... | collective-permute-start | bytes 589832 | tf_op jit(solution)/shard_map/ppermute | solution.py:16
  119.1 20.4 %collective-permute-start.7 = (bf16[2,192,256]{2,1,0:T(8,128)(2,1)}, bf16[2,192,256]{2,1,0:T(8,128)(2,1)}, u32[]{:S(2)}, u32[]{:S(2)}) collective-permute-start(bf16[2,192,256]{2,1,0:T(8,128)(2,1)} %slice.76), channel_id=1, source_target_pairs={{0,32},{32,64},{64,96},{96,128},{128,160},{160,192},{192,224},{224... | collective-permute-start | bytes 589832 | tf_op jit(solution)/shard_map/ppermute | solution.py:16
  119.4 3.4 %copy-start = (bf16[256,16384]{1,0:T(8,128)(2,1)S(1)}, bf16[256,16384]{1,0:T(8,128)(2,1)}, u32[]{:S(2)}) copy-start(bf16[256,16384]{1,0:T(8,128)(2,1)} %w_ref.5) | copy-start | bytes 25165828
  122.8 1.0 copy-start.3
  123.8 1.0 copy-start.5
  124.8 1.0 copy-start.7
  125.8 1.0 copy-start.9
  131.7 3.4 %copy-start.1 = (bf16[256,16384]{1,0:T(8,128)(2,1)S(1)}, bf16[256,16384]{1,0:T(8,128)(2,1)}, u32[]{:S(2)}) copy-start(bf16[256,16384]{1,0:T(8,128)(2,1)} %w_ref.5) | copy-start | bytes 25165828
  143.5 1.9 %collective-permute-start.24 = (f32[48,256]{1,0:T(8,128)S(1)}, f32[48,256]{1,0:T(8,128)S(1)}, u32[]{:S(2)}, u32[]{:S(2)}) collective-permute-start(f32[48,256]{1,0:T(8,128)S(1)} %get-tuple-element.9), channel_id=1, source_target_pairs={{0,1},{1,0},{2,3},{3,2},{4,5},{5,4},{6,7},{7,6},{8,9},{9,8},{10,11... | collective-permute-start | bytes 147464 | tf_op jit(solution)/shard_map/ppermute | solution.py:150
  143.5 4.2 %collective-permute-start.25 = (f32[48,256]{1,0:T(8,128)S(1)}, f32[48,256]{1,0:T(8,128)S(1)}, u32[]{:S(2)}, u32[]{:S(2)}) collective-permute-start(f32[48,256]{1,0:T(8,128)S(1)} %get-tuple-element.8), channel_id=1, source_target_pairs={{0,2},{1,3},{2,0},{3,1},{4,6},{5,7},{6,4},{7,5},{8,10},{9,11},{10,... | collective-permute-start | bytes 147464 | tf_op jit(solution)/shard_map/ppermute | solution.py:150
  145.0 3.7 %collective-permute-start.26 = (f32[48,256]{1,0:T(8,128)S(1)}, f32[48,256]{1,0:T(8,128)S(1)}, u32[]{:S(2)}, u32[]{:S(2)}) collective-permute-start(f32[48,256]{1,0:T(8,128)S(1)} %get-tuple-element.7), channel_id=1, source_target_pairs={{0,3},{1,2},{2,1},{3,0},{4,7},{5,6},{6,5},{7,4},{8,11},{9,10},{10,... | collective-permute-start | bytes 147464 | tf_op jit(solution)/shard_map/ppermute | solution.py:150
  145.4 3.3 %copy-start.10 = (f32[48,256]{1,0:T(8,128)}, f32[48,256]{1,0:T(8,128)S(1)}, u32[]{:S(2)}) copy-start(f32[48,256]{1,0:T(8,128)S(1)} %collective-permute-done.24.b_ref) | copy-start | bytes 147460
  147.7 1.0 copy-start.11
  148.7 0.6 copy-start.12

commit v2 on v1

v2 whole, which is shorter than its diff:
```python
import functools

import jax
import jax.numpy as jnp
from jax import lax
from jax.experimental import pallas as pl
from jax.experimental.pallas import tpu as pltpu
from jax.sharding import Mesh, PartitionSpec as P

NZ, NY, NX, NGP = 8, 4, 2, 4
K = 256
F32, BF16 = jnp.float32, jnp.bfloat16
VM = pl.BlockSpec(memory_space=pltpu.VMEM)
SM = pl.BlockSpec(memory_space=pltpu.SMEM)


def shift(x, axis, n, d):
    return lax.ppermute(x, axis, [(i, (i + d) % n) for i in range(n)])


def pack_kernel(lane, own_ref, out_ref):
    half = NZ * NY * NX * lane
    for z in range(NZ):
        for y in range(NY):
            for x in range(NX):
                p = (z * NY + y) * NX + x
                q = (y * NZ + z) * NX + x
                out_ref[p, :, :lane] = own_ref[0, :, p * lane:(p + 1) * lane]
                out_ref[p, :, lane:] = own_ref[0, :, half + q * lane:half + (q + 1) * lane]


def pack(valence):
    _, nv, ncol = valence.shape
    n = NZ * NY * NX
    lane = ncol // (2 * n)
    return pl.pallas_call(
        functools.partial(pack_kernel, lane),
        out_shape=jax.ShapeDtypeStruct((n, nv, 2 * lane), valence.dtype),
        in_specs=[VM],
        out_specs=VM,
        compiler_params=pltpu.CompilerParams(vmem_limit_bytes=8 << 20),
        cost_estimate=pl.CostEstimate(flops=0, bytes_accessed=4 * nv * ncol, transcendentals=0),
    )(valence)


def pair_kernel(places, first, last, me_ref, w_ref, *refs):
    blocks, rest = refs[:len(places)], refs[len(places):]
    z, y = me_ref[0], me_ref[1]
    half = w_ref.shape[1] // 2
    acc = None if first else rest[0][...]
    for ref, place in zip(blocks, places, strict=True):
        for i, (part, dz, dy) in enumerate(place):
            zz, yy = (z + dz) & (NZ - 1), (y + dy) & (NY - 1)
            column = (zz * NY + yy) * K if part == 0 else half + (yy * NZ + zz) * K
            w = w_ref[:, pl.ds(pl.multiple_of(column, K), K)]
            term = lax.dot_general(ref[i], w, (((1,), (1,)), ((), ())), preferred_element_type=F32)
            acc = term if acc is None else acc + term
    outs = rest[0 if first else 1:]
    if not last:
        outs[0][...] = acc
        return
    scratch = outs[NGP]
    scratch[...] = acc
    rows = outs[0].shape[0]
    for k in range(NGP):
        outs[k][...] = scratch[pl.ds(pl.multiple_of((me_ref[2] ^ k) * rows, 8), rows), :]


def pair_call(me, w, blocks, places, acc=None, last=False):
    n = sum(b.shape[0] for b in blocks)
    rows, g = blocks[0].shape[1], w.shape[0]
    args = [me, w, *blocks] + ([] if acc is None else [acc])
    whole = jax.ShapeDtypeStruct((rows, g), F32)
    share = jax.ShapeDtypeStruct((rows // NGP, g), F32)
    return pl.pallas_call(
        functools.partial(pair_kernel, places, acc is None, last),
        out_shape=[share] * NGP if last else whole,
        in_specs=[SM] + [VM] * (len(args) - 1),
        out_specs=[VM] * NGP if last else VM,
        scratch_shapes=[pltpu.VMEM((rows, g), F32)] if last else [],
        compiler_params=pltpu.CompilerParams(vmem_limit_bytes=16 << 20),
        cost_estimate=pl.CostEstimate(flops=2 * n * rows * g * K, bytes_accessed=n * (rows + g) * K * 2, transcendentals=0),
    )(*args)


def term_kernel(a_ref, b_ref, c_ref, d_ref, cond_ref, out_ref):
    total = (a_ref[...] + b_ref[...]) + (c_ref[...] + d_ref[...])
    rows = total.shape[0]
    hi = total.astype(BF16)
    rest = total - hi.astype(F32)
    mid = rest.astype(BF16)
    low = (rest - mid.astype(F32)).astype(BF16)
    stacked = jnp.concatenate([hi, mid, low], axis=0)
    prod = lax.dot_general(stacked, cond_ref[...], (((1,), (1,)), ((), ())), preferred_element_type=F32)
    term = prod[:rows] + (prod[rows:2 * rows] + prod[2 * rows:])
    width = out_ref.shape[2]
    for z in range(out_ref.shape[0]):
        out_ref[z] = term[:, z * width:(z + 1) * width]


def term_call(parts, cond):
    rows, nc = parts[0].shape[0], cond.shape[0]
    return pl.pallas_call(
        term_kernel,
        out_shape=jax.ShapeDtypeStruct((NZ, rows, nc // NZ), F32),
        in_specs=[VM] * 5,
        out_specs=VM,
        compiler_params=pltpu.CompilerParams(vmem_limit_bytes=8 << 20),
        cost_estimate=pl.CostEstimate(flops=6 * rows * nc * cond.shape[1], bytes_accessed=nc * cond.shape[1] * 2, transcendentals=0),
    )(*parts, cond)


def body(screened, valence, conduction, owner):
    nb = owner.shape[0]
    lane = valence.shape[2] // (2 * NZ * NY * NX)
    z, y, xh = lax.axis_index("z"), lax.axis_index("y"), lax.axis_index("xh")
    gp = lax.axis_index("xl") * 2 + lax.axis_index("c")
    me = jnp.stack([z, y, gp]).astype(jnp.int32)

    recv = lax.all_to_all(pack(valence), ("z", "y", "xh"), 0, 0, tiled=True)
    mine = jnp.concatenate([lax.dynamic_index_in_dim(recv, owner[b], 0, keepdims=False) for b in range(nb)], axis=0)

    other = shift(mine, "xh", NX, 1)
    lo, hi = jnp.where(xh == 0, mine, other), jnp.where(xh == 0, other, mine)
    a = jnp.concatenate([lo[:, :lane], hi[:, :lane]], axis=1)
    b = jnp.concatenate([lo[:, lane:], hi[:, lane:]], axis=1)

    ya = [a, shift(a, "y", NY, 1), shift(a, "y", NY, -1), shift(a, "y", NY, 2)]
    dys = [0, -1, 1, -2]
    zr = zl = b
    zb, dzs = [b], [0]
    hb = b.shape[0] // 2
    for s in (1, 2, 3):
        zr, zl = shift(zr, "z", NZ, 1), shift(zl, "z", NZ, -1)
        zb += [zr, zl]
        dzs += [-s, s]
    zb.append(jnp.concatenate([shift(zr[:hb], "z", NZ, 1), shift(zl[hb:], "z", NZ, -1)], axis=0))
    dzs.append(4)
    sa = jnp.stack(ya)
    sb = jnp.stack(zb)

    def at_a(dz):
        return [(0, dz, d) for d in dys]

    def at_b(dy):
        return [(1, d, dy) for d in dzs]

    a1r, a1l = shift(sa, "z", NZ, 1), shift(sa, "z", NZ, -1)
    a2r, a2l = shift(a1r, "z", NZ, 1), shift(a1l, "z", NZ, -1)
    acc = pair_call(me, screened, [sa, a1r, a1l], [at_a(0), at_a(-1), at_a(1)])
    a2r, a2l, acc = lax.optimization_barrier((a2r, a2l, acc))
    br, bl = shift(sb, "y", NY, 1), shift(sb, "y", NY, -1)
    a3r, a3l = shift(a2r, "z", NZ, 1), shift(a2l, "z", NZ, -1)
    acc = pair_call(me, screened, [sb, a2r, a2l], [at_b(0), at_a(-2), at_a(2)], acc)
    a3r, a3l, acc = lax.optimization_barrier((a3r, a3l, acc))
    a4r, a4l = shift(a3r[:2], "z", NZ, 1), shift(a3l[2:], "z", NZ, -1)
    b2r, b2l = shift(br[:4], "y", NY, 1), shift(bl[4:], "y", NY, -1)
    acc = pair_call(me, screened, [a3r, a3l, br, bl], [at_a(-3), at_a(3), at_b(-1), at_b(1)], acc)
    parts = pair_call(me, screened, [a4r, a4l, b2r, b2l], [at_a(4)[:2], at_a(4)[2:], at_b(2)[:4], at_b(2)[4:]], acc, last=True)

    sums = [parts[0]] + [lax.ppermute(parts[k], ("xl", "c"), [(i, i ^ k) for i in range(NGP)]) for k in (1, 2, 3)]
    term = term_call(sums, conduction)

    zsum = jnp.sum(lax.all_to_all(term, "z", 0, 0, tiled=True), axis=0)
    rows = zsum.T.reshape(NY * NX, zsum.shape[1] // (NY * NX), zsum.shape[0])
    return jnp.sum(lax.all_to_all(rows, ("y", "xh"), 0, 0, tiled=True), axis=0)


def solution(mesh):
    fine = Mesh(mesh.devices.reshape(NZ, NY, NX, 2, 2), ("z", "y", "xh", "xl", "c"))
    ga, gp = ("z", "y", "xh"), ("xl", "c")
    placed = (P(ga, gp), P(ga, None, gp), P(None, ga), P())
    return jax.shard_map(body, mesh=fine, in_specs=placed, out_specs=P(ga, gp), check_vma=False)
```

time: 182 us -> 156 us (0.86)
  local copies, waits for them, and re-layouts: 22.6 us -> 7.17 us
  Pallas kernels: 14.8 us -> 7.6 us
    unnamed x41 -> x19, local copies, waits for them, and re-layouts: 13.1 us -> 4.88 us
    pallas_call x3 -> x5, Pallas kernels: 12.6 us -> 7.31 us  [the longest x4 6.12 us: pair_call(): pl.pallas_call(functools.partial(pair_kernel, places, acc is None, last),...]
    slice x3 -> x2, local copies, waits for them, and re-layouts: 2.64 us -> 0.03 us  [body(): a4r, a4l = (shift(a3r[:2], 'z', NZ, 1), shift(a3l[2:], 'z', NZ, -1))]
    ppermute x24, waiting for transfers between devices: 25.7 us -> 27.7 us  [shift(): return lax.ppermute(x, axis, [(i, (i + d) % n) for i in range(n)])]
    pallas_call x1, Pallas kernels: 2.15 us -> 0.29 us  [term_call(): pl.pallas_call(term_kernel, out_shape=jax.ShapeDtypeStruct((NZ, rows, nc...]
    concatenate x1 -> x0, local copies, waits for them, and re-layouts: 1.84 us -> none  [body(): jnp.concatenate([part_a, part_b], axis=-1)]
  transfers between devices with their start and end apart: 28 -> 28, of which waited for: 15 -> 17; matrix products, arithmetic and copies ran while one was open for 2% -> 1% of each run, Pallas kernels for 5% -> 3%
where the time goes in v2:
time: 156 us; the launch traced here: 155 us
  starting transfers between devices  53 us (34%)
  waiting for transfers between devices  49.1 us (31%)
  blocking collectives  25.6 us (16%)
  between operations  11.2 us (7%)
  Pallas kernels  7.6 us (5%)
  local copies, waits for them, and re-layouts  7.17 us (5%)
    ppermute x24, starting transfers between devices, shift(): return lax.ppermute(x, axis, [(i, (i + d) % n) for i in range(n)])  37.3 us
    ppermute x24, waiting for transfers between devices, shift(): return lax.ppermute(x, axis, [(i, (i + d) % n) for i in range(n)])  27.7 us
    all_to_all x1, waiting for transfers between devices, body(): recv = lax.all_to_all(pack(valence), ('z', 'y', 'xh'), 0, 0, tiled=True)  18 us
    all_to_all x1, blocking collectives, body(): zsum = jnp.sum(lax.all_to_all(term, 'z', 0, 0, tiled=True), axis=0)  15.5 us
    all_to_all x1, starting transfers between devices, body(): recv = lax.all_to_all(pack(valence), ('z', 'y', 'xh'), 0, 0, tiled=True)  13.7 us
    all_to_all x1, blocking collectives, body(): return jnp.sum(lax.all_to_all(rows, ('y', 'xh'), 0, 0, tiled=True), axis=0)  10.1 us
    pallas_call x4, Pallas kernels, pair_call(): pl.pallas_call(functools.partial(pair_kernel, places, acc is None, last),...  6.12 us
    unnamed x19, local copies, waits for them, and re-layouts  4.88 us
  transfers between devices with their start and end apart: 28, of which 17 were waited for; matrix products, arithmetic and copies ran while one was open for 1% of the time, Pallas kernels for 3%

profile of v2, /device:TPU:2, one launch (start us, length us, event | category | flops | bytes accessed | tf_op | source)
XLA Modules:
  0.0 155.1 jit_solution(4328117944917902238)
XLA Ops:
  0.0 1.2 copy-done.1
  1.2 1.2 shard_map.46
  2.4 13.7 %all-to-all-start = ((bf16[64,32,256]{2,1,0:T(8,128)(2,1)}), bf16[64,32,256]{2,1,0:T(8,128)(2,1)S(1)}, u32[]{:S(2)}, u32[]{:S(2)}) async-start(bf16[64,32,256]{2,1,0:T(8,128)(2,1)} %shard_map.46), calls=%async_computation | async-start | bytes 2097152 | tf_op jit(solution)/shard_map/all_to_all | solution.py:120
  16.1 1.5 fusion.4
  28.6 18.0 %all-to-all-done = bf16[64,32,256]{2,1,0:T(8,128)(2,1)S(1)} async-done(((bf16[64,32,256]{2,1,0:T(8,128)(2,1)}), bf16[64,32,256]{2,1,0:T(8,128)(2,1)S(1)}, u32[]{:S(2)}, u32[]{:S(2)}) %all-to-all-start) | async-done | bytes 1048608 | tf_op jit(solution)/shard_map/all_to_all | solution.py:120
  46.6 0.6 collective-permute-start
  47.2 5.6 %collective-permute-done = bf16[192,256]{1,0:T(8,128)(2,1)S(1)} collective-permute-done((bf16[192,256]{1,0:T(8,128)(2,1)S(1)}, bf16[192,256]{1,0:T(8,128)(2,1)S(1)}, u32[]{:S(2)}, u32[]{:S(2)}) %collective-permute-start) | collective-permute-done | bytes 98336 | tf_op jit(solution)/shard_map/ppermute | solution.py:18
  52.9 1.5 collective-permute-start.10
  54.4 1.9 %collective-permute-start.11 = (bf16[192,256]{1,0:T(8,128)(2,1)S(1)}, bf16[192,256]{1,0:T(8,128)(2,1)S(1)}, u32[]{:S(2)}, u32[]{:S(2)}) collective-permute-start(bf16[192,256]{1,0:T(8,128)(2,1)S(1)} %pad_maximum_fusion.2), channel_id=1, source_target_pairs={{0,224},{32,0},{64,32},{96,64},{128,96},{160,128},{192,160},{224,1... | collective-permute-start | bytes 294920 | tf_op jit(solution)/shard_map/ppermute | solution.py:18
  56.5 3.1 %collective-permute-start.2 = (bf16[192,256]{1,0:T(8,128)(2,1)S(1)}, bf16[192,256]{1,0:T(8,128)(2,1)S(1)}, u32[]{:S(2)}, u32[]{:S(2)}) collective-permute-start(bf16[192,256]{1,0:T(8,128)(2,1)S(1)} %get-tuple-element.32), channel_id=1, source_target_pairs={{0,24},{8,0},{16,8},{24,16},{1,25},{9,1},{17,9},{25,17},{2,26},{10... | collective-permute-start | bytes 294920 | tf_op jit(solution)/shard_map/ppermute | solution.py:18
  59.6 2.6 %collective-permute-done.1 = bf16[192,256]{1,0:T(8,128)(2,1)S(1)} collective-permute-done((bf16[192,256]{1,0:T(8,128)(2,1)S(1)}, bf16[192,256]{1,0:T(8,128)(2,1)S(1)}, u32[]{:S(2)}, u32[]{:S(2)}) %collective-permute-start.1) | collective-permute-done | bytes 98336 | tf_op jit(solution)/shard_map/ppermute | solution.py:18
  62.2 0.6 collective-permute-done.2
  62.8 2.9 %collective-permute-done.3 = bf16[192,256]{1,0:T(8,128)(2,1)S(1)} collective-permute-done((bf16[192,256]{1,0:T(8,128)(2,1)S(1)}, bf16[192,256]{1,0:T(8,128)(2,1)S(1)}, u32[]{:S(2)}, u32[]{:S(2)}) %collective-permute-start.3) | collective-permute-done | bytes 98336 | tf_op jit(solution)/shard_map/ppermute | solution.py:18
  66.0 3.1 %collective-permute-start.6 = (bf16[4,192,256]{2,1,0:T(8,128)(2,1)S(1)}, bf16[4,192,256]{2,1,0:T(8,128)(2,1)S(1)}, u32[]{:S(2)}, u32[]{:S(2)}) collective-permute-start(bf16[4,192,256]{2,1,0:T(8,128)(2,1)S(1)} %pad_maximum_fusion.refs_0_), channel_id=1, source_target_pairs={{0,224},{32,0},{64,32},{96,64},{128,96},{160,128},{192,160},{224,1... | collective-permute-start | bytes 1179656 | tf_op jit(solution)/shard_map/ppermute | solution.py:18
  69.1 3.3 %collective-permute-start.13 = (bf16[192,256]{1,0:T(8,128)(2,1)S(1)}, bf16[192,256]{1,0:T(8,128)(2,1)S(1)}, u32[]{:S(2)}, u32[]{:S(2)}) collective-permute-start(bf16[192,256]{1,0:T(8,128)(2,1)S(1)} %collective-permute-done.11), channel_id=1, source_target_pairs={{0,224},{32,0},{64,32},{96,64},{128,96},{160,128},{192,160},{224,1... | collective-permute-start | bytes 294920 | tf_op jit(solution)/shard_map/ppermute | solution.py:18
  72.4 4.5 %collective-permute-done.12 = bf16[192,256]{1,0:T(8,128)(2,1)S(1)} collective-permute-done((bf16[192,256]{1,0:T(8,128)(2,1)S(1)}, bf16[192,256]{1,0:T(8,128)(2,1)S(1)}, u32[]{:S(2)}, u32[]{:S(2)}) %collective-permute-start.12) | collective-permute-done | bytes 98336 | tf_op jit(solution)/shard_map/ppermute | solution.py:18
  77.0 3.3 %collective-permute-start.15 = (bf16[192,256]{1,0:T(8,128)(2,1)S(1)}, bf16[192,256]{1,0:T(8,128)(2,1)S(1)}, u32[]{:S(2)}, u32[]{:S(2)}) collective-permute-start(bf16[192,256]{1,0:T(8,128)(2,1)S(1)} %collective-permute-done.13), channel_id=1, source_target_pairs={{0,224},{32,0},{64,32},{96,64},{128,96},{160,128},{192,160},{224,1... | collective-permute-start | bytes 294920 | tf_op jit(solution)/shard_map/ppermute | solution.py:18
  80.3 2.5 %collective-permute-done.14 = bf16[192,256]{1,0:T(8,128)(2,1)S(1)} collective-permute-done((bf16[192,256]{1,0:T(8,128)(2,1)S(1)}, bf16[192,256]{1,0:T(8,128)(2,1)S(1)}, u32[]{:S(2)}, u32[]{:S(2)}) %collective-permute-start.14) | collective-permute-done | bytes 98336 | tf_op jit(solution)/shard_map/ppermute | solution.py:18
  82.8 3.3 %collective-permute-start.17 = (bf16[96,256]{1,0:T(8,128)(2,1)S(1)}, bf16[96,256]{1,0:T(8,128)(2,1)S(1)}, u32[]{:S(2)}, u32[]{:S(2)}) collective-permute-start(bf16[96,256]{1,0:T(8,128)(2,1)S(1)} %slice.69), channel_id=1, source_target_pairs={{0,224},{32,0},{64,32},{96,64},{128,96},{160,128},{192,160},{224,1... | collective-permute-start | bytes 147464 | tf_op jit(solution)/shard_map/ppermute | solution.py:18
  86.1 2.5 %collective-permute-done.16 = bf16[96,256]{1,0:T(8,128)(2,1)S(1)} collective-permute-done((bf16[96,256]{1,0:T(8,128)(2,1)S(1)}, bf16[96,256]{1,0:T(8,128)(2,1)S(1)}, u32[]{:S(2)}, u32[]{:S(2)}) %collective-permute-start.16) | collective-permute-done | bytes 49184 | tf_op jit(solution)/shard_map/ppermute | solution.py:18
  88.9 3.2 %collective-permute-start.22 = (bf16[8,192,256]{2,1,0:T(8,128)(2,1)S(1)}, bf16[8,192,256]{2,1,0:T(8,128)(2,1)S(1)}, u32[]{:S(2)}, u32[]{:S(2)}) collective-permute-start(bf16[8,192,256]{2,1,0:T(8,128)(2,1)S(1)} %fusion.refs_0_), channel_id=1, source_target_pairs={{0,24},{8,0},{16,8},{24,16},{1,25},{9,1},{17,9},{25,17},{2,26},{10... | collective-permute-start | bytes 2359304 | tf_op jit(solution)/shard_map/ppermute | solution.py:18
  92.2 3.4 %collective-permute-start.7 = (bf16[4,192,256]{2,1,0:T(8,128)(2,1)S(1)}, bf16[4,192,256]{2,1,0:T(8,128)(2,1)}, u32[]{:S(2)}, u32[]{:S(2)}) collective-permute-start(bf16[4,192,256]{2,1,0:T(8,128)(2,1)S(1)} %collective-permute-done.6.refs_2_), channel_id=1, source_target_pairs={{0,224},{32,0},{64,32},{96,64},{128,96},{160,128},{192,160},{224,1... | collective-permute-start | bytes 1179656 | tf_op jit(solution)/shard_map/ppermute | solution.py:18
  95.7 3.4 %copy-done = bf16[256,16384]{1,0:T(8,128)(2,1)S(1)} copy-done((bf16[256,16384]{1,0:T(8,128)(2,1)S(1)}, bf16[256,16384]{1,0:T(8,128)(2,1)}, u32[]{:S(2)}) %copy-start) | copy-done | bytes 8388632
  99.0 1.2 shard_map.47.refs_3_
  100.3 2.4 %collective-permute-done.5.refs_1_ = bf16[4,192,256]{2,1,0:T(8,128)(2,1)} collective-permute-done((bf16[4,192,256]{2,1,0:T(8,128)(2,1)S(1)}, bf16[4,192,256]{2,1,0:T(8,128)(2,1)}, u32[]{:S(2)}, u32[]{:S(2)}) %collective-permute-start.5) | collective-permute-done | bytes 393248 | tf_op jit(solution)/shard_map/ppermute | solution.py:18
  102.7 0.3 collective-permute-done.7.refs_2_
  103.0 1.9 %collective-permute-start.8 = (bf16[4,192,256]{2,1,0:T(8,128)(2,1)}, bf16[4,192,256]{2,1,0:T(8,128)(2,1)S(1)}, u32[]{:S(2)}, u32[]{:S(2)}) collective-permute-start(bf16[4,192,256]{2,1,0:T(8,128)(2,1)} %collective-permute-done.5.refs_1_), channel_id=1, source_target_pairs={{0,32},{32,64},{64,96},{96,128},{128,160},{160,192},{192,224},{224... | collective-permute-start | bytes 1179656 | tf_op jit(solution)/shard_map/ppermute | solution.py:18
  104.9 1.3 collective-permute-start.9
  106.5 3.3 %collective-permute-start.23 = (bf16[4,192,256]{2,1,0:T(8,128)(2,1)S(1)}, bf16[4,192,256]{2,1,0:T(8,128)(2,1)S(1)}, u32[]{:S(2)}, u32[]{:S(2)}) collective-permute-start(bf16[4,192,256]{2,1,0:T(8,128)(2,1)S(1)} %slice.71), channel_id=1, source_target_pairs={{0,24},{8,0},{16,8},{24,16},{1,25},{9,1},{17,9},{25,17},{2,26},{10... | collective-permute-start | bytes 1179656 | tf_op jit(solution)/shard_map/ppermute | solution.py:18
  109.8 2.0 %shard_map.48.refs_4_ = f32[192,256]{1,0:T(8,128)S(1)} custom-call(s32[3]{0:T(128)S(1)} %pad_add_fusion.me_ref, bf16[256,16384]{1,0:T(8,128)(2,1)S(1)} %copy-done, bf16[8,192,256]{2,1,0:T(8,128)(2,1)S(1)} %fusion.refs_0_, bf16[4,192,256]{2,1,0:T(8,128)(2,1)} %collective-permute-done.5.refs_1_, bf16[4,192,256]{2,1,0:T(8,128)(2,1)} %collective-permute-done.7.refs_2_, ...), custom_call_target="tpu_custom_call" | custom-call | flops 402653184 | bytes 3670016 | tf_op jit(solution)/shard_map/pallas_call | solution.py:75
  111.8 0.4 collective-permute-done.8.refs_0_
  112.2 0.7 collective-permute-done.9.refs_1_
  113.0 1.8 %collective-permute-start.18 = (bf16[2,192,256]{2,1,0:T(8,128)(2,1)S(1)}, bf16[2,192,256]{2,1,0:T(8,128)(2,1)S(1)}, u32[]{:S(2)}, u32[]{:S(2)}) collective-permute-start(bf16[2,192,256]{2,1,0:T(8,128)(2,1)S(1)} %slice.60), channel_id=1, source_target_pairs={{0,32},{32,64},{64,96},{96,128},{128,160},{160,192},{192,224},{224... | collective-permute-start | bytes 589832 | tf_op jit(solution)/shard_map/ppermute | solution.py:18
  114.8 1.6 %collective-permute-start.19 = (bf16[2,192,256]{2,1,0:T(8,128)(2,1)S(1)}, bf16[2,192,256]{2,1,0:T(8,128)(2,1)S(1)}, u32[]{:S(2)}, u32[]{:S(2)}) collective-permute-start(bf16[2,192,256]{2,1,0:T(8,128)(2,1)S(1)} %slice.61), channel_id=1, source_target_pairs={{0,224},{32,0},{64,32},{96,64},{128,96},{160,128},{192,160},{224,1... | collective-permute-start | bytes 589832 | tf_op jit(solution)/shard_map/ppermute | solution.py:18
  116.4 1.7 %shard_map.49.refs_4_ = f32[192,256]{1,0:T(8,128)S(1)} custom-call(s32[3]{0:T(128)S(1)} %pad_add_fusion.me_ref, bf16[256,16384]{1,0:T(8,128)(2,1)S(1)} %copy-done, bf16[4,192,256]{2,1,0:T(8,128)(2,1)S(1)} %collective-permute-done.8.refs_0_, bf16[4,192,256]{2,1,0:T(8,128)(2,1)S(1)} %collective-permute-done.9.refs_1_, ...), custom_call_target="tpu_custom_call" | custom-call | flops 603979776 | bytes 5505024 | tf_op jit(solution)/shard_map/pallas_call | solution.py:75
  118.1 1.8 %collective-permute-done.18.refs_0_ = bf16[2,192,256]{2,1,0:T(8,128)(2,1)S(1)} collective-permute-done((bf16[2,192,256]{2,1,0:T(8,128)(2,1)S(1)}, bf16[2,192,256]{2,1,0:T(8,128)(2,1)S(1)}, u32[]{:S(2)}, u32[]{:S(2)}) %collective-permute-start.18) | collective-permute-done | bytes 196640 | tf_op jit(solution)/shard_map/ppermute | solution.py:18
  119.9 0.6 collective-permute-done.19.refs_1_
  120.5 1.2 shard_map.50
  121.9 1.5 collective-permute-start.25
  123.4 0.3 collective-permute-start.26
  123.7 2.3 %collective-permute-done.25.c_ref = f32[48,256]{1,0:T(8,128)S(1)} collective-permute-done((f32[48,256]{1,0:T(8,128)S(1)}, f32[48,256]{1,0:T(8,128)S(1)}, u32[]{:S(2)}, u32[]{:S(2)}) %collective-permute-start.25) | collective-permute-done | bytes 49184 | tf_op jit(solution)/shard_map/ppermute | solution.py:161
  126.1 1.1 collective-permute-done.26.d_ref
  127.1 0.3 shard_map.51
  127.4 15.5 %all_to_all.15 = f32[8,48,128]{2,1,0:T(8,128)S(1)} all-to-all(f32[8,48,128]{2,1,0:T(8,128)S(1)} %shard_map.51), channel_id=1, replica_groups=mesh['z'=8,'y'=4,'xh'=2,'xl'=2,'c'=2] {'z'}, dimensions={0} | all-to-all | bytes 393216 | tf_op jit(solution)/shard_map/all_to_all | solution.py:164
  143.1 10.1 %all_to_all.16 = f32[8,1,768]{2,1,0:T(1,128)S(1)} all-to-all(f32[8,1,768]{2,1,0:T(1,128)S(1)} %reshape.4), channel_id=1, replica_groups=mesh['z'=8,'y'=4,'xh'=2,'xl'=2,'c'=2] {'y','xh'}, dimensions={0} | all-to-all | bytes 49152 | tf_op jit(solution)/shard_map/all_to_all | solution.py:166
  153.2 0.5 broadcast
  153.7 0.7 reduce
  154.5 0.6 reduce_sum.19
  (56 shorter events, 1.8 us)
Async XLA Ops:
  0.0 1.2 copy-start.1
  2.4 44.2 %all-to-all-start = ((bf16[64,32,256]{2,1,0:T(8,128)(2,1)}), bf16[64,32,256]{2,1,0:T(8,128)(2,1)S(1)}, u32[]{:S(2)}, u32[]{:S(2)}) async-start(bf16[64,32,256]{2,1,0:T(8,128)(2,1)} %shard_map.46), calls=%async_computation | async-start | bytes 2097152 | tf_op jit(solution)/shard_map/all_to_all | solution.py:120
  46.6 6.2 %collective-permute-start = (bf16[192,256]{1,0:T(8,128)(2,1)S(1)}, bf16[192,256]{1,0:T(8,128)(2,1)S(1)}, u32[]{:S(2)}, u32[]{:S(2)}) collective-permute-start(bf16[192,256]{1,0:T(8,128)(2,1)S(1)} %constant_dynamic-update-slice_fusion), channel_id=1, source_target_pairs={{0,4},{4,0},{1,5},{5,1},{2,6},{6,2},{3,7},{7,3},{8,12},{12,8},{9,1... | collective-permute-start | bytes 294920 | tf_op jit(solution)/shard_map/ppermute | solution.py:18
  52.9 16.1 %collective-permute-start.10 = (bf16[192,256]{1,0:T(8,128)(2,1)S(1)}, bf16[192,256]{1,0:T(8,128)(2,1)S(1)}, u32[]{:S(2)}, u32[]{:S(2)}) collective-permute-start(bf16[192,256]{1,0:T(8,128)(2,1)S(1)} %pad_maximum_fusion.2), channel_id=1, source_target_pairs={{0,32},{32,64},{64,96},{96,128},{128,160},{160,192},{192,224},{224... | collective-permute-start | bytes 294920 | tf_op jit(solution)/shard_map/ppermute | solution.py:18
  54.4 14.7 %collective-permute-start.11 = (bf16[192,256]{1,0:T(8,128)(2,1)S(1)}, bf16[192,256]{1,0:T(8,128)(2,1)S(1)}, u32[]{:S(2)}, u32[]{:S(2)}) collective-permute-start(bf16[192,256]{1,0:T(8,128)(2,1)S(1)} %pad_maximum_fusion.2), channel_id=1, source_target_pairs={{0,224},{32,0},{64,32},{96,64},{128,96},{160,128},{192,160},{224,1... | collective-permute-start | bytes 294920 | tf_op jit(solution)/shard_map/ppermute | solution.py:18
  56.3 5.9 %collective-permute-start.1 = (bf16[192,256]{1,0:T(8,128)(2,1)S(1)}, bf16[192,256]{1,0:T(8,128)(2,1)S(1)}, u32[]{:S(2)}, u32[]{:S(2)}) collective-permute-start(bf16[192,256]{1,0:T(8,128)(2,1)S(1)} %get-tuple-element.32), channel_id=1, source_target_pairs={{0,8},{8,16},{16,24},{24,0},{1,9},{9,17},{17,25},{25,1},{2,10},{10... | collective-permute-start | bytes 294920 | tf_op jit(solution)/shard_map/ppermute | solution.py:18
  56.5 6.3 %collective-permute-start.2 = (bf16[192,256]{1,0:T(8,128)(2,1)S(1)}, bf16[192,256]{1,0:T(8,128)(2,1)S(1)}, u32[]{:S(2)}, u32[]{:S(2)}) collective-permute-start(bf16[192,256]{1,0:T(8,128)(2,1)S(1)} %get-tuple-element.32), channel_id=1, source_target_pairs={{0,24},{8,0},{16,8},{24,16},{1,25},{9,1},{17,9},{25,17},{2,26},{10... | collective-permute-start | bytes 294920 | tf_op jit(solution)/shard_map/ppermute | solution.py:18
  59.6 6.1 %collective-permute-start.3 = (bf16[192,256]{1,0:T(8,128)(2,1)S(1)}, bf16[192,256]{1,0:T(8,128)(2,1)S(1)}, u32[]{:S(2)}, u32[]{:S(2)}) collective-permute-start(bf16[192,256]{1,0:T(8,128)(2,1)S(1)} %get-tuple-element.32), channel_id=1, source_target_pairs={{0,16},{8,24},{16,0},{24,8},{1,17},{9,25},{17,1},{25,9},{2,18},{10... | collective-permute-start | bytes 294920 | tf_op jit(solution)/shard_map/ppermute | solution.py:18
  65.8 26.4 %collective-permute-start.4 = (bf16[4,192,256]{2,1,0:T(8,128)(2,1)S(1)}, bf16[4,192,256]{2,1,0:T(8,128)(2,1)S(1)}, u32[]{:S(2)}, u32[]{:S(2)}) collective-permute-start(bf16[4,192,256]{2,1,0:T(8,128)(2,1)S(1)} %pad_maximum_fusion.refs_0_), channel_id=1, source_target_pairs={{0,32},{32,64},{64,96},{96,128},{128,160},{160,192},{192,224},{224... | collective-permute-start | bytes 1179656 | tf_op jit(solution)/shard_map/ppermute | solution.py:18
  66.0 26.2 %collective-permute-start.6 = (bf16[4,192,256]{2,1,0:T(8,128)(2,1)S(1)}, bf16[4,192,256]{2,1,0:T(8,128)(2,1)S(1)}, u32[]{:S(2)}, u32[]{:S(2)}) collective-permute-start(bf16[4,192,256]{2,1,0:T(8,128)(2,1)S(1)} %pad_maximum_fusion.refs_0_), channel_id=1, source_target_pairs={{0,224},{32,0},{64,32},{96,64},{128,96},{160,128},{192,160},{224,1... | collective-permute-start | bytes 1179656 | tf_op jit(solution)/shard_map/ppermute | solution.py:18
  69.1 7.9 %collective-permute-start.12 = (bf16[192,256]{1,0:T(8,128)(2,1)S(1)}, bf16[192,256]{1,0:T(8,128)(2,1)S(1)}, u32[]{:S(2)}, u32[]{:S(2)}) collective-permute-start(bf16[192,256]{1,0:T(8,128)(2,1)S(1)} %collective-permute-done.10), channel_id=1, source_target_pairs={{0,32},{32,64},{64,96},{96,128},{128,160},{160,192},{192,224},{224... | collective-permute-start | bytes 294920 | tf_op jit(solution)/shard_map/ppermute | solution.py:18
  69.1 7.8 %collective-permute-start.13 = (bf16[192,256]{1,0:T(8,128)(2,1)S(1)}, bf16[192,256]{1,0:T(8,128)(2,1)S(1)}, u32[]{:S(2)}, u32[]{:S(2)}) collective-permute-start(bf16[192,256]{1,0:T(8,128)(2,1)S(1)} %collective-permute-done.11), channel_id=1, source_target_pairs={{0,224},{32,0},{64,32},{96,64},{128,96},{160,128},{192,160},{224,1... | collective-permute-start | bytes 294920 | tf_op jit(solution)/shard_map/ppermute | solution.py:18
  76.9 5.8 %collective-permute-start.14 = (bf16[192,256]{1,0:T(8,128)(2,1)S(1)}, bf16[192,256]{1,0:T(8,128)(2,1)S(1)}, u32[]{:S(2)}, u32[]{:S(2)}) collective-permute-start(bf16[192,256]{1,0:T(8,128)(2,1)S(1)} %collective-permute-done.12), channel_id=1, source_target_pairs={{0,32},{32,64},{64,96},{96,128},{128,160},{160,192},{192,224},{224... | collective-permute-start | bytes 294920 | tf_op jit(solution)/shard_map/ppermute | solution.py:18
  77.0 5.8 %collective-permute-start.15 = (bf16[192,256]{1,0:T(8,128)(2,1)S(1)}, bf16[192,256]{1,0:T(8,128)(2,1)S(1)}, u32[]{:S(2)}, u32[]{:S(2)}) collective-permute-start(bf16[192,256]{1,0:T(8,128)(2,1)S(1)} %collective-permute-done.13), channel_id=1, source_target_pairs={{0,224},{32,0},{64,32},{96,64},{128,96},{160,128},{192,160},{224,1... | collective-permute-start | bytes 294920 | tf_op jit(solution)/shard_map/ppermute | solution.py:18
  82.8 5.9 %collective-permute-start.16 = (bf16[96,256]{1,0:T(8,128)(2,1)S(1)}, bf16[96,256]{1,0:T(8,128)(2,1)S(1)}, u32[]{:S(2)}, u32[]{:S(2)}) collective-permute-start(bf16[96,256]{1,0:T(8,128)(2,1)S(1)} %slice.68), channel_id=1, source_target_pairs={{0,32},{32,64},{64,96},{96,128},{128,160},{160,192},{192,224},{224... | collective-permute-start | bytes 147464 | tf_op jit(solution)/shard_map/ppermute | solution.py:18
  82.8 5.9 %collective-permute-start.17 = (bf16[96,256]{1,0:T(8,128)(2,1)S(1)}, bf16[96,256]{1,0:T(8,128)(2,1)S(1)}, u32[]{:S(2)}, u32[]{:S(2)}) collective-permute-start(bf16[96,256]{1,0:T(8,128)(2,1)S(1)} %slice.69), channel_id=1, source_target_pairs={{0,224},{32,0},{64,32},{96,64},{128,96},{160,128},{192,160},{224,1... | collective-permute-start | bytes 147464 | tf_op jit(solution)/shard_map/ppermute | solution.py:18
  88.7 17.7 %collective-permute-start.20 = (bf16[8,192,256]{2,1,0:T(8,128)(2,1)S(1)}, bf16[8,192,256]{2,1,0:T(8,128)(2,1)S(1)}, u32[]{:S(2)}, u32[]{:S(2)}) collective-permute-start(bf16[8,192,256]{2,1,0:T(8,128)(2,1)S(1)} %fusion.refs_0_), channel_id=1, source_target_pairs={{0,8},{8,16},{16,24},{24,0},{1,9},{9,17},{17,25},{25,1},{2,10},{10... | collective-permute-start | bytes 2359304 | tf_op jit(solution)/shard_map/ppermute | solution.py:18
  88.9 17.5 %collective-permute-start.22 = (bf16[8,192,256]{2,1,0:T(8,128)(2,1)S(1)}, bf16[8,192,256]{2,1,0:T(8,128)(2,1)S(1)}, u32[]{:S(2)}, u32[]{:S(2)}) collective-permute-start(bf16[8,192,256]{2,1,0:T(8,128)(2,1)S(1)} %fusion.refs_0_), channel_id=1, source_target_pairs={{0,24},{8,0},{16,8},{24,16},{1,25},{9,1},{17,9},{25,17},{2,26},{10... | collective-permute-start | bytes 2359304 | tf_op jit(solution)/shard_map/ppermute | solution.py:18
  92.2 10.5 %collective-permute-start.5 = (bf16[4,192,256]{2,1,0:T(8,128)(2,1)S(1)}, bf16[4,192,256]{2,1,0:T(8,128)(2,1)}, u32[]{:S(2)}, u32[]{:S(2)}) collective-permute-start(bf16[4,192,256]{2,1,0:T(8,128)(2,1)S(1)} %collective-permute-done.4.refs_1_), channel_id=1, source_target_pairs={{0,32},{32,64},{64,96},{96,128},{128,160},{160,192},{192,224},{224... | collective-permute-start | bytes 1179656 | tf_op jit(solution)/shard_map/ppermute | solution.py:18
  92.2 10.8 %collective-permute-start.7 = (bf16[4,192,256]{2,1,0:T(8,128)(2,1)S(1)}, bf16[4,192,256]{2,1,0:T(8,128)(2,1)}, u32[]{:S(2)}, u32[]{:S(2)}) collective-permute-start(bf16[4,192,256]{2,1,0:T(8,128)(2,1)S(1)} %collective-permute-done.6.refs_2_), channel_id=1, source_target_pairs={{0,224},{32,0},{64,32},{96,64},{128,96},{160,128},{192,160},{224,1... | collective-permute-start | bytes 1179656 | tf_op jit(solution)/shard_map/ppermute | solution.py:18
  95.7 3.4 %copy-start = (bf16[256,16384]{1,0:T(8,128)(2,1)S(1)}, bf16[256,16384]{1,0:T(8,128)(2,1)}, u32[]{:S(2)}) copy-start(bf16[256,16384]{1,0:T(8,128)(2,1)} %w_ref.7) | copy-start | bytes 25165828
  103.0 9.2 %collective-permute-start.8 = (bf16[4,192,256]{2,1,0:T(8,128)(2,1)}, bf16[4,192,256]{2,1,0:T(8,128)(2,1)S(1)}, u32[]{:S(2)}, u32[]{:S(2)}) collective-permute-start(bf16[4,192,256]{2,1,0:T(8,128)(2,1)} %collective-permute-done.5.refs_1_), channel_id=1, source_target_pairs={{0,32},{32,64},{64,96},{96,128},{128,160},{160,192},{192,224},{224... | collective-permute-start | bytes 1179656 | tf_op jit(solution)/shard_map/ppermute | solution.py:18
  104.9 8.0 %collective-permute-start.9 = (bf16[4,192,256]{2,1,0:T(8,128)(2,1)}, bf16[4,192,256]{2,1,0:T(8,128)(2,1)S(1)}, u32[]{:S(2)}, u32[]{:S(2)}) collective-permute-start(bf16[4,192,256]{2,1,0:T(8,128)(2,1)} %collective-permute-done.7.refs_2_), channel_id=1, source_target_pairs={{0,224},{32,0},{64,32},{96,64},{128,96},{160,128},{192,160},{224,1... | collective-permute-start | bytes 1179656 | tf_op jit(solution)/shard_map/ppermute | solution.py:18
  106.4 14.2 %collective-permute-start.21 = (bf16[4,192,256]{2,1,0:T(8,128)(2,1)S(1)}, bf16[4,192,256]{2,1,0:T(8,128)(2,1)S(1)}, u32[]{:S(2)}, u32[]{:S(2)}) collective-permute-start(bf16[4,192,256]{2,1,0:T(8,128)(2,1)S(1)} %slice.70), channel_id=1, source_target_pairs={{0,8},{8,16},{16,24},{24,0},{1,9},{9,17},{17,25},{25,1},{2,10},{10... | collective-permute-start | bytes 1179656 | tf_op jit(solution)/shard_map/ppermute | solution.py:18
  106.5 14.0 %collective-permute-start.23 = (bf16[4,192,256]{2,1,0:T(8,128)(2,1)S(1)}, bf16[4,192,256]{2,1,0:T(8,128)(2,1)S(1)}, u32[]{:S(2)}, u32[]{:S(2)}) collective-permute-start(bf16[4,192,256]{2,1,0:T(8,128)(2,1)S(1)} %slice.71), channel_id=1, source_target_pairs={{0,24},{8,0},{16,8},{24,16},{1,25},{9,1},{17,9},{25,17},{2,26},{10... | collective-permute-start | bytes 1179656 | tf_op jit(solution)/shard_map/ppermute | solution.py:18
  113.0 7.0 %collective-permute-start.18 = (bf16[2,192,256]{2,1,0:T(8,128)(2,1)S(1)}, bf16[2,192,256]{2,1,0:T(8,128)(2,1)S(1)}, u32[]{:S(2)}, u32[]{:S(2)}) collective-permute-start(bf16[2,192,256]{2,1,0:T(8,128)(2,1)S(1)} %slice.60), channel_id=1, source_target_pairs={{0,32},{32,64},{64,96},{96,128},{128,160},{160,192},{192,224},{224... | collective-permute-start | bytes 589832 | tf_op jit(solution)/shard_map/ppermute | solution.py:18
  114.8 12.3 %copy-start.2 = (bf16[1024,256]{1,0:T(8,128)(2,1)S(1)}, bf16[1024,256]{1,0:T(8,128)(2,1)}, u32[]{:S(2)}) copy-start(bf16[1024,256]{1,0:T(8,128)(2,1)} %cond_ref.1) | copy-start | bytes 1572868
  114.8 5.7 %collective-permute-start.19 = (bf16[2,192,256]{2,1,0:T(8,128)(2,1)S(1)}, bf16[2,192,256]{2,1,0:T(8,128)(2,1)S(1)}, u32[]{:S(2)}, u32[]{:S(2)}) collective-permute-start(bf16[2,192,256]{2,1,0:T(8,128)(2,1)S(1)} %slice.61), channel_id=1, source_target_pairs={{0,224},{32,0},{64,32},{96,64},{128,96},{160,128},{192,160},{224,1... | collective-permute-start | bytes 589832 | tf_op jit(solution)/shard_map/ppermute | solution.py:18
  121.8 2.0 %collective-permute-start.24 = (f32[48,256]{1,0:T(8,128)S(1)}, f32[48,256]{1,0:T(8,128)S(1)}, u32[]{:S(2)}, u32[]{:S(2)}) collective-permute-start(f32[48,256]{1,0:T(8,128)S(1)} %get-tuple-element.22), channel_id=1, source_target_pairs={{0,1},{1,0},{2,3},{3,2},{4,5},{5,4},{6,7},{7,6},{8,9},{9,8},{10,11... | collective-permute-start | bytes 147464 | tf_op jit(solution)/shard_map/ppermute | solution.py:161
  121.9 4.2 %collective-permute-start.25 = (f32[48,256]{1,0:T(8,128)S(1)}, f32[48,256]{1,0:T(8,128)S(1)}, u32[]{:S(2)}, u32[]{:S(2)}) collective-permute-start(f32[48,256]{1,0:T(8,128)S(1)} %get-tuple-element.23), channel_id=1, source_target_pairs={{0,2},{1,3},{2,0},{3,1},{4,6},{5,7},{6,4},{7,5},{8,10},{9,11},{10,... | collective-permute-start | bytes 147464 | tf_op jit(solution)/shard_map/ppermute | solution.py:161
  123.4 3.7 %collective-permute-start.26 = (f32[48,256]{1,0:T(8,128)S(1)}, f32[48,256]{1,0:T(8,128)S(1)}, u32[]{:S(2)}, u32[]{:S(2)}) collective-permute-start(f32[48,256]{1,0:T(8,128)S(1)} %get-tuple-element.24), channel_id=1, source_target_pairs={{0,3},{1,2},{2,1},{3,0},{4,7},{5,6},{6,5},{7,4},{8,11},{9,10},{10,... | collective-permute-start | bytes 147464 | tf_op jit(solution)/shard_map/ppermute | solution.py:161

commit v3 on v2

--- a/solution.py
+++ b/solution.py
@@ -83,6 +83,20 @@
     )(*args)
 
 
+def regroup(tile, group):
+    n = tile.shape[0]
+    row = lax.broadcasted_iota(jnp.int32, tile.shape, 0)
+    column = lax.broadcasted_iota(jnp.int32, tile.shape, 1) // group
+    s = 1
+    while s < n:
+        r, q = (row & s) != 0, (column & s) != 0
+        lower = pltpu.roll(pltpu.roll(tile, n - s, 0), s * group, 1)
+        upper = pltpu.roll(pltpu.roll(tile, s, 0), tile.shape[1] - s * group, 1)
+        tile = jnp.where(r == q, tile, jnp.where(q, lower, upper))
+        s *= 2
+    return tile
+
+
 def term_kernel(a_ref, b_ref, c_ref, d_ref, cond_ref, out_ref):
     total = (a_ref[...] + b_ref[...]) + (c_ref[...] + d_ref[...])
     rows = total.shape[0]
@@ -93,21 +107,45 @@
     stacked = jnp.concatenate([hi, mid, low], axis=0)
     prod = lax.dot_general(stacked, cond_ref[...], (((1,), (1,)), ((), ())), preferred_element_type=F32)
     term = prod[:rows] + (prod[rows:2 * rows] + prod[2 * rows:])
-    width = out_ref.shape[2]
-    for z in range(out_ref.shape[0]):
-        out_ref[z] = term[:, z * width:(z + 1) * width]
+    for a in range(rows // 8):
+        for t in range(term.shape[1] // 128):
+            out_ref[8 * t:8 * t + 8, a, :] = regroup(term[8 * a:8 * a + 8, 128 * t:128 * t + 128], 16)
+    out_ref[:, rows // 8:, :] = jnp.zeros((out_ref.shape[0], out_ref.shape[1] - rows // 8, 128), F32)
 
 
 def term_call(parts, cond):
     rows, nc = parts[0].shape[0], cond.shape[0]
     return pl.pallas_call(
         term_kernel,
-        out_shape=jax.ShapeDtypeStruct((NZ, rows, nc // NZ), F32),
+        out_shape=jax.ShapeDtypeStruct((NZ * NY * NX, 8, 128), F32),
         in_specs=[VM] * 5,
         out_specs=VM,
         compiler_params=pltpu.CompilerParams(vmem_limit_bytes=8 << 20),
         cost_estimate=pl.CostEstimate(flops=6 * rows * nc * cond.shape[1], bytes_accessed=nc * cond.shape[1] * 2, transcendentals=0),
     )(*parts, cond)
+
+
+def final_kernel(x_ref, out_ref, scratch):
+    total = jnp.sum(x_ref[...], axis=0)
+    rows, columns = out_ref.shape
+    scratch[...] = jnp.zeros(scratch.shape, F32)
+    for b in range(8):
+        moved = total if b == 0 else pltpu.roll(total, 128 - rows * b, 1)
+        for a in range(columns // 8):
+            scratch[8 * a + b:8 * a + b + 1, :] = moved[a:a + 1, :]
+    out_ref[...] = scratch[...].T[:rows, :columns]
+
+
+def final_call(x, shape):
+    return pl.pallas_call(
+        final_kernel,
+        out_shape=jax.ShapeDtypeStruct(shape, F32),
+        in_specs=[VM],
+        out_specs=VM,
+        scratch_shapes=[pltpu.VMEM((128, 128), F32)],
+        compiler_params=pltpu.CompilerParams(vmem_limit_bytes=8 << 20),
+        cost_estimate=pl.CostEstimate(flops=x.size, bytes_accessed=x.size * 4, transcendentals=0),
+    )(x)
 
 
 def body(screened, valence, conduction, owner):
@@ -161,9 +199,8 @@
     sums = [parts[0]] + [lax.ppermute(parts[k], ("xl", "c"), [(i, i ^ k) for i in range(NGP)]) for k in (1, 2, 3)]
     term = term_call(sums, conduction)
 
-    zsum = jnp.sum(lax.all_to_all(term, "z", 0, 0, tiled=True), axis=0)
-    rows = zsum.T.reshape(NY * NX, zsum.shape[1] // (NY * NX), zsum.shape[0])
-    return jnp.sum(lax.all_to_all(rows, ("y", "xh"), 0, 0, tiled=True), axis=0)
+    recv = lax.all_to_all(term, ("z", "y", "xh"), 0, 0, tiled=True)
+    return final_call(recv, (conduction.shape[0] // (NZ * NY * NX), nb * valence.shape[1] // NGP))
 
 
 def solution(mesh):

time: 156 us -> 150 us (0.962)
  blocking collectives: 25.6 us -> 20.5 us
    all_to_all x2 -> x1, blocking collectives: 25.6 us -> 20.5 us  [body(): recv = lax.all_to_all(term, ('z', 'y', 'xh'), 0, 0, tiled=True)]
    unnamed x19 -> x17, local copies, waits for them, and re-layouts: 4.88 us -> 4.68 us
where the time goes in v3:
time: 150 us; the launch traced here: 149 us
  starting transfers between devices  53 us (35%)
  waiting for transfers between devices  48.4 us (32%)
  blocking collectives  20.5 us (14%)
  between operations  11.9 us (8%)
  Pallas kernels  8.72 us (6%)
  local copies, waits for them, and re-layouts  6.37 us (4%)
    ppermute x24, starting transfers between devices, shift(): return lax.ppermute(x, axis, [(i, (i + d) % n) for i in range(n)])  37.3 us
    ppermute x24, waiting for transfers between devices, shift(): return lax.ppermute(x, axis, [(i, (i + d) % n) for i in range(n)])  27.7 us
    all_to_all x1, blocking collectives, body(): recv = lax.all_to_all(term, ('z', 'y', 'xh'), 0, 0, tiled=True)  20.5 us
    all_to_all x1, waiting for transfers between devices, body(): recv = lax.all_to_all(pack(valence), ('z', 'y', 'xh'), 0, 0, tiled=True)  17.2 us
    all_to_all x1, starting transfers between devices, body(): recv = lax.all_to_all(pack(valence), ('z', 'y', 'xh'), 0, 0, tiled=True)  13.7 us
    pallas_call x4, Pallas kernels, pair_call(): pl.pallas_call(functools.partial(pair_kernel, places, acc is None, last),...  6.12 us
    unnamed x17, local copies, waits for them, and re-layouts  4.68 us
    ppermute x3, waiting for transfers between devices, body(): lax.ppermute(parts[k], ('xl', 'c'), [(i, i ^ k) for i in range(NGP)])  3.37 us
  transfers between devices with their start and end apart: 28, of which 17 were waited for; matrix products, arithmetic and copies ran while one was open for 1% of the time, Pallas kernels for 3%

profile of v3, /device:TPU:2, one launch (start us, length us, event | category | flops | bytes accessed | tf_op | source)
XLA Modules:
  0.0 149.0 jit_solution(2313646470008029373)
XLA Ops:
  0.0 1.2 copy-done.1
  1.2 1.2 shard_map.46
  2.4 13.7 %all-to-all-start = ((bf16[64,32,256]{2,1,0:T(8,128)(2,1)}), bf16[64,32,256]{2,1,0:T(8,128)(2,1)S(1)}, u32[]{:S(2)}, u32[]{:S(2)}) async-start(bf16[64,32,256]{2,1,0:T(8,128)(2,1)} %shard_map.46), calls=%async_computation | async-start | bytes 2097152 | tf_op jit(solution)/shard_map/all_to_all | solution.py:158
  16.1 1.5 %fusion.4 = (s32[1]{0:T(128)}, s32[1]{0:T(128)}, s32[1]{0:T(128)}, s32[1]{0:T(128)}, s32[1]{0:T(128)}, /*index=5*/s32[1]{0:T(128)}) fusion(s32[6]{0:T(128)} %param.7), kind=kLoop, calls=%fused_computation.24 | loop fusion | bytes 48 | tf_op jit(solution)/shard_map/slice | solution.py:159
  29.3 17.2 %all-to-all-done = bf16[64,32,256]{2,1,0:T(8,128)(2,1)S(1)} async-done(((bf16[64,32,256]{2,1,0:T(8,128)(2,1)}), bf16[64,32,256]{2,1,0:T(8,128)(2,1)S(1)}, u32[]{:S(2)}, u32[]{:S(2)}) %all-to-all-start) | async-done | bytes 1048608 | tf_op jit(solution)/shard_map/all_to_all | solution.py:158
  46.6 0.6 collective-permute-start
  47.2 5.6 %collective-permute-done = bf16[192,256]{1,0:T(8,128)(2,1)S(1)} collective-permute-done((bf16[192,256]{1,0:T(8,128)(2,1)S(1)}, bf16[192,256]{1,0:T(8,128)(2,1)S(1)}, u32[]{:S(2)}, u32[]{:S(2)}) %collective-permute-start) | collective-permute-done | bytes 98336 | tf_op jit(solution)/shard_map/ppermute | solution.py:18
  52.9 1.5 collective-permute-start.10
  54.4 1.9 %collective-permute-start.11 = (bf16[192,256]{1,0:T(8,128)(2,1)S(1)}, bf16[192,256]{1,0:T(8,128)(2,1)S(1)}, u32[]{:S(2)}, u32[]{:S(2)}) collective-permute-start(bf16[192,256]{1,0:T(8,128)(2,1)S(1)} %pad_maximum_fusion.2), channel_id=1, source_target_pairs={{0,224},{32,0},{64,32},{96,64},{128,96},{160,128},{192,160},{224,1... | collective-permute-start | bytes 294920 | tf_op jit(solution)/shard_map/ppermute | solution.py:18
  56.2 0.2 collective-permute-start.1
  56.5 3.1 %collective-permute-start.2 = (bf16[192,256]{1,0:T(8,128)(2,1)S(1)}, bf16[192,256]{1,0:T(8,128)(2,1)S(1)}, u32[]{:S(2)}, u32[]{:S(2)}) collective-permute-start(bf16[192,256]{1,0:T(8,128)(2,1)S(1)} %get-tuple-element.32), channel_id=1, source_target_pairs={{0,24},{8,0},{16,8},{24,16},{1,25},{9,1},{17,9},{25,17},{2,26},{10... | collective-permute-start | bytes 294920 | tf_op jit(solution)/shard_map/ppermute | solution.py:18
  59.6 2.6 %collective-permute-done.1 = bf16[192,256]{1,0:T(8,128)(2,1)S(1)} collective-permute-done((bf16[192,256]{1,0:T(8,128)(2,1)S(1)}, bf16[192,256]{1,0:T(8,128)(2,1)S(1)}, u32[]{:S(2)}, u32[]{:S(2)}) %collective-permute-start.1) | collective-permute-done | bytes 98336 | tf_op jit(solution)/shard_map/ppermute | solution.py:18
  62.1 0.6 collective-permute-done.2
  62.8 2.9 %collective-permute-done.3 = bf16[192,256]{1,0:T(8,128)(2,1)S(1)} collective-permute-done((bf16[192,256]{1,0:T(8,128)(2,1)S(1)}, bf16[192,256]{1,0:T(8,128)(2,1)S(1)}, u32[]{:S(2)}, u32[]{:S(2)}) %collective-permute-start.3) | collective-permute-done | bytes 98336 | tf_op jit(solution)/shard_map/ppermute | solution.py:18
  65.7 0.3 collective-permute-start.4
  66.0 3.1 %collective-permute-start.6 = (bf16[4,192,256]{2,1,0:T(8,128)(2,1)S(1)}, bf16[4,192,256]{2,1,0:T(8,128)(2,1)S(1)}, u32[]{:S(2)}, u32[]{:S(2)}) collective-permute-start(bf16[4,192,256]{2,1,0:T(8,128)(2,1)S(1)} %pad_maximum_fusion.refs_0_), channel_id=1, source_target_pairs={{0,224},{32,0},{64,32},{96,64},{128,96},{160,128},{192,160},{224,1... | collective-permute-start | bytes 1179656 | tf_op jit(solution)/shard_map/ppermute | solution.py:18
  69.1 3.3 %collective-permute-start.13 = (bf16[192,256]{1,0:T(8,128)(2,1)S(1)}, bf16[192,256]{1,0:T(8,128)(2,1)S(1)}, u32[]{:S(2)}, u32[]{:S(2)}) collective-permute-start(bf16[192,256]{1,0:T(8,128)(2,1)S(1)} %collective-permute-done.11), channel_id=1, source_target_pairs={{0,224},{32,0},{64,32},{96,64},{128,96},{160,128},{192,160},{224,1... | collective-permute-start | bytes 294920 | tf_op jit(solution)/shard_map/ppermute | solution.py:18
  72.4 4.5 %collective-permute-done.12 = bf16[192,256]{1,0:T(8,128)(2,1)S(1)} collective-permute-done((bf16[192,256]{1,0:T(8,128)(2,1)S(1)}, bf16[192,256]{1,0:T(8,128)(2,1)S(1)}, u32[]{:S(2)}, u32[]{:S(2)}) %collective-permute-start.12) | collective-permute-done | bytes 98336 | tf_op jit(solution)/shard_map/ppermute | solution.py:18
  76.9 3.3 %collective-permute-start.15 = (bf16[192,256]{1,0:T(8,128)(2,1)S(1)}, bf16[192,256]{1,0:T(8,128)(2,1)S(1)}, u32[]{:S(2)}, u32[]{:S(2)}) collective-permute-start(bf16[192,256]{1,0:T(8,128)(2,1)S(1)} %collective-permute-done.13), channel_id=1, source_target_pairs={{0,224},{32,0},{64,32},{96,64},{128,96},{160,128},{192,160},{224,1... | collective-permute-start | bytes 294920 | tf_op jit(solution)/shard_map/ppermute | solution.py:18
  80.2 2.5 %collective-permute-done.14 = bf16[192,256]{1,0:T(8,128)(2,1)S(1)} collective-permute-done((bf16[192,256]{1,0:T(8,128)(2,1)S(1)}, bf16[192,256]{1,0:T(8,128)(2,1)S(1)}, u32[]{:S(2)}, u32[]{:S(2)}) %collective-permute-start.14) | collective-permute-done | bytes 98336 | tf_op jit(solution)/shard_map/ppermute | solution.py:18
  82.8 3.3 %collective-permute-start.17 = (bf16[96,256]{1,0:T(8,128)(2,1)S(1)}, bf16[96,256]{1,0:T(8,128)(2,1)S(1)}, u32[]{:S(2)}, u32[]{:S(2)}) collective-permute-start(bf16[96,256]{1,0:T(8,128)(2,1)S(1)} %slice.69), channel_id=1, source_target_pairs={{0,224},{32,0},{64,32},{96,64},{128,96},{160,128},{192,160},{224,1... | collective-permute-start | bytes 147464 | tf_op jit(solution)/shard_map/ppermute | solution.py:18
  86.1 2.5 %collective-permute-done.16 = bf16[96,256]{1,0:T(8,128)(2,1)S(1)} collective-permute-done((bf16[96,256]{1,0:T(8,128)(2,1)S(1)}, bf16[96,256]{1,0:T(8,128)(2,1)S(1)}, u32[]{:S(2)}, u32[]{:S(2)}) %collective-permute-start.16) | collective-permute-done | bytes 49184 | tf_op jit(solution)/shard_map/ppermute | solution.py:18
  88.6 0.3 collective-permute-start.20
  88.9 3.2 %collective-permute-start.22 = (bf16[8,192,256]{2,1,0:T(8,128)(2,1)S(1)}, bf16[8,192,256]{2,1,0:T(8,128)(2,1)S(1)}, u32[]{:S(2)}, u32[]{:S(2)}) collective-permute-start(bf16[8,192,256]{2,1,0:T(8,128)(2,1)S(1)} %fusion.refs_0_), channel_id=1, source_target_pairs={{0,24},{8,0},{16,8},{24,16},{1,25},{9,1},{17,9},{25,17},{2,26},{10... | collective-permute-start | bytes 2359304 | tf_op jit(solution)/shard_map/ppermute | solution.py:18
  92.1 3.4 %collective-permute-start.7 = (bf16[4,192,256]{2,1,0:T(8,128)(2,1)S(1)}, bf16[4,192,256]{2,1,0:T(8,128)(2,1)}, u32[]{:S(2)}, u32[]{:S(2)}) collective-permute-start(bf16[4,192,256]{2,1,0:T(8,128)(2,1)S(1)} %collective-permute-done.6.refs_2_), channel_id=1, source_target_pairs={{0,224},{32,0},{64,32},{96,64},{128,96},{160,128},{192,160},{224,1... | collective-permute-start | bytes 1179656 | tf_op jit(solution)/shard_map/ppermute | solution.py:18
  95.6 3.4 %copy-done = bf16[256,16384]{1,0:T(8,128)(2,1)S(1)} copy-done((bf16[256,16384]{1,0:T(8,128)(2,1)S(1)}, bf16[256,16384]{1,0:T(8,128)(2,1)}, u32[]{:S(2)}) %copy-start) | copy-done | bytes 8388632
  99.0 1.2 shard_map.47.refs_3_
  100.2 2.4 %collective-permute-done.5.refs_1_ = bf16[4,192,256]{2,1,0:T(8,128)(2,1)} collective-permute-done((bf16[4,192,256]{2,1,0:T(8,128)(2,1)S(1)}, bf16[4,192,256]{2,1,0:T(8,128)(2,1)}, u32[]{:S(2)}, u32[]{:S(2)}) %collective-permute-start.5) | collective-permute-done | bytes 393248 | tf_op jit(solution)/shard_map/ppermute | solution.py:18
  102.7 0.3 collective-permute-done.7.refs_2_
  103.0 1.9 %collective-permute-start.8 = (bf16[4,192,256]{2,1,0:T(8,128)(2,1)}, bf16[4,192,256]{2,1,0:T(8,128)(2,1)S(1)}, u32[]{:S(2)}, u32[]{:S(2)}) collective-permute-start(bf16[4,192,256]{2,1,0:T(8,128)(2,1)} %collective-permute-done.5.refs_1_), channel_id=1, source_target_pairs={{0,32},{32,64},{64,96},{96,128},{128,160},{160,192},{192,224},{224... | collective-permute-start | bytes 1179656 | tf_op jit(solution)/shard_map/ppermute | solution.py:18
  104.9 1.3 collective-permute-start.9
  106.5 3.3 %collective-permute-start.23 = (bf16[4,192,256]{2,1,0:T(8,128)(2,1)S(1)}, bf16[4,192,256]{2,1,0:T(8,128)(2,1)S(1)}, u32[]{:S(2)}, u32[]{:S(2)}) collective-permute-start(bf16[4,192,256]{2,1,0:T(8,128)(2,1)S(1)} %slice.71), channel_id=1, source_target_pairs={{0,24},{8,0},{16,8},{24,16},{1,25},{9,1},{17,9},{25,17},{2,26},{10... | collective-permute-start | bytes 1179656 | tf_op jit(solution)/shard_map/ppermute | solution.py:18
  109.8 2.0 %shard_map.48.refs_4_ = f32[192,256]{1,0:T(8,128)S(1)} custom-call(s32[3]{0:T(128)S(1)} %pad_add_fusion.me_ref, bf16[256,16384]{1,0:T(8,128)(2,1)S(1)} %copy-done, bf16[8,192,256]{2,1,0:T(8,128)(2,1)S(1)} %fusion.refs_0_, bf16[4,192,256]{2,1,0:T(8,128)(2,1)} %collective-permute-done.5.refs_1_, bf16[4,192,256]{2,1,0:T(8,128)(2,1)} %collective-permute-done.7.refs_2_, ...), custom_call_target="tpu_custom_call" | custom-call | flops 402653184 | bytes 3670016 | tf_op jit(solution)/shard_map/pallas_call | solution.py:75
  111.8 0.4 collective-permute-done.8.refs_0_
  112.2 0.7 collective-permute-done.9.refs_1_
  112.9 1.8 %collective-permute-start.18 = (bf16[2,192,256]{2,1,0:T(8,128)(2,1)S(1)}, bf16[2,192,256]{2,1,0:T(8,128)(2,1)S(1)}, u32[]{:S(2)}, u32[]{:S(2)}) collective-permute-start(bf16[2,192,256]{2,1,0:T(8,128)(2,1)S(1)} %slice.60), channel_id=1, source_target_pairs={{0,32},{32,64},{64,96},{96,128},{128,160},{160,192},{192,224},{224... | collective-permute-start | bytes 589832 | tf_op jit(solution)/shard_map/ppermute | solution.py:18
  114.7 1.6 %collective-permute-start.19 = (bf16[2,192,256]{2,1,0:T(8,128)(2,1)S(1)}, bf16[2,192,256]{2,1,0:T(8,128)(2,1)S(1)}, u32[]{:S(2)}, u32[]{:S(2)}) collective-permute-start(bf16[2,192,256]{2,1,0:T(8,128)(2,1)S(1)} %slice.61), channel_id=1, source_target_pairs={{0,224},{32,0},{64,32},{96,64},{128,96},{160,128},{192,160},{224,1... | collective-permute-start | bytes 589832 | tf_op jit(solution)/shard_map/ppermute | solution.py:18
  116.3 1.7 %shard_map.49.refs_4_ = f32[192,256]{1,0:T(8,128)S(1)} custom-call(s32[3]{0:T(128)S(1)} %pad_add_fusion.me_ref, bf16[256,16384]{1,0:T(8,128)(2,1)S(1)} %copy-done, bf16[4,192,256]{2,1,0:T(8,128)(2,1)S(1)} %collective-permute-done.8.refs_0_, bf16[4,192,256]{2,1,0:T(8,128)(2,1)S(1)} %collective-permute-done.9.refs_1_, ...), custom_call_target="tpu_custom_call" | custom-call | flops 603979776 | bytes 5505024 | tf_op jit(solution)/shard_map/pallas_call | solution.py:75
  118.0 1.8 %collective-permute-done.18.refs_0_ = bf16[2,192,256]{2,1,0:T(8,128)(2,1)S(1)} collective-permute-done((bf16[2,192,256]{2,1,0:T(8,128)(2,1)S(1)}, bf16[2,192,256]{2,1,0:T(8,128)(2,1)S(1)}, u32[]{:S(2)}, u32[]{:S(2)}) %collective-permute-start.18) | collective-permute-done | bytes 196640 | tf_op jit(solution)/shard_map/ppermute | solution.py:18
  119.9 0.6 collective-permute-done.19.refs_1_
  120.5 1.2 shard_map.50
  121.8 1.5 %collective-permute-start.25 = (f32[48,256]{1,0:T(8,128)S(1)}, f32[48,256]{1,0:T(8,128)S(1)}, u32[]{:S(2)}, u32[]{:S(2)}) collective-permute-start(f32[48,256]{1,0:T(8,128)S(1)} %get-tuple-element.23), channel_id=1, source_target_pairs={{0,2},{1,3},{2,0},{3,1},{4,6},{5,7},{6,4},{7,5},{8,10},{9,11},{10,... | collective-permute-start | bytes 147464 | tf_op jit(solution)/shard_map/ppermute | solution.py:199
  123.4 0.3 collective-permute-start.26
  123.7 2.3 %collective-permute-done.25.c_ref = f32[48,256]{1,0:T(8,128)S(1)} collective-permute-done((f32[48,256]{1,0:T(8,128)S(1)}, f32[48,256]{1,0:T(8,128)S(1)}, u32[]{:S(2)}, u32[]{:S(2)}) %collective-permute-start.25) | collective-permute-done | bytes 49184 | tf_op jit(solution)/shard_map/ppermute | solution.py:199
  126.0 1.1 collective-permute-done.26.d_ref
  127.1 0.6 shard_map.51
  127.7 20.5 %all_to_all.10.x_ref = f32[64,8,128]{2,1,0:T(8,128)S(1)} all-to-all(f32[64,8,128]{2,1,0:T(8,128)S(1)} %shard_map.51), channel_id=1, replica_groups=mesh['z'=8,'y'=4,'xh'=2,'xl'=2,'c'=2] {'z','y','xh'}, dimensions={0} | all-to-all | bytes 524288 | tf_op jit(solution)/shard_map/all_to_all | solution.py:202
  148.2 0.8 shard_map.52
  (49 shorter events, 0.7 us)
Async XLA Ops:
  0.0 1.2 copy-start.1
  2.4 44.2 %all-to-all-start = ((bf16[64,32,256]{2,1,0:T(8,128)(2,1)}), bf16[64,32,256]{2,1,0:T(8,128)(2,1)S(1)}, u32[]{:S(2)}, u32[]{:S(2)}) async-start(bf16[64,32,256]{2,1,0:T(8,128)(2,1)} %shard_map.46), calls=%async_computation | async-start | bytes 2097152 | tf_op jit(solution)/shard_map/all_to_all | solution.py:158
  46.6 6.2 %collective-permute-start = (bf16[192,256]{1,0:T(8,128)(2,1)S(1)}, bf16[192,256]{1,0:T(8,128)(2,1)S(1)}, u32[]{:S(2)}, u32[]{:S(2)}) collective-permute-start(bf16[192,256]{1,0:T(8,128)(2,1)S(1)} %constant_dynamic-update-slice_fusion), channel_id=1, source_target_pairs={{0,4},{4,0},{1,5},{5,1},{2,6},{6,2},{3,7},{7,3},{8,12},{12,8},{9,1... | collective-permute-start | bytes 294920 | tf_op jit(solution)/shard_map/ppermute | solution.py:18
  52.9 16.1 %collective-permute-start.10 = (bf16[192,256]{1,0:T(8,128)(2,1)S(1)}, bf16[192,256]{1,0:T(8,128)(2,1)S(1)}, u32[]{:S(2)}, u32[]{:S(2)}) collective-permute-start(bf16[192,256]{1,0:T(8,128)(2,1)S(1)} %pad_maximum_fusion.2), channel_id=1, source_target_pairs={{0,32},{32,64},{64,96},{96,128},{128,160},{160,192},{192,224},{224... | collective-permute-start | bytes 294920 | tf_op jit(solution)/shard_map/ppermute | solution.py:18
  54.4 14.7 %collective-permute-start.11 = (bf16[192,256]{1,0:T(8,128)(2,1)S(1)}, bf16[192,256]{1,0:T(8,128)(2,1)S(1)}, u32[]{:S(2)}, u32[]{:S(2)}) collective-permute-start(bf16[192,256]{1,0:T(8,128)(2,1)S(1)} %pad_maximum_fusion.2), channel_id=1, source_target_pairs={{0,224},{32,0},{64,32},{96,64},{128,96},{160,128},{192,160},{224,1... | collective-permute-start | bytes 294920 | tf_op jit(solution)/shard_map/ppermute | solution.py:18
  56.2 5.9 %collective-permute-start.1 = (bf16[192,256]{1,0:T(8,128)(2,1)S(1)}, bf16[192,256]{1,0:T(8,128)(2,1)S(1)}, u32[]{:S(2)}, u32[]{:S(2)}) collective-permute-start(bf16[192,256]{1,0:T(8,128)(2,1)S(1)} %get-tuple-element.32), channel_id=1, source_target_pairs={{0,8},{8,16},{16,24},{24,0},{1,9},{9,17},{17,25},{25,1},{2,10},{10... | collective-permute-start | bytes 294920 | tf_op jit(solution)/shard_map/ppermute | solution.py:18
  56.5 6.3 %collective-permute-start.2 = (bf16[192,256]{1,0:T(8,128)(2,1)S(1)}, bf16[192,256]{1,0:T(8,128)(2,1)S(1)}, u32[]{:S(2)}, u32[]{:S(2)}) collective-permute-start(bf16[192,256]{1,0:T(8,128)(2,1)S(1)} %get-tuple-element.32), channel_id=1, source_target_pairs={{0,24},{8,0},{16,8},{24,16},{1,25},{9,1},{17,9},{25,17},{2,26},{10... | collective-permute-start | bytes 294920 | tf_op jit(solution)/shard_map/ppermute | solution.py:18
  59.6 6.1 %collective-permute-start.3 = (bf16[192,256]{1,0:T(8,128)(2,1)S(1)}, bf16[192,256]{1,0:T(8,128)(2,1)S(1)}, u32[]{:S(2)}, u32[]{:S(2)}) collective-permute-start(bf16[192,256]{1,0:T(8,128)(2,1)S(1)} %get-tuple-element.32), channel_id=1, source_target_pairs={{0,16},{8,24},{16,0},{24,8},{1,17},{9,25},{17,1},{25,9},{2,18},{10... | collective-permute-start | bytes 294920 | tf_op jit(solution)/shard_map/ppermute | solution.py:18
  65.7 26.4 %collective-permute-start.4 = (bf16[4,192,256]{2,1,0:T(8,128)(2,1)S(1)}, bf16[4,192,256]{2,1,0:T(8,128)(2,1)S(1)}, u32[]{:S(2)}, u32[]{:S(2)}) collective-permute-start(bf16[4,192,256]{2,1,0:T(8,128)(2,1)S(1)} %pad_maximum_fusion.refs_0_), channel_id=1, source_target_pairs={{0,32},{32,64},{64,96},{96,128},{128,160},{160,192},{192,224},{224... | collective-permute-start | bytes 1179656 | tf_op jit(solution)/shard_map/ppermute | solution.py:18
  66.0 26.2 %collective-permute-start.6 = (bf16[4,192,256]{2,1,0:T(8,128)(2,1)S(1)}, bf16[4,192,256]{2,1,0:T(8,128)(2,1)S(1)}, u32[]{:S(2)}, u32[]{:S(2)}) collective-permute-start(bf16[4,192,256]{2,1,0:T(8,128)(2,1)S(1)} %pad_maximum_fusion.refs_0_), channel_id=1, source_target_pairs={{0,224},{32,0},{64,32},{96,64},{128,96},{160,128},{192,160},{224,1... | collective-permute-start | bytes 1179656 | tf_op jit(solution)/shard_map/ppermute | solution.py:18
  69.0 7.9 %collective-permute-start.12 = (bf16[192,256]{1,0:T(8,128)(2,1)S(1)}, bf16[192,256]{1,0:T(8,128)(2,1)S(1)}, u32[]{:S(2)}, u32[]{:S(2)}) collective-permute-start(bf16[192,256]{1,0:T(8,128)(2,1)S(1)} %collective-permute-done.10), channel_id=1, source_target_pairs={{0,32},{32,64},{64,96},{96,128},{128,160},{160,192},{192,224},{224... | collective-permute-start | bytes 294920 | tf_op jit(solution)/shard_map/ppermute | solution.py:18
  69.1 7.8 %collective-permute-start.13 = (bf16[192,256]{1,0:T(8,128)(2,1)S(1)}, bf16[192,256]{1,0:T(8,128)(2,1)S(1)}, u32[]{:S(2)}, u32[]{:S(2)}) collective-permute-start(bf16[192,256]{1,0:T(8,128)(2,1)S(1)} %collective-permute-done.11), channel_id=1, source_target_pairs={{0,224},{32,0},{64,32},{96,64},{128,96},{160,128},{192,160},{224,1... | collective-permute-start | bytes 294920 | tf_op jit(solution)/shard_map/ppermute | solution.py:18
  76.9 5.8 %collective-permute-start.14 = (bf16[192,256]{1,0:T(8,128)(2,1)S(1)}, bf16[192,256]{1,0:T(8,128)(2,1)S(1)}, u32[]{:S(2)}, u32[]{:S(2)}) collective-permute-start(bf16[192,256]{1,0:T(8,128)(2,1)S(1)} %collective-permute-done.12), channel_id=1, source_target_pairs={{0,32},{32,64},{64,96},{96,128},{128,160},{160,192},{192,224},{224... | collective-permute-start | bytes 294920 | tf_op jit(solution)/shard_map/ppermute | solution.py:18
  76.9 5.8 %collective-permute-start.15 = (bf16[192,256]{1,0:T(8,128)(2,1)S(1)}, bf16[192,256]{1,0:T(8,128)(2,1)S(1)}, u32[]{:S(2)}, u32[]{:S(2)}) collective-permute-start(bf16[192,256]{1,0:T(8,128)(2,1)S(1)} %collective-permute-done.13), channel_id=1, source_target_pairs={{0,224},{32,0},{64,32},{96,64},{128,96},{160,128},{192,160},{224,1... | collective-permute-start | bytes 294920 | tf_op jit(solution)/shard_map/ppermute | solution.py:18
  82.7 5.9 %collective-permute-start.16 = (bf16[96,256]{1,0:T(8,128)(2,1)S(1)}, bf16[96,256]{1,0:T(8,128)(2,1)S(1)}, u32[]{:S(2)}, u32[]{:S(2)}) collective-permute-start(bf16[96,256]{1,0:T(8,128)(2,1)S(1)} %slice.68), channel_id=1, source_target_pairs={{0,32},{32,64},{64,96},{96,128},{128,160},{160,192},{192,224},{224... | collective-permute-start | bytes 147464 | tf_op jit(solution)/shard_map/ppermute | solution.py:18
  82.8 5.9 %collective-permute-start.17 = (bf16[96,256]{1,0:T(8,128)(2,1)S(1)}, bf16[96,256]{1,0:T(8,128)(2,1)S(1)}, u32[]{:S(2)}, u32[]{:S(2)}) collective-permute-start(bf16[96,256]{1,0:T(8,128)(2,1)S(1)} %slice.69), channel_id=1, source_target_pairs={{0,224},{32,0},{64,32},{96,64},{128,96},{160,128},{192,160},{224,1... | collective-permute-start | bytes 147464 | tf_op jit(solution)/shard_map/ppermute | solution.py:18
  88.6 17.7 %collective-permute-start.20 = (bf16[8,192,256]{2,1,0:T(8,128)(2,1)S(1)}, bf16[8,192,256]{2,1,0:T(8,128)(2,1)S(1)}, u32[]{:S(2)}, u32[]{:S(2)}) collective-permute-start(bf16[8,192,256]{2,1,0:T(8,128)(2,1)S(1)} %fusion.refs_0_), channel_id=1, source_target_pairs={{0,8},{8,16},{16,24},{24,0},{1,9},{9,17},{17,25},{25,1},{2,10},{10... | collective-permute-start | bytes 2359304 | tf_op jit(solution)/shard_map/ppermute | solution.py:18
  88.9 17.5 %collective-permute-start.22 = (bf16[8,192,256]{2,1,0:T(8,128)(2,1)S(1)}, bf16[8,192,256]{2,1,0:T(8,128)(2,1)S(1)}, u32[]{:S(2)}, u32[]{:S(2)}) collective-permute-start(bf16[8,192,256]{2,1,0:T(8,128)(2,1)S(1)} %fusion.refs_0_), channel_id=1, source_target_pairs={{0,24},{8,0},{16,8},{24,16},{1,25},{9,1},{17,9},{25,17},{2,26},{10... | collective-permute-start | bytes 2359304 | tf_op jit(solution)/shard_map/ppermute | solution.py:18
  92.1 10.5 %collective-permute-start.5 = (bf16[4,192,256]{2,1,0:T(8,128)(2,1)S(1)}, bf16[4,192,256]{2,1,0:T(8,128)(2,1)}, u32[]{:S(2)}, u32[]{:S(2)}) collective-permute-start(bf16[4,192,256]{2,1,0:T(8,128)(2,1)S(1)} %collective-permute-done.4.refs_1_), channel_id=1, source_target_pairs={{0,32},{32,64},{64,96},{96,128},{128,160},{160,192},{192,224},{224... | collective-permute-start | bytes 1179656 | tf_op jit(solution)/shard_map/ppermute | solution.py:18
  92.1 10.8 %collective-permute-start.7 = (bf16[4,192,256]{2,1,0:T(8,128)(2,1)S(1)}, bf16[4,192,256]{2,1,0:T(8,128)(2,1)}, u32[]{:S(2)}, u32[]{:S(2)}) collective-permute-start(bf16[4,192,256]{2,1,0:T(8,128)(2,1)S(1)} %collective-permute-done.6.refs_2_), channel_id=1, source_target_pairs={{0,224},{32,0},{64,32},{96,64},{128,96},{160,128},{192,160},{224,1... | collective-permute-start | bytes 1179656 | tf_op jit(solution)/shard_map/ppermute | solution.py:18
  95.6 3.4 %copy-start = (bf16[256,16384]{1,0:T(8,128)(2,1)S(1)}, bf16[256,16384]{1,0:T(8,128)(2,1)}, u32[]{:S(2)}) copy-start(bf16[256,16384]{1,0:T(8,128)(2,1)} %w_ref.7) | copy-start | bytes 25165828
  103.0 9.2 %collective-permute-start.8 = (bf16[4,192,256]{2,1,0:T(8,128)(2,1)}, bf16[4,192,256]{2,1,0:T(8,128)(2,1)S(1)}, u32[]{:S(2)}, u32[]{:S(2)}) collective-permute-start(bf16[4,192,256]{2,1,0:T(8,128)(2,1)} %collective-permute-done.5.refs_1_), channel_id=1, source_target_pairs={{0,32},{32,64},{64,96},{96,128},{128,160},{160,192},{192,224},{224... | collective-permute-start | bytes 1179656 | tf_op jit(solution)/shard_map/ppermute | solution.py:18
  104.9 8.0 %collective-permute-start.9 = (bf16[4,192,256]{2,1,0:T(8,128)(2,1)}, bf16[4,192,256]{2,1,0:T(8,128)(2,1)S(1)}, u32[]{:S(2)}, u32[]{:S(2)}) collective-permute-start(bf16[4,192,256]{2,1,0:T(8,128)(2,1)} %collective-permute-done.7.refs_2_), channel_id=1, source_target_pairs={{0,224},{32,0},{64,32},{96,64},{128,96},{160,128},{192,160},{224,1... | collective-permute-start | bytes 1179656 | tf_op jit(solution)/shard_map/ppermute | solution.py:18
  106.3 14.2 %collective-permute-start.21 = (bf16[4,192,256]{2,1,0:T(8,128)(2,1)S(1)}, bf16[4,192,256]{2,1,0:T(8,128)(2,1)S(1)}, u32[]{:S(2)}, u32[]{:S(2)}) collective-permute-start(bf16[4,192,256]{2,1,0:T(8,128)(2,1)S(1)} %slice.70), channel_id=1, source_target_pairs={{0,8},{8,16},{16,24},{24,0},{1,9},{9,17},{17,25},{25,1},{2,10},{10... | collective-permute-start | bytes 1179656 | tf_op jit(solution)/shard_map/ppermute | solution.py:18
  106.5 14.0 %collective-permute-start.23 = (bf16[4,192,256]{2,1,0:T(8,128)(2,1)S(1)}, bf16[4,192,256]{2,1,0:T(8,128)(2,1)S(1)}, u32[]{:S(2)}, u32[]{:S(2)}) collective-permute-start(bf16[4,192,256]{2,1,0:T(8,128)(2,1)S(1)} %slice.71), channel_id=1, source_target_pairs={{0,24},{8,0},{16,8},{24,16},{1,25},{9,1},{17,9},{25,17},{2,26},{10... | collective-permute-start | bytes 1179656 | tf_op jit(solution)/shard_map/ppermute | solution.py:18
  112.9 7.0 %collective-permute-start.18 = (bf16[2,192,256]{2,1,0:T(8,128)(2,1)S(1)}, bf16[2,192,256]{2,1,0:T(8,128)(2,1)S(1)}, u32[]{:S(2)}, u32[]{:S(2)}) collective-permute-start(bf16[2,192,256]{2,1,0:T(8,128)(2,1)S(1)} %slice.60), channel_id=1, source_target_pairs={{0,32},{32,64},{64,96},{96,128},{128,160},{160,192},{192,224},{224... | collective-permute-start | bytes 589832 | tf_op jit(solution)/shard_map/ppermute | solution.py:18
  114.7 12.3 %copy-start.2 = (bf16[1024,256]{1,0:T(8,128)(2,1)S(1)}, bf16[1024,256]{1,0:T(8,128)(2,1)}, u32[]{:S(2)}) copy-start(bf16[1024,256]{1,0:T(8,128)(2,1)} %cond_ref.1) | copy-start | bytes 1572868
  114.7 5.7 %collective-permute-start.19 = (bf16[2,192,256]{2,1,0:T(8,128)(2,1)S(1)}, bf16[2,192,256]{2,1,0:T(8,128)(2,1)S(1)}, u32[]{:S(2)}, u32[]{:S(2)}) collective-permute-start(bf16[2,192,256]{2,1,0:T(8,128)(2,1)S(1)} %slice.61), channel_id=1, source_target_pairs={{0,224},{32,0},{64,32},{96,64},{128,96},{160,128},{192,160},{224,1... | collective-permute-start | bytes 589832 | tf_op jit(solution)/shard_map/ppermute | solution.py:18
  121.7 2.0 %collective-permute-start.24 = (f32[48,256]{1,0:T(8,128)S(1)}, f32[48,256]{1,0:T(8,128)S(1)}, u32[]{:S(2)}, u32[]{:S(2)}) collective-permute-start(f32[48,256]{1,0:T(8,128)S(1)} %get-tuple-element.22), channel_id=1, source_target_pairs={{0,1},{1,0},{2,3},{3,2},{4,5},{5,4},{6,7},{7,6},{8,9},{9,8},{10,11... | collective-permute-start | bytes 147464 | tf_op jit(solution)/shard_map/ppermute | solution.py:199
  121.8 4.2 %collective-permute-start.25 = (f32[48,256]{1,0:T(8,128)S(1)}, f32[48,256]{1,0:T(8,128)S(1)}, u32[]{:S(2)}, u32[]{:S(2)}) collective-permute-start(f32[48,256]{1,0:T(8,128)S(1)} %get-tuple-element.23), channel_id=1, source_target_pairs={{0,2},{1,3},{2,0},{3,1},{4,6},{5,7},{6,4},{7,5},{8,10},{9,11},{10,... | collective-permute-start | bytes 147464 | tf_op jit(solution)/shard_map/ppermute | solution.py:199
  123.4 3.7 %collective-permute-start.26 = (f32[48,256]{1,0:T(8,128)S(1)}, f32[48,256]{1,0:T(8,128)S(1)}, u32[]{:S(2)}, u32[]{:S(2)}) collective-permute-start(f32[48,256]{1,0:T(8,128)S(1)} %get-tuple-element.24), channel_id=1, source_target_pairs={{0,3},{1,2},{2,1},{3,0},{4,7},{5,6},{6,5},{7,4},{8,11},{9,10},{10,... | collective-permute-start | bytes 147464 | tf_op jit(solution)/shard_map/ppermute | solution.py:199

commit v4 on v3

--- a/solution.py
+++ b/solution.py
@@ -18,24 +18,20 @@
     return lax.ppermute(x, axis, [(i, (i + d) % n) for i in range(n)])
 
 
-def pack_kernel(lane, own_ref, out_ref):
-    half = NZ * NY * NX * lane
+def pack_kernel(own_ref, out_ref):
+    half = NZ * NY * K
     for z in range(NZ):
         for y in range(NY):
-            for x in range(NX):
-                p = (z * NY + y) * NX + x
-                q = (y * NZ + z) * NX + x
-                out_ref[p, :, :lane] = own_ref[0, :, p * lane:(p + 1) * lane]
-                out_ref[p, :, lane:] = own_ref[0, :, half + q * lane:half + (q + 1) * lane]
+            p, q = z * NY + y, y * NZ + z
+            out_ref[p, :, :K] = own_ref[0, :, p * K:(p + 1) * K]
+            out_ref[p, :, K:] = own_ref[0, :, half + q * K:half + (q + 1) * K]
 
 
 def pack(valence):
     _, nv, ncol = valence.shape
-    n = NZ * NY * NX
-    lane = ncol // (2 * n)
-    return pl.pallas_call(
-        functools.partial(pack_kernel, lane),
-        out_shape=jax.ShapeDtypeStruct((n, nv, 2 * lane), valence.dtype),
+    return pl.pallas_call(
+        pack_kernel,
+        out_shape=jax.ShapeDtypeStruct((NZ * NY, nv, 2 * K), valence.dtype),
         in_specs=[VM],
         out_specs=VM,
         compiler_params=pltpu.CompilerParams(vmem_limit_bytes=8 << 20),
@@ -150,51 +146,48 @@
 
 def body(screened, valence, conduction, owner):
     nb = owner.shape[0]
-    lane = valence.shape[2] // (2 * NZ * NY * NX)
     z, y, xh = lax.axis_index("z"), lax.axis_index("y"), lax.axis_index("xh")
     gp = lax.axis_index("xl") * 2 + lax.axis_index("c")
     me = jnp.stack([z, y, gp]).astype(jnp.int32)
 
-    recv = lax.all_to_all(pack(valence), ("z", "y", "xh"), 0, 0, tiled=True)
-    mine = jnp.concatenate([lax.dynamic_index_in_dim(recv, owner[b], 0, keepdims=False) for b in range(nb)], axis=0)
-
+    recv = lax.all_to_all(pack(valence), ("z", "y"), 0, 0, tiled=True)
+    mine = jnp.stack([lax.dynamic_index_in_dim(recv, owner[b] // NX, 0, keepdims=False) for b in range(nb)])
     other = shift(mine, "xh", NX, 1)
-    lo, hi = jnp.where(xh == 0, mine, other), jnp.where(xh == 0, other, mine)
-    a = jnp.concatenate([lo[:, :lane], hi[:, :lane]], axis=1)
-    b = jnp.concatenate([lo[:, lane:], hi[:, lane:]], axis=1)
+    here = (owner % NX == xh)[:, None, None]
+    a = jnp.where(here, mine[:, :, :K], other[:, :, :K]).reshape(-1, K)
+    b = jnp.where(here, mine[:, :, K:], other[:, :, K:]).reshape(-1, K)
 
     ya = [a, shift(a, "y", NY, 1), shift(a, "y", NY, -1), shift(a, "y", NY, 2)]
     dys = [0, -1, 1, -2]
-    zr = zl = b
-    zb, dzs = [b], [0]
-    hb = b.shape[0] // 2
-    for s in (1, 2, 3):
-        zr, zl = shift(zr, "z", NZ, 1), shift(zl, "z", NZ, -1)
-        zb += [zr, zl]
-        dzs += [-s, s]
-    zb.append(jnp.concatenate([shift(zr[:hb], "z", NZ, 1), shift(zl[hb:], "z", NZ, -1)], axis=0))
-    dzs.append(4)
-    sa = jnp.stack(ya)
-    sb = jnp.stack(zb)
+    dzs = [0, -1, 1, -2, 2, -3, 3, -4]
+    z1r, z1l = shift(b, "z", NZ, 1), shift(b, "z", NZ, -1)
+    sa, z1r, z1l = lax.optimization_barrier((jnp.stack(ya), z1r, z1l))
+    a1r, a1l = shift(sa, "z", NZ, 1), shift(sa, "z", NZ, -1)
+    z2r, z2l = shift(z1r, "z", NZ, 1), shift(z1l, "z", NZ, -1)
+    acc = pair_call(me, screened, [sa], [[(0, 0, d) for d in dys]])
+    a1r, a1l, z2r, z2l, acc = lax.optimization_barrier((a1r, a1l, z2r, z2l, acc))
+    z3r, z3l = shift(z2r, "z", NZ, 1), shift(z2l, "z", NZ, -1)
+    acc = pair_call(me, screened, [a1r, a1l], [[(0, -1, d) for d in dys], [(0, 1, d) for d in dys]], acc)
+    z3r, z3l, acc = lax.optimization_barrier((z3r, z3l, acc))
+    zb = [b, z1r, z1l, z2r, z2l, z3r, z3l, shift(z3r, "z", NZ, 1)]
+    sb0, sb1 = jnp.stack(zb[:4]), jnp.stack(zb[4:])
 
     def at_a(dz):
         return [(0, dz, d) for d in dys]
 
-    def at_b(dy):
-        return [(1, d, dy) for d in dzs]
-
-    a1r, a1l = shift(sa, "z", NZ, 1), shift(sa, "z", NZ, -1)
+    def at_b(dy, h):
+        return [(1, d, dy) for d in dzs[4 * h:4 * h + 4]]
+
     a2r, a2l = shift(a1r, "z", NZ, 1), shift(a1l, "z", NZ, -1)
-    acc = pair_call(me, screened, [sa, a1r, a1l], [at_a(0), at_a(-1), at_a(1)])
-    a2r, a2l, acc = lax.optimization_barrier((a2r, a2l, acc))
-    br, bl = shift(sb, "y", NY, 1), shift(sb, "y", NY, -1)
+    br0, br1 = shift(sb0, "y", NY, 1), shift(sb1, "y", NY, 1)
+    bl0, bl1 = shift(sb0, "y", NY, -1), shift(sb1, "y", NY, -1)
     a3r, a3l = shift(a2r, "z", NZ, 1), shift(a2l, "z", NZ, -1)
-    acc = pair_call(me, screened, [sb, a2r, a2l], [at_b(0), at_a(-2), at_a(2)], acc)
+    acc = pair_call(me, screened, [sb0, sb1, a2r, a2l], [at_b(0, 0), at_b(0, 1), at_a(-2), at_a(2)], acc)
     a3r, a3l, acc = lax.optimization_barrier((a3r, a3l, acc))
     a4r, a4l = shift(a3r[:2], "z", NZ, 1), shift(a3l[2:], "z", NZ, -1)
-    b2r, b2l = shift(br[:4], "y", NY, 1), shift(bl[4:], "y", NY, -1)
-    acc = pair_call(me, screened, [a3r, a3l, br, bl], [at_a(-3), at_a(3), at_b(-1), at_b(1)], acc)
-    parts = pair_call(me, screened, [a4r, a4l, b2r, b2l], [at_a(4)[:2], at_a(4)[2:], at_b(2)[:4], at_b(2)[4:]], acc, last=True)
+    b2r, b2l = shift(br0, "y", NY, 1), shift(bl1, "y", NY, -1)
+    acc = pair_call(me, screened, [a3r, a3l, br0, br1, bl0, bl1], [at_a(-3), at_a(3), at_b(-1, 0), at_b(-1, 1), at_b(1, 0), at_b(1, 1)], acc)
+    parts = pair_call(me, screened, [a4r, a4l, b2r, b2l], [at_a(4)[:2], at_a(4)[2:], at_b(2, 0), at_b(2, 1)], acc, last=True)
 
     sums = [parts[0]] + [lax.ppermute(parts[k], ("xl", "c"), [(i, i ^ k) for i in range(NGP)]) for k in (1, 2, 3)]
     term = term_call(sums, conduction)

time: 150 us -> 146 us (0.973)
  waiting for transfers between devices: 48.4 us -> 40.9 us
  between operations: 11.9 us -> 15.4 us
  starting transfers between devices: 53 us -> 50.5 us
  blocking collectives: 20.5 us -> 22.3 us
    all_to_all x1, waiting for transfers between devices: 17.2 us -> 11.3 us  [body(): recv = lax.all_to_all(pack(valence), ('z', 'y'), 0, 0, tiled=True)]
    all_to_all x1, starting transfers between devices: 13.7 us -> 11.5 us  [body(): recv = lax.all_to_all(pack(valence), ('z', 'y'), 0, 0, tiled=True)]
    all_to_all x1, blocking collectives: 20.5 us -> 22.3 us  [body(): recv = lax.all_to_all(term, ('z', 'y', 'xh'), 0, 0, tiled=True)]
    ppermute x24 -> x25, waiting for transfers between devices: 27.7 us -> 26.7 us  [shift(): return lax.ppermute(x, axis, [(i, (i + d) % n) for i in range(n)])]
    ppermute x24 -> x25, starting transfers between devices: 37.3 us -> 37.1 us  [shift(): return lax.ppermute(x, axis, [(i, (i + d) % n) for i in range(n)])]
    pallas_call x4 -> x5, Pallas kernels: 6.12 us -> 6.27 us  [pair_call(): pl.pallas_call(functools.partial(pair_kernel, places, acc is None, last),...]
    unnamed x17 -> x11, local copies, waits for them, and re-layouts: 4.68 us -> 4.65 us
  transfers between devices with their start and end apart: 28 -> 29, of which waited for: 17 -> 11; matrix products, arithmetic and copies ran while one was open for 1% -> 2% of each run, Pallas kernels for 3% -> 3%
where the time goes in v4:
time: 146 us; the launch traced here: 145 us
  starting transfers between devices  50.5 us (35%)
  waiting for transfers between devices  40.9 us (28%)
  blocking collectives  22.3 us (15%)
  between operations  15.4 us (11%)
  Pallas kernels  8.78 us (6%)
  local copies, waits for them, and re-layouts  6.24 us (4%)
    ppermute x25, starting transfers between devices, shift(): return lax.ppermute(x, axis, [(i, (i + d) % n) for i in range(n)])  37.1 us
    ppermute x25, waiting for transfers between devices, shift(): return lax.ppermute(x, axis, [(i, (i + d) % n) for i in range(n)])  26.7 us
    all_to_all x1, blocking collectives, body(): recv = lax.all_to_all(term, ('z', 'y', 'xh'), 0, 0, tiled=True)  22.3 us
    all_to_all x1, starting transfers between devices, body(): recv = lax.all_to_all(pack(valence), ('z', 'y'), 0, 0, tiled=True)  11.5 us
    all_to_all x1, waiting for transfers between devices, body(): recv = lax.all_to_all(pack(valence), ('z', 'y'), 0, 0, tiled=True)  11.3 us
    pallas_call x5, Pallas kernels, pair_call(): pl.pallas_call(functools.partial(pair_kernel, places, acc is None, last),...  6.27 us
    unnamed x11, local copies, waits for them, and re-layouts  4.65 us
  transfers between devices with their start and end apart: 29, of which 11 were waited for; matrix products, arithmetic and copies ran while one was open for 2% of the time, Pallas kernels for 3%

profile of v4, /device:TPU:2, one launch (start us, length us, event | category | flops | bytes accessed | tf_op | source)
XLA Modules:
  0.0 145.1 jit_solution(16669742146952470880)
XLA Ops:
  0.0 1.2 copy-done.1
  1.2 1.1 shard_map.46
  2.3 11.5 %all-to-all-start = ((bf16[32,32,512]{2,1,0:T(8,128)(2,1)}), bf16[32,32,512]{2,1,0:T(8,128)(2,1)S(1)}, u32[]{:S(2)}, u32[]{:S(2)}) async-start(bf16[32,32,512]{2,1,0:T(8,128)(2,1)} %shard_map.46), calls=%async_computation | async-start | bytes 2097152 | tf_op jit(solution)/shard_map/all_to_all | solution.py:153
  13.8 1.6 %fusion.2 = (s32[1]{0:T(128)}, s32[1]{0:T(128)}, s32[1]{0:T(128)}, s32[1]{0:T(128)}, s32[1]{0:T(128)}, /*index=5*/s32[1]{0:T(128)}) fusion(s32[6]{0:T(128)} %param.7), kind=kLoop, calls=%fused_computation.17 | loop fusion | bytes 48 | tf_op jit(solution)/shard_map/slice | solution.py:154
  30.5 11.3 %all-to-all-done = bf16[32,32,512]{2,1,0:T(8,128)(2,1)S(1)} async-done(((bf16[32,32,512]{2,1,0:T(8,128)(2,1)}), bf16[32,32,512]{2,1,0:T(8,128)(2,1)S(1)}, u32[]{:S(2)}, u32[]{:S(2)}) %all-to-all-start) | async-done | bytes 1048608 | tf_op jit(solution)/shard_map/all_to_all | solution.py:153
  41.9 2.2 %collective-permute-start = (bf16[6,32,512]{2,1,0:T(8,128)(2,1)S(1)}, bf16[6,32,512]{2,1,0:T(8,128)(2,1)S(1)}, u32[]{:S(2)}, u32[]{:S(2)}) collective-permute-start(bf16[6,32,512]{2,1,0:T(8,128)(2,1)S(1)} %dynamic-slice_dynamic-update-slice_fusion), channel_id=1, source_target_pairs={{0,4},{4,0},{1,5},{5,1},{2,6},{6,2},{3,7},{7,3},{8,12},{12,8},{9,1... | collective-permute-start | bytes 589832 | tf_op jit(solution)/shard_map/ppermute | solution.py:18
  44.2 0.7 fusion
  44.8 4.4 %collective-permute-done = bf16[6,32,512]{2,1,0:T(8,128)(2,1)S(1)} collective-permute-done((bf16[6,32,512]{2,1,0:T(8,128)(2,1)S(1)}, bf16[6,32,512]{2,1,0:T(8,128)(2,1)S(1)}, u32[]{:S(2)}, u32[]{:S(2)}) %collective-permute-start) | collective-permute-done | bytes 196640 | tf_op jit(solution)/shard_map/ppermute | solution.py:18
  49.2 0.1 slice_select_fusion
  49.3 1.8 %collective-permute-start.1 = (bf16[192,256]{1,0:T(8,128)(2,1)S(1)}, bf16[192,256]{1,0:T(8,128)(2,1)S(1)}, u32[]{:S(2)}, u32[]{:S(2)}) collective-permute-start(bf16[192,256]{1,0:T(8,128)(2,1)S(1)} %bitcast.26), channel_id=1, source_target_pairs={{0,8},{8,16},{16,24},{24,0},{1,9},{9,17},{17,25},{25,1},{2,10},{10... | collective-permute-start | bytes 294920 | tf_op jit(solution)/shard_map/ppermute | solution.py:18
  51.2 1.5 %collective-permute-start.2 = (bf16[192,256]{1,0:T(8,128)(2,1)S(1)}, bf16[192,256]{1,0:T(8,128)(2,1)S(1)}, u32[]{:S(2)}, u32[]{:S(2)}) collective-permute-start(bf16[192,256]{1,0:T(8,128)(2,1)S(1)} %bitcast.27), channel_id=1, source_target_pairs={{0,24},{8,0},{16,8},{24,16},{1,25},{9,1},{17,9},{25,17},{2,26},{10... | collective-permute-start | bytes 294920 | tf_op jit(solution)/shard_map/ppermute | solution.py:18
  52.6 2.1 %collective-permute-start.3 = (bf16[192,256]{1,0:T(8,128)(2,1)S(1)}, bf16[192,256]{1,0:T(8,128)(2,1)S(1)}, u32[]{:S(2)}, u32[]{:S(2)}) collective-permute-start(bf16[192,256]{1,0:T(8,128)(2,1)S(1)} %bitcast.28), channel_id=1, source_target_pairs={{0,16},{8,24},{16,0},{24,8},{1,17},{9,25},{17,1},{25,9},{2,18},{10... | collective-permute-start | bytes 294920 | tf_op jit(solution)/shard_map/ppermute | solution.py:18
  54.7 0.6 collective-permute-start.4
  55.3 2.6 %collective-permute-start.5 = (bf16[192,256]{1,0:T(8,128)(2,1)S(1)}, bf16[192,256]{1,0:T(8,128)(2,1)S(1)}, u32[]{:S(2)}, u32[]{:S(2)}) collective-permute-start(bf16[192,256]{1,0:T(8,128)(2,1)S(1)} %bitcast.24), channel_id=1, source_target_pairs={{0,224},{32,0},{64,32},{96,64},{128,96},{160,128},{192,160},{224,1... | collective-permute-start | bytes 294920 | tf_op jit(solution)/shard_map/ppermute | solution.py:18
  57.9 0.8 collective-permute-done.3
  58.8 2.6 %collective-permute-done.4 = bf16[192,256]{1,0:T(8,128)(2,1)S(1)} collective-permute-done((bf16[192,256]{1,0:T(8,128)(2,1)S(1)}, bf16[192,256]{1,0:T(8,128)(2,1)S(1)}, u32[]{:S(2)}, u32[]{:S(2)}) %collective-permute-start.4) | collective-permute-done | bytes 98336 | tf_op jit(solution)/shard_map/ppermute | solution.py:18
  61.4 3.4 %collective-permute-start.7 = (bf16[4,192,256]{2,1,0:T(8,128)(2,1)S(1)}, bf16[4,192,256]{2,1,0:T(8,128)(2,1)S(1)}, u32[]{:S(2)}, u32[]{:S(2)}) collective-permute-start(bf16[4,192,256]{2,1,0:T(8,128)(2,1)S(1)} %pad_maximum_fusion.refs_0_), channel_id=1, source_target_pairs={{0,224},{32,0},{64,32},{96,64},{128,96},{160,128},{192,160},{224,1... | collective-permute-start | bytes 1179656 | tf_op jit(solution)/shard_map/ppermute | solution.py:18
  64.8 3.2 %collective-permute-start.9 = (bf16[192,256]{1,0:T(8,128)(2,1)S(1)}, bf16[192,256]{1,0:T(8,128)(2,1)S(1)}, u32[]{:S(2)}, u32[]{:S(2)}) collective-permute-start(bf16[192,256]{1,0:T(8,128)(2,1)S(1)} %collective-permute-done.5), channel_id=1, source_target_pairs={{0,224},{32,0},{64,32},{96,64},{128,96},{160,128},{192,160},{224,1... | collective-permute-start | bytes 294920 | tf_op jit(solution)/shard_map/ppermute | solution.py:18
  68.1 3.4 %copy-done = bf16[256,16384]{1,0:T(8,128)(2,1)S(1)} copy-done((bf16[256,16384]{1,0:T(8,128)(2,1)S(1)}, bf16[256,16384]{1,0:T(8,128)(2,1)}, u32[]{:S(2)}) %copy-start) | copy-done | bytes 8388632
  71.5 0.9 shard_map.47.refs_2_
  72.4 1.2 collective-permute-done.8
  73.6 0.1 collective-permute-start.10
  73.8 3.3 %collective-permute-start.15 = (bf16[192,256]{1,0:T(8,128)(2,1)S(1)}, bf16[192,256]{1,0:T(8,128)(2,1)S(1)}, u32[]{:S(2)}, u32[]{:S(2)}) collective-permute-start(bf16[192,256]{1,0:T(8,128)(2,1)S(1)} %collective-permute-done.9), channel_id=1, source_target_pairs={{0,224},{32,0},{64,32},{96,64},{128,96},{160,128},{192,160},{224,1... | collective-permute-start | bytes 294920 | tf_op jit(solution)/shard_map/ppermute | solution.py:18
  77.1 1.9 %collective-permute-start.12 = (bf16[4,192,256]{2,1,0:T(8,128)(2,1)S(1)}, bf16[4,192,256]{2,1,0:T(8,128)(2,1)S(1)}, u32[]{:S(2)}, u32[]{:S(2)}) collective-permute-start(bf16[4,192,256]{2,1,0:T(8,128)(2,1)S(1)} %collective-permute-done.7.refs_1_), channel_id=1, source_target_pairs={{0,224},{32,0},{64,32},{96,64},{128,96},{160,128},{192,160},{224,1... | collective-permute-start | bytes 1179656 | tf_op jit(solution)/shard_map/ppermute | solution.py:18
  79.0 1.1 shard_map.48.refs_4_
  80.1 4.7 %collective-permute-done.14 = bf16[192,256]{1,0:T(8,128)(2,1)S(1)} collective-permute-done((bf16[192,256]{1,0:T(8,128)(2,1)S(1)}, bf16[192,256]{1,0:T(8,128)(2,1)S(1)}, u32[]{:S(2)}, u32[]{:S(2)}) %collective-permute-start.14) | collective-permute-done | bytes 98336 | tf_op jit(solution)/shard_map/ppermute | solution.py:18
  84.8 0.9 collective-permute-start.19
  85.7 6.0 %collective-permute-done.16 = bf16[192,256]{1,0:T(8,128)(2,1)S(1)} collective-permute-done((bf16[192,256]{1,0:T(8,128)(2,1)S(1)}, bf16[192,256]{1,0:T(8,128)(2,1)S(1)}, u32[]{:S(2)}, u32[]{:S(2)}) %collective-permute-start.16) | collective-permute-done | bytes 98336 | tf_op jit(solution)/shard_map/ppermute | solution.py:18
  91.8 1.4 collective-permute-start.21
  93.2 3.2 %collective-permute-start.13 = (bf16[4,192,256]{2,1,0:T(8,128)(2,1)S(1)}, bf16[4,192,256]{2,1,0:T(8,128)(2,1)S(1)}, u32[]{:S(2)}, u32[]{:S(2)}) collective-permute-start(bf16[4,192,256]{2,1,0:T(8,128)(2,1)S(1)} %collective-permute-done.12.refs_3_), channel_id=1, source_target_pairs={{0,224},{32,0},{64,32},{96,64},{128,96},{160,128},{192,160},{224,1... | collective-permute-start | bytes 1179656 | tf_op jit(solution)/shard_map/ppermute | solution.py:18
  96.4 1.8 %collective-permute-start.24 = (bf16[4,192,256]{2,1,0:T(8,128)(2,1)S(1)}, bf16[4,192,256]{2,1,0:T(8,128)(2,1)S(1)}, u32[]{:S(2)}, u32[]{:S(2)}) collective-permute-start(bf16[4,192,256]{2,1,0:T(8,128)(2,1)S(1)} %pad_maximum_fusion.1.refs_0_), channel_id=1, source_target_pairs={{0,24},{8,0},{16,8},{24,16},{1,25},{9,1},{17,9},{25,17},{2,26},{10... | collective-permute-start | bytes 1179656 | tf_op jit(solution)/shard_map/ppermute | solution.py:18
  98.2 0.2 collective-permute-start.23
  98.5 5.2 %collective-permute-done.21.refs_5_ = bf16[4,192,256]{2,1,0:T(8,128)(2,1)S(1)} collective-permute-done((bf16[4,192,256]{2,1,0:T(8,128)(2,1)S(1)}, bf16[4,192,256]{2,1,0:T(8,128)(2,1)S(1)}, u32[]{:S(2)}, u32[]{:S(2)}) %collective-permute-start.21) | collective-permute-done | bytes 393248 | tf_op jit(solution)/shard_map/ppermute | solution.py:18
  103.7 0.9 collective-permute-start.20
  104.6 2.3 %collective-permute-start.22 = (bf16[4,192,256]{2,1,0:T(8,128)(2,1)S(1)}, bf16[4,192,256]{2,1,0:T(8,128)(2,1)S(1)}, u32[]{:S(2)}, u32[]{:S(2)}) collective-permute-start(bf16[4,192,256]{2,1,0:T(8,128)(2,1)S(1)} %collective-permute-done.21.refs_5_), channel_id=1, source_target_pairs={{0,24},{8,0},{16,8},{24,16},{1,25},{9,1},{17,9},{25,17},{2,26},{10... | collective-permute-start | bytes 1179656 | tf_op jit(solution)/shard_map/ppermute | solution.py:18
  106.9 1.4 shard_map.49.refs_6_
  108.5 3.3 %collective-permute-start.18 = (bf16[2,192,256]{2,1,0:T(8,128)(2,1)S(1)}, bf16[2,192,256]{2,1,0:T(8,128)(2,1)S(1)}, u32[]{:S(2)}, u32[]{:S(2)}) collective-permute-start(bf16[2,192,256]{2,1,0:T(8,128)(2,1)S(1)} %slice.47), channel_id=1, source_target_pairs={{0,224},{32,0},{64,32},{96,64},{128,96},{160,128},{192,160},{224,1... | collective-permute-start | bytes 589832 | tf_op jit(solution)/shard_map/ppermute | solution.py:18
  111.8 1.7 %shard_map.50.refs_4_ = f32[192,256]{1,0:T(8,128)S(1)} custom-call(s32[3]{0:T(128)S(1)} %pad_add_fusion.me_ref, bf16[256,16384]{1,0:T(8,128)(2,1)S(1)} %copy-done, bf16[4,192,256]{2,1,0:T(8,128)(2,1)S(1)} %collective-permute-done.11.refs_0_, bf16[4,192,256]{2,1,0:T(8,128)(2,1)S(1)} %collective-permute-done.13.refs_1_, ...), custom_call_target="tpu_custom_call" | custom-call | flops 603979776 | bytes 5505024 | tf_op jit(solution)/shard_map/pallas_call | solution.py:71
  113.5 1.8 %collective-permute-done.17.refs_0_ = bf16[2,192,256]{2,1,0:T(8,128)(2,1)S(1)} collective-permute-done((bf16[2,192,256]{2,1,0:T(8,128)(2,1)S(1)}, bf16[2,192,256]{2,1,0:T(8,128)(2,1)S(1)}, u32[]{:S(2)}, u32[]{:S(2)}) %collective-permute-start.17) | collective-permute-done | bytes 196640 | tf_op jit(solution)/shard_map/ppermute | solution.py:18
  115.3 1.2 shard_map.51
  116.6 0.1 collective-permute-start.25
  116.7 0.6 collective-permute-start.26
  117.3 1.2 collective-permute-start.27
  118.5 2.8 %collective-permute-done.26.c_ref = f32[48,256]{1,0:T(8,128)S(1)} collective-permute-done((f32[48,256]{1,0:T(8,128)S(1)}, f32[48,256]{1,0:T(8,128)S(1)}, u32[]{:S(2)}, u32[]{:S(2)}) %collective-permute-start.26) | collective-permute-done | bytes 49184 | tf_op jit(solution)/shard_map/ppermute | solution.py:192
  121.3 0.1 collective-permute-done.27.d_ref
  121.4 0.6 shard_map.52
  122.1 22.3 %all_to_all.10.x_ref = f32[64,8,128]{2,1,0:T(8,128)S(1)} all-to-all(f32[64,8,128]{2,1,0:T(8,128)S(1)} %shard_map.52), channel_id=1, replica_groups=mesh['z'=8,'y'=4,'xh'=2,'xl'=2,'c'=2] {'z','y','xh'}, dimensions={0} | all-to-all | bytes 524288 | tf_op jit(solution)/shard_map/all_to_all | solution.py:195
  144.3 0.8 shard_map.53
  (40 shorter events, 0.5 us)
Async XLA Ops:
  0.0 1.2 copy-start.1
  2.3 39.6 %all-to-all-start = ((bf16[32,32,512]{2,1,0:T(8,128)(2,1)}), bf16[32,32,512]{2,1,0:T(8,128)(2,1)S(1)}, u32[]{:S(2)}, u32[]{:S(2)}) async-start(bf16[32,32,512]{2,1,0:T(8,128)(2,1)} %shard_map.46), calls=%async_computation | async-start | bytes 2097152 | tf_op jit(solution)/shard_map/all_to_all | solution.py:153
  41.9 7.3 %collective-permute-start = (bf16[6,32,512]{2,1,0:T(8,128)(2,1)S(1)}, bf16[6,32,512]{2,1,0:T(8,128)(2,1)S(1)}, u32[]{:S(2)}, u32[]{:S(2)}) collective-permute-start(bf16[6,32,512]{2,1,0:T(8,128)(2,1)S(1)} %dynamic-slice_dynamic-update-slice_fusion), channel_id=1, source_target_pairs={{0,4},{4,0},{1,5},{5,1},{2,6},{6,2},{3,7},{7,3},{8,12},{12,8},{9,1... | collective-permute-start | bytes 589832 | tf_op jit(solution)/shard_map/ppermute | solution.py:18
  49.3 8.6 %collective-permute-start.1 = (bf16[192,256]{1,0:T(8,128)(2,1)S(1)}, bf16[192,256]{1,0:T(8,128)(2,1)S(1)}, u32[]{:S(2)}, u32[]{:S(2)}) collective-permute-start(bf16[192,256]{1,0:T(8,128)(2,1)S(1)} %bitcast.26), channel_id=1, source_target_pairs={{0,8},{8,16},{16,24},{24,0},{1,9},{9,17},{17,25},{25,1},{2,10},{10... | collective-permute-start | bytes 294920 | tf_op jit(solution)/shard_map/ppermute | solution.py:18
  51.2 6.8 %collective-permute-start.2 = (bf16[192,256]{1,0:T(8,128)(2,1)S(1)}, bf16[192,256]{1,0:T(8,128)(2,1)S(1)}, u32[]{:S(2)}, u32[]{:S(2)}) collective-permute-start(bf16[192,256]{1,0:T(8,128)(2,1)S(1)} %bitcast.27), channel_id=1, source_target_pairs={{0,24},{8,0},{16,8},{24,16},{1,25},{9,1},{17,9},{25,17},{2,26},{10... | collective-permute-start | bytes 294920 | tf_op jit(solution)/shard_map/ppermute | solution.py:18
  52.6 6.1 %collective-permute-start.3 = (bf16[192,256]{1,0:T(8,128)(2,1)S(1)}, bf16[192,256]{1,0:T(8,128)(2,1)S(1)}, u32[]{:S(2)}, u32[]{:S(2)}) collective-permute-start(bf16[192,256]{1,0:T(8,128)(2,1)S(1)} %bitcast.28), channel_id=1, source_target_pairs={{0,16},{8,24},{16,0},{24,8},{1,17},{9,25},{17,1},{25,9},{2,18},{10... | collective-permute-start | bytes 294920 | tf_op jit(solution)/shard_map/ppermute | solution.py:18
  54.7 6.7 %collective-permute-start.4 = (bf16[192,256]{1,0:T(8,128)(2,1)S(1)}, bf16[192,256]{1,0:T(8,128)(2,1)S(1)}, u32[]{:S(2)}, u32[]{:S(2)}) collective-permute-start(bf16[192,256]{1,0:T(8,128)(2,1)S(1)} %bitcast.23), channel_id=1, source_target_pairs={{0,32},{32,64},{64,96},{96,128},{128,160},{160,192},{192,224},{224... | collective-permute-start | bytes 294920 | tf_op jit(solution)/shard_map/ppermute | solution.py:18
  55.3 6.1 %collective-permute-start.5 = (bf16[192,256]{1,0:T(8,128)(2,1)S(1)}, bf16[192,256]{1,0:T(8,128)(2,1)S(1)}, u32[]{:S(2)}, u32[]{:S(2)}) collective-permute-start(bf16[192,256]{1,0:T(8,128)(2,1)S(1)} %bitcast.24), channel_id=1, source_target_pairs={{0,224},{32,0},{64,32},{96,64},{128,96},{160,128},{192,160},{224,1... | collective-permute-start | bytes 294920 | tf_op jit(solution)/shard_map/ppermute | solution.py:18
  61.4 12.2 %collective-permute-start.6 = (bf16[4,192,256]{2,1,0:T(8,128)(2,1)S(1)}, bf16[4,192,256]{2,1,0:T(8,128)(2,1)S(1)}, u32[]{:S(2)}, u32[]{:S(2)}) collective-permute-start(bf16[4,192,256]{2,1,0:T(8,128)(2,1)S(1)} %pad_maximum_fusion.refs_0_), channel_id=1, source_target_pairs={{0,32},{32,64},{64,96},{96,128},{128,160},{160,192},{192,224},{224... | collective-permute-start | bytes 1179656 | tf_op jit(solution)/shard_map/ppermute | solution.py:18
  61.4 12.2 %collective-permute-start.7 = (bf16[4,192,256]{2,1,0:T(8,128)(2,1)S(1)}, bf16[4,192,256]{2,1,0:T(8,128)(2,1)S(1)}, u32[]{:S(2)}, u32[]{:S(2)}) collective-permute-start(bf16[4,192,256]{2,1,0:T(8,128)(2,1)S(1)} %pad_maximum_fusion.refs_0_), channel_id=1, source_target_pairs={{0,224},{32,0},{64,32},{96,64},{128,96},{160,128},{192,160},{224,1... | collective-permute-start | bytes 1179656 | tf_op jit(solution)/shard_map/ppermute | solution.py:18
  64.8 8.8 %collective-permute-start.8 = (bf16[192,256]{1,0:T(8,128)(2,1)S(1)}, bf16[192,256]{1,0:T(8,128)(2,1)S(1)}, u32[]{:S(2)}, u32[]{:S(2)}) collective-permute-start(bf16[192,256]{1,0:T(8,128)(2,1)S(1)} %collective-permute-done.4), channel_id=1, source_target_pairs={{0,32},{32,64},{64,96},{96,128},{128,160},{160,192},{192,224},{224... | collective-permute-start | bytes 294920 | tf_op jit(solution)/shard_map/ppermute | solution.py:18
  64.8 8.8 %collective-permute-start.9 = (bf16[192,256]{1,0:T(8,128)(2,1)S(1)}, bf16[192,256]{1,0:T(8,128)(2,1)S(1)}, u32[]{:S(2)}, u32[]{:S(2)}) collective-permute-start(bf16[192,256]{1,0:T(8,128)(2,1)S(1)} %collective-permute-done.5), channel_id=1, source_target_pairs={{0,224},{32,0},{64,32},{96,64},{128,96},{160,128},{192,160},{224,1... | collective-permute-start | bytes 294920 | tf_op jit(solution)/shard_map/ppermute | solution.py:18
  68.1 3.4 %copy-start = (bf16[256,16384]{1,0:T(8,128)(2,1)S(1)}, bf16[256,16384]{1,0:T(8,128)(2,1)}, u32[]{:S(2)}) copy-start(bf16[256,16384]{1,0:T(8,128)(2,1)} %w_ref.9) | copy-start | bytes 25165828
  73.6 19.6 %collective-permute-start.10 = (bf16[4,192,256]{2,1,0:T(8,128)(2,1)S(1)}, bf16[4,192,256]{2,1,0:T(8,128)(2,1)S(1)}, u32[]{:S(2)}, u32[]{:S(2)}) collective-permute-start(bf16[4,192,256]{2,1,0:T(8,128)(2,1)S(1)} %collective-permute-done.6.refs_0_), channel_id=1, source_target_pairs={{0,32},{32,64},{64,96},{96,128},{128,160},{160,192},{192,224},{224... | collective-permute-start | bytes 1179656 | tf_op jit(solution)/shard_map/ppermute | solution.py:18
  73.7 11.1 %collective-permute-start.14 = (bf16[192,256]{1,0:T(8,128)(2,1)S(1)}, bf16[192,256]{1,0:T(8,128)(2,1)S(1)}, u32[]{:S(2)}, u32[]{:S(2)}) collective-permute-start(bf16[192,256]{1,0:T(8,128)(2,1)S(1)} %collective-permute-done.8), channel_id=1, source_target_pairs={{0,32},{32,64},{64,96},{96,128},{128,160},{160,192},{192,224},{224... | collective-permute-start | bytes 294920 | tf_op jit(solution)/shard_map/ppermute | solution.py:18
  73.8 11.0 %collective-permute-start.15 = (bf16[192,256]{1,0:T(8,128)(2,1)S(1)}, bf16[192,256]{1,0:T(8,128)(2,1)S(1)}, u32[]{:S(2)}, u32[]{:S(2)}) collective-permute-start(bf16[192,256]{1,0:T(8,128)(2,1)S(1)} %collective-permute-done.9), channel_id=1, source_target_pairs={{0,224},{32,0},{64,32},{96,64},{128,96},{160,128},{192,160},{224,1... | collective-permute-start | bytes 294920 | tf_op jit(solution)/shard_map/ppermute | solution.py:18
  77.1 16.1 %collective-permute-start.12 = (bf16[4,192,256]{2,1,0:T(8,128)(2,1)S(1)}, bf16[4,192,256]{2,1,0:T(8,128)(2,1)S(1)}, u32[]{:S(2)}, u32[]{:S(2)}) collective-permute-start(bf16[4,192,256]{2,1,0:T(8,128)(2,1)S(1)} %collective-permute-done.7.refs_1_), channel_id=1, source_target_pairs={{0,224},{32,0},{64,32},{96,64},{128,96},{160,128},{192,160},{224,1... | collective-permute-start | bytes 1179656 | tf_op jit(solution)/shard_map/ppermute | solution.py:18
  84.8 6.9 %collective-permute-start.16 = (bf16[192,256]{1,0:T(8,128)(2,1)S(1)}, bf16[192,256]{1,0:T(8,128)(2,1)S(1)}, u32[]{:S(2)}, u32[]{:S(2)}) collective-permute-start(bf16[192,256]{1,0:T(8,128)(2,1)S(1)} %collective-permute-done.14), channel_id=1, source_target_pairs={{0,32},{32,64},{64,96},{96,128},{128,160},{160,192},{192,224},{224... | collective-permute-start | bytes 294920 | tf_op jit(solution)/shard_map/ppermute | solution.py:18
  84.8 13.4 %collective-permute-start.19 = (bf16[4,192,256]{2,1,0:T(8,128)(2,1)S(1)}, bf16[4,192,256]{2,1,0:T(8,128)(2,1)S(1)}, u32[]{:S(2)}, u32[]{:S(2)}) collective-permute-start(bf16[4,192,256]{2,1,0:T(8,128)(2,1)S(1)} %pad_maximum_fusion.1.refs_0_), channel_id=1, source_target_pairs={{0,8},{8,16},{16,24},{24,0},{1,9},{9,17},{17,25},{25,1},{2,10},{10... | collective-permute-start | bytes 1179656 | tf_op jit(solution)/shard_map/ppermute | solution.py:18
  91.8 11.9 %collective-permute-start.21 = (bf16[4,192,256]{2,1,0:T(8,128)(2,1)S(1)}, bf16[4,192,256]{2,1,0:T(8,128)(2,1)S(1)}, u32[]{:S(2)}, u32[]{:S(2)}) collective-permute-start(bf16[4,192,256]{2,1,0:T(8,128)(2,1)S(1)} %pad_maximum_fusion.2.refs_1_), channel_id=1, source_target_pairs={{0,24},{8,0},{16,8},{24,16},{1,25},{9,1},{17,9},{25,17},{2,26},{10... | collective-permute-start | bytes 1179656 | tf_op jit(solution)/shard_map/ppermute | solution.py:18
  93.2 11.4 %collective-permute-start.11 = (bf16[4,192,256]{2,1,0:T(8,128)(2,1)S(1)}, bf16[4,192,256]{2,1,0:T(8,128)(2,1)S(1)}, u32[]{:S(2)}, u32[]{:S(2)}) collective-permute-start(bf16[4,192,256]{2,1,0:T(8,128)(2,1)S(1)} %collective-permute-done.10.refs_2_), channel_id=1, source_target_pairs={{0,32},{32,64},{64,96},{96,128},{128,160},{160,192},{192,224},{224... | collective-permute-start | bytes 1179656 | tf_op jit(solution)/shard_map/ppermute | solution.py:18
  93.2 15.1 %collective-permute-start.13 = (bf16[4,192,256]{2,1,0:T(8,128)(2,1)S(1)}, bf16[4,192,256]{2,1,0:T(8,128)(2,1)S(1)}, u32[]{:S(2)}, u32[]{:S(2)}) collective-permute-start(bf16[4,192,256]{2,1,0:T(8,128)(2,1)S(1)} %collective-permute-done.12.refs_3_), channel_id=1, source_target_pairs={{0,224},{32,0},{64,32},{96,64},{128,96},{160,128},{192,160},{224,1... | collective-permute-start | bytes 1179656 | tf_op jit(solution)/shard_map/ppermute | solution.py:18
  96.4 12.1 %collective-permute-start.24 = (bf16[4,192,256]{2,1,0:T(8,128)(2,1)S(1)}, bf16[4,192,256]{2,1,0:T(8,128)(2,1)S(1)}, u32[]{:S(2)}, u32[]{:S(2)}) collective-permute-start(bf16[4,192,256]{2,1,0:T(8,128)(2,1)S(1)} %pad_maximum_fusion.1.refs_0_), channel_id=1, source_target_pairs={{0,24},{8,0},{16,8},{24,16},{1,25},{9,1},{17,9},{25,17},{2,26},{10... | collective-permute-start | bytes 1179656 | tf_op jit(solution)/shard_map/ppermute | solution.py:18
  98.2 13.6 %collective-permute-start.23 = (bf16[4,192,256]{2,1,0:T(8,128)(2,1)S(1)}, bf16[4,192,256]{2,1,0:T(8,128)(2,1)S(1)}, u32[]{:S(2)}, u32[]{:S(2)}) collective-permute-start(bf16[4,192,256]{2,1,0:T(8,128)(2,1)S(1)} %pad_maximum_fusion.2.refs_1_), channel_id=1, source_target_pairs={{0,8},{8,16},{16,24},{24,0},{1,9},{9,17},{17,25},{25,1},{2,10},{10... | collective-permute-start | bytes 1179656 | tf_op jit(solution)/shard_map/ppermute | solution.py:18
  103.7 9.8 %collective-permute-start.20 = (bf16[4,192,256]{2,1,0:T(8,128)(2,1)S(1)}, bf16[4,192,256]{2,1,0:T(8,128)(2,1)S(1)}, u32[]{:S(2)}, u32[]{:S(2)}) collective-permute-start(bf16[4,192,256]{2,1,0:T(8,128)(2,1)S(1)} %collective-permute-done.19.refs_2_), channel_id=1, source_target_pairs={{0,8},{8,16},{16,24},{24,0},{1,9},{9,17},{17,25},{25,1},{2,10},{10... | collective-permute-start | bytes 1179656 | tf_op jit(solution)/shard_map/ppermute | solution.py:18
  104.6 8.9 %collective-permute-start.22 = (bf16[4,192,256]{2,1,0:T(8,128)(2,1)S(1)}, bf16[4,192,256]{2,1,0:T(8,128)(2,1)S(1)}, u32[]{:S(2)}, u32[]{:S(2)}) collective-permute-start(bf16[4,192,256]{2,1,0:T(8,128)(2,1)S(1)} %collective-permute-done.21.refs_5_), channel_id=1, source_target_pairs={{0,24},{8,0},{16,8},{24,16},{1,25},{9,1},{17,9},{25,17},{2,26},{10... | collective-permute-start | bytes 1179656 | tf_op jit(solution)/shard_map/ppermute | solution.py:18
  108.4 7.0 %collective-permute-start.17 = (bf16[2,192,256]{2,1,0:T(8,128)(2,1)S(1)}, bf16[2,192,256]{2,1,0:T(8,128)(2,1)S(1)}, u32[]{:S(2)}, u32[]{:S(2)}) collective-permute-start(bf16[2,192,256]{2,1,0:T(8,128)(2,1)S(1)} %slice.46), channel_id=1, source_target_pairs={{0,32},{32,64},{64,96},{96,128},{128,160},{160,192},{192,224},{224... | collective-permute-start | bytes 589832 | tf_op jit(solution)/shard_map/ppermute | solution.py:18
  108.5 12.9 %copy-start.2 = (bf16[1024,256]{1,0:T(8,128)(2,1)S(1)}, bf16[1024,256]{1,0:T(8,128)(2,1)}, u32[]{:S(2)}) copy-start(bf16[1024,256]{1,0:T(8,128)(2,1)} %cond_ref.1) | copy-start | bytes 1572868
  108.5 6.8 %collective-permute-start.18 = (bf16[2,192,256]{2,1,0:T(8,128)(2,1)S(1)}, bf16[2,192,256]{2,1,0:T(8,128)(2,1)S(1)}, u32[]{:S(2)}, u32[]{:S(2)}) collective-permute-start(bf16[2,192,256]{2,1,0:T(8,128)(2,1)S(1)} %slice.47), channel_id=1, source_target_pairs={{0,224},{32,0},{64,32},{96,64},{128,96},{160,128},{192,160},{224,1... | collective-permute-start | bytes 589832 | tf_op jit(solution)/shard_map/ppermute | solution.py:18
  116.6 2.0 %collective-permute-start.25 = (f32[48,256]{1,0:T(8,128)S(1)}, f32[48,256]{1,0:T(8,128)S(1)}, u32[]{:S(2)}, u32[]{:S(2)}) collective-permute-start(f32[48,256]{1,0:T(8,128)S(1)} %get-tuple-element.38), channel_id=1, source_target_pairs={{0,1},{1,0},{2,3},{3,2},{4,5},{5,4},{6,7},{7,6},{8,9},{9,8},{10,11... | collective-permute-start | bytes 147464 | tf_op jit(solution)/shard_map/ppermute | solution.py:192
  116.7 4.6 %collective-permute-start.26 = (f32[48,256]{1,0:T(8,128)S(1)}, f32[48,256]{1,0:T(8,128)S(1)}, u32[]{:S(2)}, u32[]{:S(2)}) collective-permute-start(f32[48,256]{1,0:T(8,128)S(1)} %get-tuple-element.39), channel_id=1, source_target_pairs={{0,2},{1,3},{2,0},{3,1},{4,6},{5,7},{6,4},{7,5},{8,10},{9,11},{10,... | collective-permute-start | bytes 147464 | tf_op jit(solution)/shard_map/ppermute | solution.py:192
  117.3 4.1 %collective-permute-start.27 = (f32[48,256]{1,0:T(8,128)S(1)}, f32[48,256]{1,0:T(8,128)S(1)}, u32[]{:S(2)}, u32[]{:S(2)}) collective-permute-start(f32[48,256]{1,0:T(8,128)S(1)} %get-tuple-element.40), channel_id=1, source_target_pairs={{0,3},{1,2},{2,1},{3,0},{4,7},{5,6},{6,5},{7,4},{8,11},{9,10},{10,... | collective-permute-start | bytes 147464 | tf_op jit(solution)/shard_map/ppermute | solution.py:192

commit v5 on v4

--- a/solution.py
+++ b/solution.py
@@ -167,9 +167,10 @@
     acc = pair_call(me, screened, [sa], [[(0, 0, d) for d in dys]])
     a1r, a1l, z2r, z2l, acc = lax.optimization_barrier((a1r, a1l, z2r, z2l, acc))
     z3r, z3l = shift(z2r, "z", NZ, 1), shift(z2l, "z", NZ, -1)
+    z4 = shift(z2l, "z", NZ, -2)
     acc = pair_call(me, screened, [a1r, a1l], [[(0, -1, d) for d in dys], [(0, 1, d) for d in dys]], acc)
-    z3r, z3l, acc = lax.optimization_barrier((z3r, z3l, acc))
-    zb = [b, z1r, z1l, z2r, z2l, z3r, z3l, shift(z3r, "z", NZ, 1)]
+    z3r, z3l, z4, acc = lax.optimization_barrier((z3r, z3l, z4, acc))
+    zb = [b, z1r, z1l, z2r, z2l, z3r, z3l, z4]
     sb0, sb1 = jnp.stack(zb[:4]), jnp.stack(zb[4:])
 
     def at_a(dz):
@@ -179,8 +180,9 @@
         return [(1, d, dy) for d in dzs[4 * h:4 * h + 4]]
 
     a2r, a2l = shift(a1r, "z", NZ, 1), shift(a1l, "z", NZ, -1)
-    br0, br1 = shift(sb0, "y", NY, 1), shift(sb1, "y", NY, 1)
-    bl0, bl1 = shift(sb0, "y", NY, -1), shift(sb1, "y", NY, -1)
+    br0, bl0 = shift(sb0, "y", NY, 1), shift(sb0, "y", NY, -1)
+    sb1, br0, bl0 = lax.optimization_barrier((sb1, br0, bl0))
+    br1, bl1 = shift(sb1, "y", NY, 1), shift(sb1, "y", NY, -1)
     a3r, a3l = shift(a2r, "z", NZ, 1), shift(a2l, "z", NZ, -1)
     acc = pair_call(me, screened, [sb0, sb1, a2r, a2l], [at_b(0, 0), at_b(0, 1), at_a(-2), at_a(2)], acc)
     a3r, a3l, acc = lax.optimization_barrier((a3r, a3l, acc))

time: 146 us -> 142 us (0.973)
  waiting for transfers between devices: 40.9 us -> 33.4 us
  starting transfers between devices: 50.5 us -> 53.4 us
    ppermute x25, waiting for transfers between devices: 26.7 us -> 19.2 us  [shift(): return lax.ppermute(x, axis, [(i, (i + d) % n) for i in range(n)])]
    ppermute x25, starting transfers between devices: 37.1 us -> 40 us  [shift(): return lax.ppermute(x, axis, [(i, (i + d) % n) for i in range(n)])]
  transfers between devices with their start and end apart: 29 -> 29, of which waited for: 11 -> 10; matrix products, arithmetic and copies ran while one was open for 2% -> 2% of each run, Pallas kernels for 3% -> 4%
where the time goes in v5:
time: 142 us; the launch traced here: 141 us
  starting transfers between devices  53.4 us (38%)
  waiting for transfers between devices  33.4 us (24%)
  blocking collectives  23.2 us (16%)
  between operations  15.4 us (11%)
  Pallas kernels  8.77 us (6%)
  local copies, waits for them, and re-layouts  6.24 us (4%)
    ppermute x25, starting transfers between devices, shift(): return lax.ppermute(x, axis, [(i, (i + d) % n) for i in range(n)])  40 us
    all_to_all x1, blocking collectives, body(): recv = lax.all_to_all(term, ('z', 'y', 'xh'), 0, 0, tiled=True)  23.2 us
    ppermute x25, waiting for transfers between devices, shift(): return lax.ppermute(x, axis, [(i, (i + d) % n) for i in range(n)])  19.2 us
    all_to_all x1, starting transfers between devices, body(): recv = lax.all_to_all(pack(valence), ('z', 'y'), 0, 0, tiled=True)  11.5 us
    all_to_all x1, waiting for transfers between devices, body(): recv = lax.all_to_all(pack(valence), ('z', 'y'), 0, 0, tiled=True)  11.3 us
    pallas_call x5, Pallas kernels, pair_call(): pl.pallas_call(functools.partial(pair_kernel, places, acc is None, last),...  6.26 us
    unnamed x11, local copies, waits for them, and re-layouts  4.65 us
    ppermute x3, waiting for transfers between devices, body(): lax.ppermute(parts[k], ('xl', 'c'), [(i, i ^ k) for i in range(NGP)])  2.87 us
  transfers between devices with their start and end apart: 29, of which 10 were waited for; matrix products, arithmetic and copies ran while one was open for 2% of the time, Pallas kernels for 4%

profile of v5, /device:TPU:2, one launch (start us, length us, event | category | flops | bytes accessed | tf_op | source)
XLA Modules:
  0.0 141.5 jit_solution(16111637868405130038)
XLA Ops:
  0.0 1.2 copy-done.1
  1.2 1.1 shard_map.46
  2.3 11.5 %all-to-all-start = ((bf16[32,32,512]{2,1,0:T(8,128)(2,1)}), bf16[32,32,512]{2,1,0:T(8,128)(2,1)S(1)}, u32[]{:S(2)}, u32[]{:S(2)}) async-start(bf16[32,32,512]{2,1,0:T(8,128)(2,1)} %shard_map.46), calls=%async_computation | async-start | bytes 2097152 | tf_op jit(solution)/shard_map/all_to_all | solution.py:153
  13.8 1.6 %fusion.2 = (s32[1]{0:T(128)}, s32[1]{0:T(128)}, s32[1]{0:T(128)}, s32[1]{0:T(128)}, s32[1]{0:T(128)}, /*index=5*/s32[1]{0:T(128)}) fusion(s32[6]{0:T(128)} %param.7), kind=kLoop, calls=%fused_computation.17 | loop fusion | bytes 48 | tf_op jit(solution)/shard_map/slice | solution.py:154
  30.5 11.3 %all-to-all-done = bf16[32,32,512]{2,1,0:T(8,128)(2,1)S(1)} async-done(((bf16[32,32,512]{2,1,0:T(8,128)(2,1)}), bf16[32,32,512]{2,1,0:T(8,128)(2,1)S(1)}, u32[]{:S(2)}, u32[]{:S(2)}) %all-to-all-start) | async-done | bytes 1048608 | tf_op jit(solution)/shard_map/all_to_all | solution.py:153
  41.9 2.2 %collective-permute-start = (bf16[6,32,512]{2,1,0:T(8,128)(2,1)S(1)}, bf16[6,32,512]{2,1,0:T(8,128)(2,1)S(1)}, u32[]{:S(2)}, u32[]{:S(2)}) collective-permute-start(bf16[6,32,512]{2,1,0:T(8,128)(2,1)S(1)} %dynamic-slice_dynamic-update-slice_fusion), channel_id=1, source_target_pairs={{0,4},{4,0},{1,5},{5,1},{2,6},{6,2},{3,7},{7,3},{8,12},{12,8},{9,1... | collective-permute-start | bytes 589832 | tf_op jit(solution)/shard_map/ppermute | solution.py:18
  44.2 0.7 fusion
  44.8 4.4 %collective-permute-done = bf16[6,32,512]{2,1,0:T(8,128)(2,1)S(1)} collective-permute-done((bf16[6,32,512]{2,1,0:T(8,128)(2,1)S(1)}, bf16[6,32,512]{2,1,0:T(8,128)(2,1)S(1)}, u32[]{:S(2)}, u32[]{:S(2)}) %collective-permute-start) | collective-permute-done | bytes 196640 | tf_op jit(solution)/shard_map/ppermute | solution.py:18
  49.2 0.1 slice_select_fusion
  49.3 1.8 %collective-permute-start.1 = (bf16[192,256]{1,0:T(8,128)(2,1)S(1)}, bf16[192,256]{1,0:T(8,128)(2,1)S(1)}, u32[]{:S(2)}, u32[]{:S(2)}) collective-permute-start(bf16[192,256]{1,0:T(8,128)(2,1)S(1)} %bitcast.26), channel_id=1, source_target_pairs={{0,8},{8,16},{16,24},{24,0},{1,9},{9,17},{17,25},{25,1},{2,10},{10... | collective-permute-start | bytes 294920 | tf_op jit(solution)/shard_map/ppermute | solution.py:18
  51.2 1.5 %collective-permute-start.2 = (bf16[192,256]{1,0:T(8,128)(2,1)S(1)}, bf16[192,256]{1,0:T(8,128)(2,1)S(1)}, u32[]{:S(2)}, u32[]{:S(2)}) collective-permute-start(bf16[192,256]{1,0:T(8,128)(2,1)S(1)} %bitcast.27), channel_id=1, source_target_pairs={{0,24},{8,0},{16,8},{24,16},{1,25},{9,1},{17,9},{25,17},{2,26},{10... | collective-permute-start | bytes 294920 | tf_op jit(solution)/shard_map/ppermute | solution.py:18
  52.6 2.1 %collective-permute-start.3 = (bf16[192,256]{1,0:T(8,128)(2,1)S(1)}, bf16[192,256]{1,0:T(8,128)(2,1)S(1)}, u32[]{:S(2)}, u32[]{:S(2)}) collective-permute-start(bf16[192,256]{1,0:T(8,128)(2,1)S(1)} %bitcast.28), channel_id=1, source_target_pairs={{0,16},{8,24},{16,0},{24,8},{1,17},{9,25},{17,1},{25,9},{2,18},{10... | collective-permute-start | bytes 294920 | tf_op jit(solution)/shard_map/ppermute | solution.py:18
  54.7 0.6 collective-permute-start.4
  55.3 2.6 %collective-permute-start.5 = (bf16[192,256]{1,0:T(8,128)(2,1)S(1)}, bf16[192,256]{1,0:T(8,128)(2,1)S(1)}, u32[]{:S(2)}, u32[]{:S(2)}) collective-permute-start(bf16[192,256]{1,0:T(8,128)(2,1)S(1)} %bitcast.24), channel_id=1, source_target_pairs={{0,224},{32,0},{64,32},{96,64},{128,96},{160,128},{192,160},{224,1... | collective-permute-start | bytes 294920 | tf_op jit(solution)/shard_map/ppermute | solution.py:18
  57.9 0.8 collective-permute-done.3
  58.8 2.6 %collective-permute-done.4 = bf16[192,256]{1,0:T(8,128)(2,1)S(1)} collective-permute-done((bf16[192,256]{1,0:T(8,128)(2,1)S(1)}, bf16[192,256]{1,0:T(8,128)(2,1)S(1)}, u32[]{:S(2)}, u32[]{:S(2)}) %collective-permute-start.4) | collective-permute-done | bytes 98336 | tf_op jit(solution)/shard_map/ppermute | solution.py:18
  61.4 3.4 %collective-permute-start.7 = (bf16[4,192,256]{2,1,0:T(8,128)(2,1)S(1)}, bf16[4,192,256]{2,1,0:T(8,128)(2,1)S(1)}, u32[]{:S(2)}, u32[]{:S(2)}) collective-permute-start(bf16[4,192,256]{2,1,0:T(8,128)(2,1)S(1)} %pad_maximum_fusion.refs_0_), channel_id=1, source_target_pairs={{0,224},{32,0},{64,32},{96,64},{128,96},{160,128},{192,160},{224,1... | collective-permute-start | bytes 1179656 | tf_op jit(solution)/shard_map/ppermute | solution.py:18
  64.8 3.2 %collective-permute-start.9 = (bf16[192,256]{1,0:T(8,128)(2,1)S(1)}, bf16[192,256]{1,0:T(8,128)(2,1)S(1)}, u32[]{:S(2)}, u32[]{:S(2)}) collective-permute-start(bf16[192,256]{1,0:T(8,128)(2,1)S(1)} %collective-permute-done.5), channel_id=1, source_target_pairs={{0,224},{32,0},{64,32},{96,64},{128,96},{160,128},{192,160},{224,1... | collective-permute-start | bytes 294920 | tf_op jit(solution)/shard_map/ppermute | solution.py:18
  68.0 0.1 pad_add_fusion.me_ref
  68.1 3.4 %copy-done = bf16[256,16384]{1,0:T(8,128)(2,1)S(1)} copy-done((bf16[256,16384]{1,0:T(8,128)(2,1)S(1)}, bf16[256,16384]{1,0:T(8,128)(2,1)}, u32[]{:S(2)}) %copy-start) | copy-done | bytes 8388632
  71.5 0.9 shard_map.47.refs_2_
  72.5 0.6 collective-permute-start.17
  73.1 2.7 %collective-permute-start.18 = (bf16[4,192,256]{2,1,0:T(8,128)(2,1)S(1)}, bf16[4,192,256]{2,1,0:T(8,128)(2,1)S(1)}, u32[]{:S(2)}, u32[]{:S(2)}) collective-permute-start(bf16[4,192,256]{2,1,0:T(8,128)(2,1)S(1)} %pad_maximum_fusion.1.refs_0_), channel_id=1, source_target_pairs={{0,24},{8,0},{16,8},{24,16},{1,25},{9,1},{17,9},{25,17},{2,26},{10... | collective-permute-start | bytes 1179656 | tf_op jit(solution)/shard_map/ppermute | solution.py:18
  75.8 3.2 %collective-permute-start.15 = (bf16[192,256]{1,0:T(8,128)(2,1)S(1)}, bf16[192,256]{1,0:T(8,128)(2,1)S(1)}, u32[]{:S(2)}, u32[]{:S(2)}) collective-permute-start(bf16[192,256]{1,0:T(8,128)(2,1)S(1)} %collective-permute-done.9), channel_id=1, source_target_pairs={{0,224},{32,0},{64,32},{96,64},{128,96},{160,128},{192,160},{224,1... | collective-permute-start | bytes 294920 | tf_op jit(solution)/shard_map/ppermute | solution.py:18
  79.1 1.5 %collective-permute-start.16 = (bf16[192,256]{1,0:T(8,128)(2,1)S(1)}, bf16[192,256]{1,0:T(8,128)(2,1)S(1)}, u32[]{:S(2)}, u32[]{:S(2)}) collective-permute-start(bf16[192,256]{1,0:T(8,128)(2,1)S(1)} %collective-permute-done.9), channel_id=1, source_target_pairs={{0,192},{32,224},{64,0},{96,32},{128,64},{160,96},{192,128},{224,1... | collective-permute-start | bytes 294920 | tf_op jit(solution)/shard_map/ppermute | solution.py:18
  80.5 1.8 %collective-permute-done.14 = bf16[192,256]{1,0:T(8,128)(2,1)S(1)} collective-permute-done((bf16[192,256]{1,0:T(8,128)(2,1)S(1)}, bf16[192,256]{1,0:T(8,128)(2,1)S(1)}, u32[]{:S(2)}, u32[]{:S(2)}) %collective-permute-start.14) | collective-permute-done | bytes 98336 | tf_op jit(solution)/shard_map/ppermute | solution.py:18
  82.3 3.2 %collective-permute-start.12 = (bf16[4,192,256]{2,1,0:T(8,128)(2,1)S(1)}, bf16[4,192,256]{2,1,0:T(8,128)(2,1)S(1)}, u32[]{:S(2)}, u32[]{:S(2)}) collective-permute-start(bf16[4,192,256]{2,1,0:T(8,128)(2,1)S(1)} %collective-permute-done.7.refs_1_), channel_id=1, source_target_pairs={{0,224},{32,0},{64,32},{96,64},{128,96},{160,128},{192,160},{224,1... | collective-permute-start | bytes 1179656 | tf_op jit(solution)/shard_map/ppermute | solution.py:18
  85.6 1.1 shard_map.48.refs_4_
  86.7 1.2 collective-permute-start.22
  87.9 6.3 %collective-permute-done.10.refs_2_ = bf16[4,192,256]{2,1,0:T(8,128)(2,1)S(1)} collective-permute-done((bf16[4,192,256]{2,1,0:T(8,128)(2,1)S(1)}, bf16[4,192,256]{2,1,0:T(8,128)(2,1)S(1)}, u32[]{:S(2)}, u32[]{:S(2)}) %collective-permute-start.10) | collective-permute-done | bytes 393248 | tf_op jit(solution)/shard_map/ppermute | solution.py:18
  94.3 3.2 %collective-permute-start.13 = (bf16[4,192,256]{2,1,0:T(8,128)(2,1)S(1)}, bf16[4,192,256]{2,1,0:T(8,128)(2,1)S(1)}, u32[]{:S(2)}, u32[]{:S(2)}) collective-permute-start(bf16[4,192,256]{2,1,0:T(8,128)(2,1)S(1)} %collective-permute-done.12.refs_3_), channel_id=1, source_target_pairs={{0,224},{32,0},{64,32},{96,64},{128,96},{160,128},{192,160},{224,1... | collective-permute-start | bytes 1179656 | tf_op jit(solution)/shard_map/ppermute | solution.py:18
  97.5 0.2 collective-permute-start.24
  97.8 3.2 %collective-permute-start.23 = (bf16[4,192,256]{2,1,0:T(8,128)(2,1)S(1)}, bf16[4,192,256]{2,1,0:T(8,128)(2,1)S(1)}, u32[]{:S(2)}, u32[]{:S(2)}) collective-permute-start(bf16[4,192,256]{2,1,0:T(8,128)(2,1)S(1)} %collective-permute-done.22.refs_5_), channel_id=1, source_target_pairs={{0,24},{8,0},{16,8},{24,16},{1,25},{9,1},{17,9},{25,17},{2,26},{10... | collective-permute-start | bytes 1179656 | tf_op jit(solution)/shard_map/ppermute | solution.py:18
  101.0 1.4 shard_map.49.refs_6_
  102.4 1.2 collective-permute-done.11.refs_0_
  103.6 0.1 collective-permute-start.19
  103.7 3.3 %collective-permute-start.20 = (bf16[2,192,256]{2,1,0:T(8,128)(2,1)S(1)}, bf16[2,192,256]{2,1,0:T(8,128)(2,1)S(1)}, u32[]{:S(2)}, u32[]{:S(2)}) collective-permute-start(bf16[2,192,256]{2,1,0:T(8,128)(2,1)S(1)} %slice.47), channel_id=1, source_target_pairs={{0,224},{32,0},{64,32},{96,64},{128,96},{160,128},{192,160},{224,1... | collective-permute-start | bytes 589832 | tf_op jit(solution)/shard_map/ppermute | solution.py:18
  107.0 1.7 %shard_map.50.refs_4_ = f32[192,256]{1,0:T(8,128)S(1)} custom-call(s32[3]{0:T(128)S(1)} %pad_add_fusion.me_ref, bf16[256,16384]{1,0:T(8,128)(2,1)S(1)} %copy-done, bf16[4,192,256]{2,1,0:T(8,128)(2,1)S(1)} %collective-permute-done.11.refs_0_, bf16[4,192,256]{2,1,0:T(8,128)(2,1)S(1)} %collective-permute-done.13.refs_1_, ...), custom_call_target="tpu_custom_call" | custom-call | flops 603979776 | bytes 5505024 | tf_op jit(solution)/shard_map/pallas_call | solution.py:71
  108.7 2.0 %collective-permute-done.21.refs_2_ = bf16[4,192,256]{2,1,0:T(8,128)(2,1)S(1)} collective-permute-done((bf16[4,192,256]{2,1,0:T(8,128)(2,1)S(1)}, bf16[4,192,256]{2,1,0:T(8,128)(2,1)S(1)}, u32[]{:S(2)}, u32[]{:S(2)}) %collective-permute-start.21) | collective-permute-done | bytes 393248 | tf_op jit(solution)/shard_map/ppermute | solution.py:18
  110.7 1.2 shard_map.51
  112.0 0.1 collective-permute-start.25
  112.1 0.6 collective-permute-start.26
  112.7 1.2 collective-permute-start.27
  113.9 2.8 %collective-permute-done.26.c_ref = f32[48,256]{1,0:T(8,128)S(1)} collective-permute-done((f32[48,256]{1,0:T(8,128)S(1)}, f32[48,256]{1,0:T(8,128)S(1)}, u32[]{:S(2)}, u32[]{:S(2)}) %collective-permute-start.26) | collective-permute-done | bytes 49184 | tf_op jit(solution)/shard_map/ppermute | solution.py:194
  116.7 0.1 collective-permute-done.27.d_ref
  116.8 0.6 shard_map.52
  117.4 23.2 %all_to_all.10.x_ref = f32[64,8,128]{2,1,0:T(8,128)S(1)} all-to-all(f32[64,8,128]{2,1,0:T(8,128)S(1)} %shard_map.52), channel_id=1, replica_groups=mesh['z'=8,'y'=4,'xh'=2,'xl'=2,'c'=2] {'z','y','xh'}, dimensions={0} | all-to-all | bytes 524288 | tf_op jit(solution)/shard_map/all_to_all | solution.py:197
  140.6 0.8 shard_map.53
  (40 shorter events, 0.3 us)
Async XLA Ops:
  0.0 1.2 copy-start.1
  2.3 39.6 %all-to-all-start = ((bf16[32,32,512]{2,1,0:T(8,128)(2,1)}), bf16[32,32,512]{2,1,0:T(8,128)(2,1)S(1)}, u32[]{:S(2)}, u32[]{:S(2)}) async-start(bf16[32,32,512]{2,1,0:T(8,128)(2,1)} %shard_map.46), calls=%async_computation | async-start | bytes 2097152 | tf_op jit(solution)/shard_map/all_to_all | solution.py:153
  41.9 7.3 %collective-permute-start = (bf16[6,32,512]{2,1,0:T(8,128)(2,1)S(1)}, bf16[6,32,512]{2,1,0:T(8,128)(2,1)S(1)}, u32[]{:S(2)}, u32[]{:S(2)}) collective-permute-start(bf16[6,32,512]{2,1,0:T(8,128)(2,1)S(1)} %dynamic-slice_dynamic-update-slice_fusion), channel_id=1, source_target_pairs={{0,4},{4,0},{1,5},{5,1},{2,6},{6,2},{3,7},{7,3},{8,12},{12,8},{9,1... | collective-permute-start | bytes 589832 | tf_op jit(solution)/shard_map/ppermute | solution.py:18
  49.3 8.6 %collective-permute-start.1 = (bf16[192,256]{1,0:T(8,128)(2,1)S(1)}, bf16[192,256]{1,0:T(8,128)(2,1)S(1)}, u32[]{:S(2)}, u32[]{:S(2)}) collective-permute-start(bf16[192,256]{1,0:T(8,128)(2,1)S(1)} %bitcast.26), channel_id=1, source_target_pairs={{0,8},{8,16},{16,24},{24,0},{1,9},{9,17},{17,25},{25,1},{2,10},{10... | collective-permute-start | bytes 294920 | tf_op jit(solution)/shard_map/ppermute | solution.py:18
  51.2 6.8 %collective-permute-start.2 = (bf16[192,256]{1,0:T(8,128)(2,1)S(1)}, bf16[192,256]{1,0:T(8,128)(2,1)S(1)}, u32[]{:S(2)}, u32[]{:S(2)}) collective-permute-start(bf16[192,256]{1,0:T(8,128)(2,1)S(1)} %bitcast.27), channel_id=1, source_target_pairs={{0,24},{8,0},{16,8},{24,16},{1,25},{9,1},{17,9},{25,17},{2,26},{10... | collective-permute-start | bytes 294920 | tf_op jit(solution)/shard_map/ppermute | solution.py:18
  52.6 6.1 %collective-permute-start.3 = (bf16[192,256]{1,0:T(8,128)(2,1)S(1)}, bf16[192,256]{1,0:T(8,128)(2,1)S(1)}, u32[]{:S(2)}, u32[]{:S(2)}) collective-permute-start(bf16[192,256]{1,0:T(8,128)(2,1)S(1)} %bitcast.28), channel_id=1, source_target_pairs={{0,16},{8,24},{16,0},{24,8},{1,17},{9,25},{17,1},{25,9},{2,18},{10... | collective-permute-start | bytes 294920 | tf_op jit(solution)/shard_map/ppermute | solution.py:18
  54.7 6.7 %collective-permute-start.4 = (bf16[192,256]{1,0:T(8,128)(2,1)S(1)}, bf16[192,256]{1,0:T(8,128)(2,1)S(1)}, u32[]{:S(2)}, u32[]{:S(2)}) collective-permute-start(bf16[192,256]{1,0:T(8,128)(2,1)S(1)} %bitcast.23), channel_id=1, source_target_pairs={{0,32},{32,64},{64,96},{96,128},{128,160},{160,192},{192,224},{224... | collective-permute-start | bytes 294920 | tf_op jit(solution)/shard_map/ppermute | solution.py:18
  55.3 6.1 %collective-permute-start.5 = (bf16[192,256]{1,0:T(8,128)(2,1)S(1)}, bf16[192,256]{1,0:T(8,128)(2,1)S(1)}, u32[]{:S(2)}, u32[]{:S(2)}) collective-permute-start(bf16[192,256]{1,0:T(8,128)(2,1)S(1)} %bitcast.24), channel_id=1, source_target_pairs={{0,224},{32,0},{64,32},{96,64},{128,96},{160,128},{192,160},{224,1... | collective-permute-start | bytes 294920 | tf_op jit(solution)/shard_map/ppermute | solution.py:18
  61.4 11.0 %collective-permute-start.6 = (bf16[4,192,256]{2,1,0:T(8,128)(2,1)S(1)}, bf16[4,192,256]{2,1,0:T(8,128)(2,1)S(1)}, u32[]{:S(2)}, u32[]{:S(2)}) collective-permute-start(bf16[4,192,256]{2,1,0:T(8,128)(2,1)S(1)} %pad_maximum_fusion.refs_0_), channel_id=1, source_target_pairs={{0,32},{32,64},{64,96},{96,128},{128,160},{160,192},{192,224},{224... | collective-permute-start | bytes 1179656 | tf_op jit(solution)/shard_map/ppermute | solution.py:18
  61.4 11.0 %collective-permute-start.7 = (bf16[4,192,256]{2,1,0:T(8,128)(2,1)S(1)}, bf16[4,192,256]{2,1,0:T(8,128)(2,1)S(1)}, u32[]{:S(2)}, u32[]{:S(2)}) collective-permute-start(bf16[4,192,256]{2,1,0:T(8,128)(2,1)S(1)} %pad_maximum_fusion.refs_0_), channel_id=1, source_target_pairs={{0,224},{32,0},{64,32},{96,64},{128,96},{160,128},{192,160},{224,1... | collective-permute-start | bytes 1179656 | tf_op jit(solution)/shard_map/ppermute | solution.py:18
  64.8 7.6 %collective-permute-start.8 = (bf16[192,256]{1,0:T(8,128)(2,1)S(1)}, bf16[192,256]{1,0:T(8,128)(2,1)S(1)}, u32[]{:S(2)}, u32[]{:S(2)}) collective-permute-start(bf16[192,256]{1,0:T(8,128)(2,1)S(1)} %collective-permute-done.4), channel_id=1, source_target_pairs={{0,32},{32,64},{64,96},{96,128},{128,160},{160,192},{192,224},{224... | collective-permute-start | bytes 294920 | tf_op jit(solution)/shard_map/ppermute | solution.py:18
  64.8 7.6 %collective-permute-start.9 = (bf16[192,256]{1,0:T(8,128)(2,1)S(1)}, bf16[192,256]{1,0:T(8,128)(2,1)S(1)}, u32[]{:S(2)}, u32[]{:S(2)}) collective-permute-start(bf16[192,256]{1,0:T(8,128)(2,1)S(1)} %collective-permute-done.5), channel_id=1, source_target_pairs={{0,224},{32,0},{64,32},{96,64},{128,96},{160,128},{192,160},{224,1... | collective-permute-start | bytes 294920 | tf_op jit(solution)/shard_map/ppermute | solution.py:18
  68.1 3.4 %copy-start = (bf16[256,16384]{1,0:T(8,128)(2,1)S(1)}, bf16[256,16384]{1,0:T(8,128)(2,1)}, u32[]{:S(2)}) copy-start(bf16[256,16384]{1,0:T(8,128)(2,1)} %w_ref.9) | copy-start | bytes 25165828
  72.5 14.2 %collective-permute-start.17 = (bf16[4,192,256]{2,1,0:T(8,128)(2,1)S(1)}, bf16[4,192,256]{2,1,0:T(8,128)(2,1)S(1)}, u32[]{:S(2)}, u32[]{:S(2)}) collective-permute-start(bf16[4,192,256]{2,1,0:T(8,128)(2,1)S(1)} %pad_maximum_fusion.1.refs_0_), channel_id=1, source_target_pairs={{0,8},{8,16},{16,24},{24,0},{1,9},{9,17},{17,25},{25,1},{2,10},{10... | collective-permute-start | bytes 1179656 | tf_op jit(solution)/shard_map/ppermute | solution.py:18
  73.1 13.6 %collective-permute-start.18 = (bf16[4,192,256]{2,1,0:T(8,128)(2,1)S(1)}, bf16[4,192,256]{2,1,0:T(8,128)(2,1)S(1)}, u32[]{:S(2)}, u32[]{:S(2)}) collective-permute-start(bf16[4,192,256]{2,1,0:T(8,128)(2,1)S(1)} %pad_maximum_fusion.1.refs_0_), channel_id=1, source_target_pairs={{0,24},{8,0},{16,8},{24,16},{1,25},{9,1},{17,9},{25,17},{2,26},{10... | collective-permute-start | bytes 1179656 | tf_op jit(solution)/shard_map/ppermute | solution.py:18
  75.8 6.5 %collective-permute-start.14 = (bf16[192,256]{1,0:T(8,128)(2,1)S(1)}, bf16[192,256]{1,0:T(8,128)(2,1)S(1)}, u32[]{:S(2)}, u32[]{:S(2)}) collective-permute-start(bf16[192,256]{1,0:T(8,128)(2,1)S(1)} %collective-permute-done.8), channel_id=1, source_target_pairs={{0,32},{32,64},{64,96},{96,128},{128,160},{160,192},{192,224},{224... | collective-permute-start | bytes 294920 | tf_op jit(solution)/shard_map/ppermute | solution.py:18
  75.8 6.5 %collective-permute-start.15 = (bf16[192,256]{1,0:T(8,128)(2,1)S(1)}, bf16[192,256]{1,0:T(8,128)(2,1)S(1)}, u32[]{:S(2)}, u32[]{:S(2)}) collective-permute-start(bf16[192,256]{1,0:T(8,128)(2,1)S(1)} %collective-permute-done.9), channel_id=1, source_target_pairs={{0,224},{32,0},{64,32},{96,64},{128,96},{160,128},{192,160},{224,1... | collective-permute-start | bytes 294920 | tf_op jit(solution)/shard_map/ppermute | solution.py:18
  79.1 7.6 %collective-permute-start.16 = (bf16[192,256]{1,0:T(8,128)(2,1)S(1)}, bf16[192,256]{1,0:T(8,128)(2,1)S(1)}, u32[]{:S(2)}, u32[]{:S(2)}) collective-permute-start(bf16[192,256]{1,0:T(8,128)(2,1)S(1)} %collective-permute-done.9), channel_id=1, source_target_pairs={{0,192},{32,224},{64,0},{96,32},{128,64},{160,96},{192,128},{224,1... | collective-permute-start | bytes 294920 | tf_op jit(solution)/shard_map/ppermute | solution.py:18
  82.3 11.9 %collective-permute-start.10 = (bf16[4,192,256]{2,1,0:T(8,128)(2,1)S(1)}, bf16[4,192,256]{2,1,0:T(8,128)(2,1)S(1)}, u32[]{:S(2)}, u32[]{:S(2)}) collective-permute-start(bf16[4,192,256]{2,1,0:T(8,128)(2,1)S(1)} %collective-permute-done.6.refs_0_), channel_id=1, source_target_pairs={{0,32},{32,64},{64,96},{96,128},{128,160},{160,192},{192,224},{224... | collective-permute-start | bytes 1179656 | tf_op jit(solution)/shard_map/ppermute | solution.py:18
  82.3 11.9 %collective-permute-start.12 = (bf16[4,192,256]{2,1,0:T(8,128)(2,1)S(1)}, bf16[4,192,256]{2,1,0:T(8,128)(2,1)S(1)}, u32[]{:S(2)}, u32[]{:S(2)}) collective-permute-start(bf16[4,192,256]{2,1,0:T(8,128)(2,1)S(1)} %collective-permute-done.7.refs_1_), channel_id=1, source_target_pairs={{0,224},{32,0},{64,32},{96,64},{128,96},{160,128},{192,160},{224,1... | collective-permute-start | bytes 1179656 | tf_op jit(solution)/shard_map/ppermute | solution.py:18
  86.7 11.0 %collective-permute-start.22 = (bf16[4,192,256]{2,1,0:T(8,128)(2,1)S(1)}, bf16[4,192,256]{2,1,0:T(8,128)(2,1)S(1)}, u32[]{:S(2)}, u32[]{:S(2)}) collective-permute-start(bf16[4,192,256]{2,1,0:T(8,128)(2,1)S(1)} %pad_maximum_fusion.2.refs_1_), channel_id=1, source_target_pairs={{0,24},{8,0},{16,8},{24,16},{1,25},{9,1},{17,9},{25,17},{2,26},{10... | collective-permute-start | bytes 1179656 | tf_op jit(solution)/shard_map/ppermute | solution.py:18
  94.3 9.3 %collective-permute-start.11 = (bf16[4,192,256]{2,1,0:T(8,128)(2,1)S(1)}, bf16[4,192,256]{2,1,0:T(8,128)(2,1)S(1)}, u32[]{:S(2)}, u32[]{:S(2)}) collective-permute-start(bf16[4,192,256]{2,1,0:T(8,128)(2,1)S(1)} %collective-permute-done.10.refs_2_), channel_id=1, source_target_pairs={{0,32},{32,64},{64,96},{96,128},{128,160},{160,192},{192,224},{224... | collective-permute-start | bytes 1179656 | tf_op jit(solution)/shard_map/ppermute | solution.py:18
  94.3 9.3 %collective-permute-start.13 = (bf16[4,192,256]{2,1,0:T(8,128)(2,1)S(1)}, bf16[4,192,256]{2,1,0:T(8,128)(2,1)S(1)}, u32[]{:S(2)}, u32[]{:S(2)}) collective-permute-start(bf16[4,192,256]{2,1,0:T(8,128)(2,1)S(1)} %collective-permute-done.12.refs_3_), channel_id=1, source_target_pairs={{0,224},{32,0},{64,32},{96,64},{128,96},{160,128},{192,160},{224,1... | collective-permute-start | bytes 1179656 | tf_op jit(solution)/shard_map/ppermute | solution.py:18
  97.5 9.5 %collective-permute-start.24 = (bf16[4,192,256]{2,1,0:T(8,128)(2,1)S(1)}, bf16[4,192,256]{2,1,0:T(8,128)(2,1)S(1)}, u32[]{:S(2)}, u32[]{:S(2)}) collective-permute-start(bf16[4,192,256]{2,1,0:T(8,128)(2,1)S(1)} %pad_maximum_fusion.2.refs_1_), channel_id=1, source_target_pairs={{0,8},{8,16},{16,24},{24,0},{1,9},{9,17},{17,25},{25,1},{2,10},{10... | collective-permute-start | bytes 1179656 | tf_op jit(solution)/shard_map/ppermute | solution.py:18
  97.7 13.0 %collective-permute-start.21 = (bf16[4,192,256]{2,1,0:T(8,128)(2,1)S(1)}, bf16[4,192,256]{2,1,0:T(8,128)(2,1)S(1)}, u32[]{:S(2)}, u32[]{:S(2)}) collective-permute-start(bf16[4,192,256]{2,1,0:T(8,128)(2,1)S(1)} %collective-permute-done.17.refs_2_), channel_id=1, source_target_pairs={{0,8},{8,16},{16,24},{24,0},{1,9},{9,17},{17,25},{25,1},{2,10},{10... | collective-permute-start | bytes 1179656 | tf_op jit(solution)/shard_map/ppermute | solution.py:18
  97.8 13.0 %collective-permute-start.23 = (bf16[4,192,256]{2,1,0:T(8,128)(2,1)S(1)}, bf16[4,192,256]{2,1,0:T(8,128)(2,1)S(1)}, u32[]{:S(2)}, u32[]{:S(2)}) collective-permute-start(bf16[4,192,256]{2,1,0:T(8,128)(2,1)S(1)} %collective-permute-done.22.refs_5_), channel_id=1, source_target_pairs={{0,24},{8,0},{16,8},{24,16},{1,25},{9,1},{17,9},{25,17},{2,26},{10... | collective-permute-start | bytes 1179656 | tf_op jit(solution)/shard_map/ppermute | solution.py:18
  103.6 7.1 %collective-permute-start.19 = (bf16[2,192,256]{2,1,0:T(8,128)(2,1)S(1)}, bf16[2,192,256]{2,1,0:T(8,128)(2,1)S(1)}, u32[]{:S(2)}, u32[]{:S(2)}) collective-permute-start(bf16[2,192,256]{2,1,0:T(8,128)(2,1)S(1)} %slice.46), channel_id=1, source_target_pairs={{0,32},{32,64},{64,96},{96,128},{128,160},{160,192},{192,224},{224... | collective-permute-start | bytes 589832 | tf_op jit(solution)/shard_map/ppermute | solution.py:18
  103.7 13.1 %copy-start.2 = (bf16[1024,256]{1,0:T(8,128)(2,1)S(1)}, bf16[1024,256]{1,0:T(8,128)(2,1)}, u32[]{:S(2)}) copy-start(bf16[1024,256]{1,0:T(8,128)(2,1)} %cond_ref.1) | copy-start | bytes 1572868
  103.7 7.0 %collective-permute-start.20 = (bf16[2,192,256]{2,1,0:T(8,128)(2,1)S(1)}, bf16[2,192,256]{2,1,0:T(8,128)(2,1)S(1)}, u32[]{:S(2)}, u32[]{:S(2)}) collective-permute-start(bf16[2,192,256]{2,1,0:T(8,128)(2,1)S(1)} %slice.47), channel_id=1, source_target_pairs={{0,224},{32,0},{64,32},{96,64},{128,96},{160,128},{192,160},{224,1... | collective-permute-start | bytes 589832 | tf_op jit(solution)/shard_map/ppermute | solution.py:18
  112.0 2.0 %collective-permute-start.25 = (f32[48,256]{1,0:T(8,128)S(1)}, f32[48,256]{1,0:T(8,128)S(1)}, u32[]{:S(2)}, u32[]{:S(2)}) collective-permute-start(f32[48,256]{1,0:T(8,128)S(1)} %get-tuple-element.46), channel_id=1, source_target_pairs={{0,1},{1,0},{2,3},{3,2},{4,5},{5,4},{6,7},{7,6},{8,9},{9,8},{10,11... | collective-permute-start | bytes 147464 | tf_op jit(solution)/shard_map/ppermute | solution.py:194
  112.1 4.6 %collective-permute-start.26 = (f32[48,256]{1,0:T(8,128)S(1)}, f32[48,256]{1,0:T(8,128)S(1)}, u32[]{:S(2)}, u32[]{:S(2)}) collective-permute-start(f32[48,256]{1,0:T(8,128)S(1)} %get-tuple-element.47), channel_id=1, source_target_pairs={{0,2},{1,3},{2,0},{3,1},{4,6},{5,7},{6,4},{7,5},{8,10},{9,11},{10,... | collective-permute-start | bytes 147464 | tf_op jit(solution)/shard_map/ppermute | solution.py:194
  112.7 4.1 %collective-permute-start.27 = (f32[48,256]{1,0:T(8,128)S(1)}, f32[48,256]{1,0:T(8,128)S(1)}, u32[]{:S(2)}, u32[]{:S(2)}) collective-permute-start(f32[48,256]{1,0:T(8,128)S(1)} %get-tuple-element.48), channel_id=1, source_target_pairs={{0,3},{1,2},{2,1},{3,0},{4,7},{5,6},{6,5},{7,4},{8,11},{9,10},{10,... | collective-permute-start | bytes 147464 | tf_op jit(solution)/shard_map/ppermute | solution.py:194

commit v6 on v5

--- a/solution.py
+++ b/solution.py
@@ -168,8 +168,6 @@
     a1r, a1l, z2r, z2l, acc = lax.optimization_barrier((a1r, a1l, z2r, z2l, acc))
     z3r, z3l = shift(z2r, "z", NZ, 1), shift(z2l, "z", NZ, -1)
     z4 = shift(z2l, "z", NZ, -2)
-    acc = pair_call(me, screened, [a1r, a1l], [[(0, -1, d) for d in dys], [(0, 1, d) for d in dys]], acc)
-    z3r, z3l, z4, acc = lax.optimization_barrier((z3r, z3l, z4, acc))
     zb = [b, z1r, z1l, z2r, z2l, z3r, z3l, z4]
     sb0, sb1 = jnp.stack(zb[:4]), jnp.stack(zb[4:])
 
@@ -184,7 +182,7 @@
     sb1, br0, bl0 = lax.optimization_barrier((sb1, br0, bl0))
     br1, bl1 = shift(sb1, "y", NY, 1), shift(sb1, "y", NY, -1)
     a3r, a3l = shift(a2r, "z", NZ, 1), shift(a2l, "z", NZ, -1)
-    acc = pair_call(me, screened, [sb0, sb1, a2r, a2l], [at_b(0, 0), at_b(0, 1), at_a(-2), at_a(2)], acc)
+    acc = pair_call(me, screened, [a1r, a1l, sb0, sb1, a2r, a2l], [at_a(-1), at_a(1), at_b(0, 0), at_b(0, 1), at_a(-2), at_a(2)], acc)
     a3r, a3l, acc = lax.optimization_barrier((a3r, a3l, acc))
     a4r, a4l = shift(a3r[:2], "z", NZ, 1), shift(a3l[2:], "z", NZ, -1)
     b2r, b2l = shift(br0, "y", NY, 1), shift(bl1, "y", NY, -1)

time: 142 us -> 142 us (level)
  starting transfers between devices: 53.4 us -> 55.7 us
  waiting for transfers between devices: 33.4 us -> 31.9 us
    ppermute x25, starting transfers between devices: 40 us -> 42.3 us  [shift(): return lax.ppermute(x, axis, [(i, (i + d) % n) for i in range(n)])]
    ppermute x25, waiting for transfers between devices: 19.2 us -> 17.7 us  [shift(): return lax.ppermute(x, axis, [(i, (i + d) % n) for i in range(n)])]
    pallas_call x5 -> x4, Pallas kernels: 6.26 us -> 5.54 us  [pair_call(): pl.pallas_call(functools.partial(pair_kernel, places, acc is None, last),...]
  transfers between devices with their start and end apart: 29 -> 29, of which waited for: 10 -> 10; matrix products, arithmetic and copies ran while one was open for 2% -> 2% of each run, Pallas kernels for 4% -> 3%
where the time goes in v6:
time: 142 us; the launch traced here: 141 us
  starting transfers between devices  55.7 us (39%)
  waiting for transfers between devices  31.9 us (22%)
  blocking collectives  23.2 us (16%)
  between operations  15.4 us (11%)
  Pallas kernels  8.04 us (6%)
  local copies, waits for them, and re-layouts  6.24 us (4%)
    ppermute x25, starting transfers between devices, shift(): return lax.ppermute(x, axis, [(i, (i + d) % n) for i in range(n)])  42.3 us
    all_to_all x1, blocking collectives, body(): recv = lax.all_to_all(term, ('z', 'y', 'xh'), 0, 0, tiled=True)  23.2 us
    ppermute x25, waiting for transfers between devices, shift(): return lax.ppermute(x, axis, [(i, (i + d) % n) for i in range(n)])  17.7 us
    all_to_all x1, starting transfers between devices, body(): recv = lax.all_to_all(pack(valence), ('z', 'y'), 0, 0, tiled=True)  11.5 us
    all_to_all x1, waiting for transfers between devices, body(): recv = lax.all_to_all(pack(valence), ('z', 'y'), 0, 0, tiled=True)  11.3 us
    pallas_call x4, Pallas kernels, pair_call(): pl.pallas_call(functools.partial(pair_kernel, places, acc is None, last),...  5.54 us
    unnamed x11, local copies, waits for them, and re-layouts  4.65 us
    ppermute x3, waiting for transfers between devices, body(): lax.ppermute(parts[k], ('xl', 'c'), [(i, i ^ k) for i in range(NGP)])  2.87 us
  transfers between devices with their start and end apart: 29, of which 10 were waited for; matrix products, arithmetic and copies ran while one was open for 2% of the time, Pallas kernels for 3%

profile of v6, /device:TPU:2, one launch (start us, length us, event | category | flops | bytes accessed | tf_op | source)
XLA Modules:
  0.0 141.5 jit_solution(15017600097254207127)
XLA Ops:
  0.0 1.2 copy-done.1
  1.2 1.1 shard_map.46
  2.3 11.5 %all-to-all-start = ((bf16[32,32,512]{2,1,0:T(8,128)(2,1)}), bf16[32,32,512]{2,1,0:T(8,128)(2,1)S(1)}, u32[]{:S(2)}, u32[]{:S(2)}) async-start(bf16[32,32,512]{2,1,0:T(8,128)(2,1)} %shard_map.46), calls=%async_computation | async-start | bytes 2097152 | tf_op jit(solution)/shard_map/all_to_all | solution.py:153
  13.8 1.6 %fusion.2 = (s32[1]{0:T(128)}, s32[1]{0:T(128)}, s32[1]{0:T(128)}, s32[1]{0:T(128)}, s32[1]{0:T(128)}, /*index=5*/s32[1]{0:T(128)}) fusion(s32[6]{0:T(128)} %param.7), kind=kLoop, calls=%fused_computation.17 | loop fusion | bytes 48 | tf_op jit(solution)/shard_map/slice | solution.py:154
  30.5 11.3 %all-to-all-done = bf16[32,32,512]{2,1,0:T(8,128)(2,1)S(1)} async-done(((bf16[32,32,512]{2,1,0:T(8,128)(2,1)}), bf16[32,32,512]{2,1,0:T(8,128)(2,1)S(1)}, u32[]{:S(2)}, u32[]{:S(2)}) %all-to-all-start) | async-done | bytes 1048608 | tf_op jit(solution)/shard_map/all_to_all | solution.py:153
  41.9 2.2 %collective-permute-start = (bf16[6,32,512]{2,1,0:T(8,128)(2,1)S(1)}, bf16[6,32,512]{2,1,0:T(8,128)(2,1)S(1)}, u32[]{:S(2)}, u32[]{:S(2)}) collective-permute-start(bf16[6,32,512]{2,1,0:T(8,128)(2,1)S(1)} %dynamic-slice_dynamic-update-slice_fusion), channel_id=1, source_target_pairs={{0,4},{4,0},{1,5},{5,1},{2,6},{6,2},{3,7},{7,3},{8,12},{12,8},{9,1... | collective-permute-start | bytes 589832 | tf_op jit(solution)/shard_map/ppermute | solution.py:18
  44.2 0.7 fusion
  44.8 4.4 %collective-permute-done = bf16[6,32,512]{2,1,0:T(8,128)(2,1)S(1)} collective-permute-done((bf16[6,32,512]{2,1,0:T(8,128)(2,1)S(1)}, bf16[6,32,512]{2,1,0:T(8,128)(2,1)S(1)}, u32[]{:S(2)}, u32[]{:S(2)}) %collective-permute-start) | collective-permute-done | bytes 196640 | tf_op jit(solution)/shard_map/ppermute | solution.py:18
  49.2 0.1 slice_select_fusion
  49.3 1.8 %collective-permute-start.1 = (bf16[192,256]{1,0:T(8,128)(2,1)S(1)}, bf16[192,256]{1,0:T(8,128)(2,1)S(1)}, u32[]{:S(2)}, u32[]{:S(2)}) collective-permute-start(bf16[192,256]{1,0:T(8,128)(2,1)S(1)} %bitcast.26), channel_id=1, source_target_pairs={{0,8},{8,16},{16,24},{24,0},{1,9},{9,17},{17,25},{25,1},{2,10},{10... | collective-permute-start | bytes 294920 | tf_op jit(solution)/shard_map/ppermute | solution.py:18
  51.2 1.5 %collective-permute-start.2 = (bf16[192,256]{1,0:T(8,128)(2,1)S(1)}, bf16[192,256]{1,0:T(8,128)(2,1)S(1)}, u32[]{:S(2)}, u32[]{:S(2)}) collective-permute-start(bf16[192,256]{1,0:T(8,128)(2,1)S(1)} %bitcast.27), channel_id=1, source_target_pairs={{0,24},{8,0},{16,8},{24,16},{1,25},{9,1},{17,9},{25,17},{2,26},{10... | collective-permute-start | bytes 294920 | tf_op jit(solution)/shard_map/ppermute | solution.py:18
  52.6 2.1 %collective-permute-start.3 = (bf16[192,256]{1,0:T(8,128)(2,1)S(1)}, bf16[192,256]{1,0:T(8,128)(2,1)S(1)}, u32[]{:S(2)}, u32[]{:S(2)}) collective-permute-start(bf16[192,256]{1,0:T(8,128)(2,1)S(1)} %bitcast.28), channel_id=1, source_target_pairs={{0,16},{8,24},{16,0},{24,8},{1,17},{9,25},{17,1},{25,9},{2,18},{10... | collective-permute-start | bytes 294920 | tf_op jit(solution)/shard_map/ppermute | solution.py:18
  54.7 0.6 collective-permute-start.4
  55.3 2.6 %collective-permute-start.5 = (bf16[192,256]{1,0:T(8,128)(2,1)S(1)}, bf16[192,256]{1,0:T(8,128)(2,1)S(1)}, u32[]{:S(2)}, u32[]{:S(2)}) collective-permute-start(bf16[192,256]{1,0:T(8,128)(2,1)S(1)} %bitcast.24), channel_id=1, source_target_pairs={{0,224},{32,0},{64,32},{96,64},{128,96},{160,128},{192,160},{224,1... | collective-permute-start | bytes 294920 | tf_op jit(solution)/shard_map/ppermute | solution.py:18
  57.9 0.8 collective-permute-done.3
  58.8 2.6 %collective-permute-done.4 = bf16[192,256]{1,0:T(8,128)(2,1)S(1)} collective-permute-done((bf16[192,256]{1,0:T(8,128)(2,1)S(1)}, bf16[192,256]{1,0:T(8,128)(2,1)S(1)}, u32[]{:S(2)}, u32[]{:S(2)}) %collective-permute-start.4) | collective-permute-done | bytes 98336 | tf_op jit(solution)/shard_map/ppermute | solution.py:18
  61.4 3.4 %collective-permute-start.7 = (bf16[4,192,256]{2,1,0:T(8,128)(2,1)S(1)}, bf16[4,192,256]{2,1,0:T(8,128)(2,1)S(1)}, u32[]{:S(2)}, u32[]{:S(2)}) collective-permute-start(bf16[4,192,256]{2,1,0:T(8,128)(2,1)S(1)} %pad_maximum_fusion.refs_0_), channel_id=1, source_target_pairs={{0,224},{32,0},{64,32},{96,64},{128,96},{160,128},{192,160},{224,1... | collective-permute-start | bytes 1179656 | tf_op jit(solution)/shard_map/ppermute | solution.py:18
  64.8 3.2 %collective-permute-start.9 = (bf16[192,256]{1,0:T(8,128)(2,1)S(1)}, bf16[192,256]{1,0:T(8,128)(2,1)S(1)}, u32[]{:S(2)}, u32[]{:S(2)}) collective-permute-start(bf16[192,256]{1,0:T(8,128)(2,1)S(1)} %collective-permute-done.5), channel_id=1, source_target_pairs={{0,224},{32,0},{64,32},{96,64},{128,96},{160,128},{192,160},{224,1... | collective-permute-start | bytes 294920 | tf_op jit(solution)/shard_map/ppermute | solution.py:18
  68.0 0.1 pad_add_fusion.me_ref
  68.1 3.4 %copy-done = bf16[256,16384]{1,0:T(8,128)(2,1)S(1)} copy-done((bf16[256,16384]{1,0:T(8,128)(2,1)S(1)}, bf16[256,16384]{1,0:T(8,128)(2,1)}, u32[]{:S(2)}) %copy-start) | copy-done | bytes 8388632
  71.5 0.9 shard_map.47.refs_6_
  72.4 0.1 pad_maximum_fusion.1.refs_2_
  72.5 0.6 collective-permute-start.17
  73.1 2.7 %collective-permute-start.18 = (bf16[4,192,256]{2,1,0:T(8,128)(2,1)S(1)}, bf16[4,192,256]{2,1,0:T(8,128)(2,1)S(1)}, u32[]{:S(2)}, u32[]{:S(2)}) collective-permute-start(bf16[4,192,256]{2,1,0:T(8,128)(2,1)S(1)} %pad_maximum_fusion.1.refs_2_), channel_id=1, source_target_pairs={{0,24},{8,0},{16,8},{24,16},{1,25},{9,1},{17,9},{25,17},{2,26},{10... | collective-permute-start | bytes 1179656 | tf_op jit(solution)/shard_map/ppermute | solution.py:18
  75.8 3.2 %collective-permute-start.15 = (bf16[192,256]{1,0:T(8,128)(2,1)S(1)}, bf16[192,256]{1,0:T(8,128)(2,1)S(1)}, u32[]{:S(2)}, u32[]{:S(2)}) collective-permute-start(bf16[192,256]{1,0:T(8,128)(2,1)S(1)} %collective-permute-done.9), channel_id=1, source_target_pairs={{0,224},{32,0},{64,32},{96,64},{128,96},{160,128},{192,160},{224,1... | collective-permute-start | bytes 294920 | tf_op jit(solution)/shard_map/ppermute | solution.py:18
  79.1 1.5 %collective-permute-start.16 = (bf16[192,256]{1,0:T(8,128)(2,1)S(1)}, bf16[192,256]{1,0:T(8,128)(2,1)S(1)}, u32[]{:S(2)}, u32[]{:S(2)}) collective-permute-start(bf16[192,256]{1,0:T(8,128)(2,1)S(1)} %collective-permute-done.9), channel_id=1, source_target_pairs={{0,192},{32,224},{64,0},{96,32},{128,64},{160,96},{192,128},{224,1... | collective-permute-start | bytes 294920 | tf_op jit(solution)/shard_map/ppermute | solution.py:18
  80.5 1.8 %collective-permute-done.14 = bf16[192,256]{1,0:T(8,128)(2,1)S(1)} collective-permute-done((bf16[192,256]{1,0:T(8,128)(2,1)S(1)}, bf16[192,256]{1,0:T(8,128)(2,1)S(1)}, u32[]{:S(2)}, u32[]{:S(2)}) %collective-permute-start.14) | collective-permute-done | bytes 98336 | tf_op jit(solution)/shard_map/ppermute | solution.py:18
  82.3 3.2 %collective-permute-start.12 = (bf16[4,192,256]{2,1,0:T(8,128)(2,1)S(1)}, bf16[4,192,256]{2,1,0:T(8,128)(2,1)S(1)}, u32[]{:S(2)}, u32[]{:S(2)}) collective-permute-start(bf16[4,192,256]{2,1,0:T(8,128)(2,1)S(1)} %collective-permute-done.7.refs_1_), channel_id=1, source_target_pairs={{0,224},{32,0},{64,32},{96,64},{128,96},{160,128},{192,160},{224,1... | collective-permute-start | bytes 1179656 | tf_op jit(solution)/shard_map/ppermute | solution.py:18
  85.7 3.1 %collective-permute-start.22 = (bf16[4,192,256]{2,1,0:T(8,128)(2,1)S(1)}, bf16[4,192,256]{2,1,0:T(8,128)(2,1)S(1)}, u32[]{:S(2)}, u32[]{:S(2)}) collective-permute-start(bf16[4,192,256]{2,1,0:T(8,128)(2,1)S(1)} %pad_maximum_fusion.2.refs_3_), channel_id=1, source_target_pairs={{0,24},{8,0},{16,8},{24,16},{1,25},{9,1},{17,9},{25,17},{2,26},{10... | collective-permute-start | bytes 1179656 | tf_op jit(solution)/shard_map/ppermute | solution.py:18
  88.7 5.5 %collective-permute-done.10.refs_4_ = bf16[4,192,256]{2,1,0:T(8,128)(2,1)S(1)} collective-permute-done((bf16[4,192,256]{2,1,0:T(8,128)(2,1)S(1)}, bf16[4,192,256]{2,1,0:T(8,128)(2,1)S(1)}, u32[]{:S(2)}, u32[]{:S(2)}) %collective-permute-start.10) | collective-permute-done | bytes 393248 | tf_op jit(solution)/shard_map/ppermute | solution.py:18
  94.3 3.2 %collective-permute-start.13 = (bf16[4,192,256]{2,1,0:T(8,128)(2,1)S(1)}, bf16[4,192,256]{2,1,0:T(8,128)(2,1)S(1)}, u32[]{:S(2)}, u32[]{:S(2)}) collective-permute-start(bf16[4,192,256]{2,1,0:T(8,128)(2,1)S(1)} %collective-permute-done.12.refs_5_), channel_id=1, source_target_pairs={{0,224},{32,0},{64,32},{96,64},{128,96},{160,128},{192,160},{224,1... | collective-permute-start | bytes 1179656 | tf_op jit(solution)/shard_map/ppermute | solution.py:18
  97.5 0.2 collective-permute-start.24
  97.8 3.6 %collective-permute-start.23 = (bf16[4,192,256]{2,1,0:T(8,128)(2,1)S(1)}, bf16[4,192,256]{2,1,0:T(8,128)(2,1)S(1)}, u32[]{:S(2)}, u32[]{:S(2)}) collective-permute-start(bf16[4,192,256]{2,1,0:T(8,128)(2,1)S(1)} %collective-permute-done.22.refs_5_), channel_id=1, source_target_pairs={{0,24},{8,0},{16,8},{24,16},{1,25},{9,1},{17,9},{25,17},{2,26},{10... | collective-permute-start | bytes 1179656 | tf_op jit(solution)/shard_map/ppermute | solution.py:18
  101.4 1.7 %shard_map.48.refs_6_ = f32[192,256]{1,0:T(8,128)S(1)} custom-call(s32[3]{0:T(128)S(1)} %pad_add_fusion.me_ref, bf16[256,16384]{1,0:T(8,128)(2,1)S(1)} %copy-done, bf16[4,192,256]{2,1,0:T(8,128)(2,1)S(1)} %collective-permute-done.6.refs_0_, bf16[4,192,256]{2,1,0:T(8,128)(2,1)S(1)} %collective-permute-done.7.refs_1_, ...), custom_call_target="tpu_custom_call" | custom-call | flops 603979776 | bytes 5505024 | tf_op jit(solution)/shard_map/pallas_call | solution.py:71
  103.1 0.5 collective-permute-done.11.refs_0_
  103.6 0.1 collective-permute-start.19
  103.7 3.3 %collective-permute-start.20 = (bf16[2,192,256]{2,1,0:T(8,128)(2,1)S(1)}, bf16[2,192,256]{2,1,0:T(8,128)(2,1)S(1)}, u32[]{:S(2)}, u32[]{:S(2)}) collective-permute-start(bf16[2,192,256]{2,1,0:T(8,128)(2,1)S(1)} %slice.47), channel_id=1, source_target_pairs={{0,224},{32,0},{64,32},{96,64},{128,96},{160,128},{192,160},{224,1... | collective-permute-start | bytes 589832 | tf_op jit(solution)/shard_map/ppermute | solution.py:18
  107.0 1.7 %shard_map.49.refs_4_ = f32[192,256]{1,0:T(8,128)S(1)} custom-call(s32[3]{0:T(128)S(1)} %pad_add_fusion.me_ref, bf16[256,16384]{1,0:T(8,128)(2,1)S(1)} %copy-done, bf16[4,192,256]{2,1,0:T(8,128)(2,1)S(1)} %collective-permute-done.11.refs_0_, bf16[4,192,256]{2,1,0:T(8,128)(2,1)S(1)} %collective-permute-done.13.refs_1_, ...), custom_call_target="tpu_custom_call" | custom-call | flops 603979776 | bytes 5505024 | tf_op jit(solution)/shard_map/pallas_call | solution.py:71
  108.7 2.0 %collective-permute-done.21.refs_2_ = bf16[4,192,256]{2,1,0:T(8,128)(2,1)S(1)} collective-permute-done((bf16[4,192,256]{2,1,0:T(8,128)(2,1)S(1)}, bf16[4,192,256]{2,1,0:T(8,128)(2,1)S(1)}, u32[]{:S(2)}, u32[]{:S(2)}) %collective-permute-start.21) | collective-permute-done | bytes 393248 | tf_op jit(solution)/shard_map/ppermute | solution.py:18
  110.7 1.2 shard_map.50
  112.0 0.1 collective-permute-start.25
  112.1 0.6 collective-permute-start.26
  112.7 1.2 collective-permute-start.27
  113.9 2.8 %collective-permute-done.26.c_ref = f32[48,256]{1,0:T(8,128)S(1)} collective-permute-done((f32[48,256]{1,0:T(8,128)S(1)}, f32[48,256]{1,0:T(8,128)S(1)}, u32[]{:S(2)}, u32[]{:S(2)}) %collective-permute-start.26) | collective-permute-done | bytes 49184 | tf_op jit(solution)/shard_map/ppermute | solution.py:192
  116.7 0.1 collective-permute-done.27.d_ref
  116.8 0.6 shard_map.51
  117.4 23.2 %all_to_all.10.x_ref = f32[64,8,128]{2,1,0:T(8,128)S(1)} all-to-all(f32[64,8,128]{2,1,0:T(8,128)S(1)} %shard_map.51), channel_id=1, replica_groups=mesh['z'=8,'y'=4,'xh'=2,'xl'=2,'c'=2] {'z','y','xh'}, dimensions={0} | all-to-all | bytes 524288 | tf_op jit(solution)/shard_map/all_to_all | solution.py:195
  140.6 0.8 shard_map.52
  (39 shorter events, 0.3 us)
Async XLA Ops:
  0.0 1.2 copy-start.1
  2.3 39.6 %all-to-all-start = ((bf16[32,32,512]{2,1,0:T(8,128)(2,1)}), bf16[32,32,512]{2,1,0:T(8,128)(2,1)S(1)}, u32[]{:S(2)}, u32[]{:S(2)}) async-start(bf16[32,32,512]{2,1,0:T(8,128)(2,1)} %shard_map.46), calls=%async_computation | async-start | bytes 2097152 | tf_op jit(solution)/shard_map/all_to_all | solution.py:153
  41.9 7.3 %collective-permute-start = (bf16[6,32,512]{2,1,0:T(8,128)(2,1)S(1)}, bf16[6,32,512]{2,1,0:T(8,128)(2,1)S(1)}, u32[]{:S(2)}, u32[]{:S(2)}) collective-permute-start(bf16[6,32,512]{2,1,0:T(8,128)(2,1)S(1)} %dynamic-slice_dynamic-update-slice_fusion), channel_id=1, source_target_pairs={{0,4},{4,0},{1,5},{5,1},{2,6},{6,2},{3,7},{7,3},{8,12},{12,8},{9,1... | collective-permute-start | bytes 589832 | tf_op jit(solution)/shard_map/ppermute | solution.py:18
  49.3 8.6 %collective-permute-start.1 = (bf16[192,256]{1,0:T(8,128)(2,1)S(1)}, bf16[192,256]{1,0:T(8,128)(2,1)S(1)}, u32[]{:S(2)}, u32[]{:S(2)}) collective-permute-start(bf16[192,256]{1,0:T(8,128)(2,1)S(1)} %bitcast.26), channel_id=1, source_target_pairs={{0,8},{8,16},{16,24},{24,0},{1,9},{9,17},{17,25},{25,1},{2,10},{10... | collective-permute-start | bytes 294920 | tf_op jit(solution)/shard_map/ppermute | solution.py:18
  51.2 6.8 %collective-permute-start.2 = (bf16[192,256]{1,0:T(8,128)(2,1)S(1)}, bf16[192,256]{1,0:T(8,128)(2,1)S(1)}, u32[]{:S(2)}, u32[]{:S(2)}) collective-permute-start(bf16[192,256]{1,0:T(8,128)(2,1)S(1)} %bitcast.27), channel_id=1, source_target_pairs={{0,24},{8,0},{16,8},{24,16},{1,25},{9,1},{17,9},{25,17},{2,26},{10... | collective-permute-start | bytes 294920 | tf_op jit(solution)/shard_map/ppermute | solution.py:18
  52.6 6.1 %collective-permute-start.3 = (bf16[192,256]{1,0:T(8,128)(2,1)S(1)}, bf16[192,256]{1,0:T(8,128)(2,1)S(1)}, u32[]{:S(2)}, u32[]{:S(2)}) collective-permute-start(bf16[192,256]{1,0:T(8,128)(2,1)S(1)} %bitcast.28), channel_id=1, source_target_pairs={{0,16},{8,24},{16,0},{24,8},{1,17},{9,25},{17,1},{25,9},{2,18},{10... | collective-permute-start | bytes 294920 | tf_op jit(solution)/shard_map/ppermute | solution.py:18
  54.7 6.7 %collective-permute-start.4 = (bf16[192,256]{1,0:T(8,128)(2,1)S(1)}, bf16[192,256]{1,0:T(8,128)(2,1)S(1)}, u32[]{:S(2)}, u32[]{:S(2)}) collective-permute-start(bf16[192,256]{1,0:T(8,128)(2,1)S(1)} %bitcast.23), channel_id=1, source_target_pairs={{0,32},{32,64},{64,96},{96,128},{128,160},{160,192},{192,224},{224... | collective-permute-start | bytes 294920 | tf_op jit(solution)/shard_map/ppermute | solution.py:18
  55.3 6.1 %collective-permute-start.5 = (bf16[192,256]{1,0:T(8,128)(2,1)S(1)}, bf16[192,256]{1,0:T(8,128)(2,1)S(1)}, u32[]{:S(2)}, u32[]{:S(2)}) collective-permute-start(bf16[192,256]{1,0:T(8,128)(2,1)S(1)} %bitcast.24), channel_id=1, source_target_pairs={{0,224},{32,0},{64,32},{96,64},{128,96},{160,128},{192,160},{224,1... | collective-permute-start | bytes 294920 | tf_op jit(solution)/shard_map/ppermute | solution.py:18
  61.4 11.0 %collective-permute-start.6 = (bf16[4,192,256]{2,1,0:T(8,128)(2,1)S(1)}, bf16[4,192,256]{2,1,0:T(8,128)(2,1)S(1)}, u32[]{:S(2)}, u32[]{:S(2)}) collective-permute-start(bf16[4,192,256]{2,1,0:T(8,128)(2,1)S(1)} %pad_maximum_fusion.refs_0_), channel_id=1, source_target_pairs={{0,32},{32,64},{64,96},{96,128},{128,160},{160,192},{192,224},{224... | collective-permute-start | bytes 1179656 | tf_op jit(solution)/shard_map/ppermute | solution.py:18
  61.4 11.0 %collective-permute-start.7 = (bf16[4,192,256]{2,1,0:T(8,128)(2,1)S(1)}, bf16[4,192,256]{2,1,0:T(8,128)(2,1)S(1)}, u32[]{:S(2)}, u32[]{:S(2)}) collective-permute-start(bf16[4,192,256]{2,1,0:T(8,128)(2,1)S(1)} %pad_maximum_fusion.refs_0_), channel_id=1, source_target_pairs={{0,224},{32,0},{64,32},{96,64},{128,96},{160,128},{192,160},{224,1... | collective-permute-start | bytes 1179656 | tf_op jit(solution)/shard_map/ppermute | solution.py:18
  64.8 7.6 %collective-permute-start.8 = (bf16[192,256]{1,0:T(8,128)(2,1)S(1)}, bf16[192,256]{1,0:T(8,128)(2,1)S(1)}, u32[]{:S(2)}, u32[]{:S(2)}) collective-permute-start(bf16[192,256]{1,0:T(8,128)(2,1)S(1)} %collective-permute-done.4), channel_id=1, source_target_pairs={{0,32},{32,64},{64,96},{96,128},{128,160},{160,192},{192,224},{224... | collective-permute-start | bytes 294920 | tf_op jit(solution)/shard_map/ppermute | solution.py:18
  64.8 7.6 %collective-permute-start.9 = (bf16[192,256]{1,0:T(8,128)(2,1)S(1)}, bf16[192,256]{1,0:T(8,128)(2,1)S(1)}, u32[]{:S(2)}, u32[]{:S(2)}) collective-permute-start(bf16[192,256]{1,0:T(8,128)(2,1)S(1)} %collective-permute-done.5), channel_id=1, source_target_pairs={{0,224},{32,0},{64,32},{96,64},{128,96},{160,128},{192,160},{224,1... | collective-permute-start | bytes 294920 | tf_op jit(solution)/shard_map/ppermute | solution.py:18
  68.1 3.4 %copy-start = (bf16[256,16384]{1,0:T(8,128)(2,1)S(1)}, bf16[256,16384]{1,0:T(8,128)(2,1)}, u32[]{:S(2)}) copy-start(bf16[256,16384]{1,0:T(8,128)(2,1)} %w_ref.7) | copy-start | bytes 25165828
  72.5 13.1 %collective-permute-start.17 = (bf16[4,192,256]{2,1,0:T(8,128)(2,1)S(1)}, bf16[4,192,256]{2,1,0:T(8,128)(2,1)S(1)}, u32[]{:S(2)}, u32[]{:S(2)}) collective-permute-start(bf16[4,192,256]{2,1,0:T(8,128)(2,1)S(1)} %pad_maximum_fusion.1.refs_2_), channel_id=1, source_target_pairs={{0,8},{8,16},{16,24},{24,0},{1,9},{9,17},{17,25},{25,1},{2,10},{10... | collective-permute-start | bytes 1179656 | tf_op jit(solution)/shard_map/ppermute | solution.py:18
  73.1 12.5 %collective-permute-start.18 = (bf16[4,192,256]{2,1,0:T(8,128)(2,1)S(1)}, bf16[4,192,256]{2,1,0:T(8,128)(2,1)S(1)}, u32[]{:S(2)}, u32[]{:S(2)}) collective-permute-start(bf16[4,192,256]{2,1,0:T(8,128)(2,1)S(1)} %pad_maximum_fusion.1.refs_2_), channel_id=1, source_target_pairs={{0,24},{8,0},{16,8},{24,16},{1,25},{9,1},{17,9},{25,17},{2,26},{10... | collective-permute-start | bytes 1179656 | tf_op jit(solution)/shard_map/ppermute | solution.py:18
  75.8 6.5 %collective-permute-start.14 = (bf16[192,256]{1,0:T(8,128)(2,1)S(1)}, bf16[192,256]{1,0:T(8,128)(2,1)S(1)}, u32[]{:S(2)}, u32[]{:S(2)}) collective-permute-start(bf16[192,256]{1,0:T(8,128)(2,1)S(1)} %collective-permute-done.8), channel_id=1, source_target_pairs={{0,32},{32,64},{64,96},{96,128},{128,160},{160,192},{192,224},{224... | collective-permute-start | bytes 294920 | tf_op jit(solution)/shard_map/ppermute | solution.py:18
  75.8 6.5 %collective-permute-start.15 = (bf16[192,256]{1,0:T(8,128)(2,1)S(1)}, bf16[192,256]{1,0:T(8,128)(2,1)S(1)}, u32[]{:S(2)}, u32[]{:S(2)}) collective-permute-start(bf16[192,256]{1,0:T(8,128)(2,1)S(1)} %collective-permute-done.9), channel_id=1, source_target_pairs={{0,224},{32,0},{64,32},{96,64},{128,96},{160,128},{192,160},{224,1... | collective-permute-start | bytes 294920 | tf_op jit(solution)/shard_map/ppermute | solution.py:18
  79.1 6.5 %collective-permute-start.16 = (bf16[192,256]{1,0:T(8,128)(2,1)S(1)}, bf16[192,256]{1,0:T(8,128)(2,1)S(1)}, u32[]{:S(2)}, u32[]{:S(2)}) collective-permute-start(bf16[192,256]{1,0:T(8,128)(2,1)S(1)} %collective-permute-done.9), channel_id=1, source_target_pairs={{0,192},{32,224},{64,0},{96,32},{128,64},{160,96},{192,128},{224,1... | collective-permute-start | bytes 294920 | tf_op jit(solution)/shard_map/ppermute | solution.py:18
  82.3 11.9 %collective-permute-start.10 = (bf16[4,192,256]{2,1,0:T(8,128)(2,1)S(1)}, bf16[4,192,256]{2,1,0:T(8,128)(2,1)S(1)}, u32[]{:S(2)}, u32[]{:S(2)}) collective-permute-start(bf16[4,192,256]{2,1,0:T(8,128)(2,1)S(1)} %collective-permute-done.6.refs_0_), channel_id=1, source_target_pairs={{0,32},{32,64},{64,96},{96,128},{128,160},{160,192},{192,224},{224... | collective-permute-start | bytes 1179656 | tf_op jit(solution)/shard_map/ppermute | solution.py:18
  82.3 11.9 %collective-permute-start.12 = (bf16[4,192,256]{2,1,0:T(8,128)(2,1)S(1)}, bf16[4,192,256]{2,1,0:T(8,128)(2,1)S(1)}, u32[]{:S(2)}, u32[]{:S(2)}) collective-permute-start(bf16[4,192,256]{2,1,0:T(8,128)(2,1)S(1)} %collective-permute-done.7.refs_1_), channel_id=1, source_target_pairs={{0,224},{32,0},{64,32},{96,64},{128,96},{160,128},{192,160},{224,1... | collective-permute-start | bytes 1179656 | tf_op jit(solution)/shard_map/ppermute | solution.py:18
  85.7 12.1 %collective-permute-start.22 = (bf16[4,192,256]{2,1,0:T(8,128)(2,1)S(1)}, bf16[4,192,256]{2,1,0:T(8,128)(2,1)S(1)}, u32[]{:S(2)}, u32[]{:S(2)}) collective-permute-start(bf16[4,192,256]{2,1,0:T(8,128)(2,1)S(1)} %pad_maximum_fusion.2.refs_3_), channel_id=1, source_target_pairs={{0,24},{8,0},{16,8},{24,16},{1,25},{9,1},{17,9},{25,17},{2,26},{10... | collective-permute-start | bytes 1179656 | tf_op jit(solution)/shard_map/ppermute | solution.py:18
  94.3 9.3 %collective-permute-start.11 = (bf16[4,192,256]{2,1,0:T(8,128)(2,1)S(1)}, bf16[4,192,256]{2,1,0:T(8,128)(2,1)S(1)}, u32[]{:S(2)}, u32[]{:S(2)}) collective-permute-start(bf16[4,192,256]{2,1,0:T(8,128)(2,1)S(1)} %collective-permute-done.10.refs_4_), channel_id=1, source_target_pairs={{0,32},{32,64},{64,96},{96,128},{128,160},{160,192},{192,224},{224... | collective-permute-start | bytes 1179656 | tf_op jit(solution)/shard_map/ppermute | solution.py:18
  94.3 9.3 %collective-permute-start.13 = (bf16[4,192,256]{2,1,0:T(8,128)(2,1)S(1)}, bf16[4,192,256]{2,1,0:T(8,128)(2,1)S(1)}, u32[]{:S(2)}, u32[]{:S(2)}) collective-permute-start(bf16[4,192,256]{2,1,0:T(8,128)(2,1)S(1)} %collective-permute-done.12.refs_5_), channel_id=1, source_target_pairs={{0,224},{32,0},{64,32},{96,64},{128,96},{160,128},{192,160},{224,1... | collective-permute-start | bytes 1179656 | tf_op jit(solution)/shard_map/ppermute | solution.py:18
  97.5 9.5 %collective-permute-start.24 = (bf16[4,192,256]{2,1,0:T(8,128)(2,1)S(1)}, bf16[4,192,256]{2,1,0:T(8,128)(2,1)S(1)}, u32[]{:S(2)}, u32[]{:S(2)}) collective-permute-start(bf16[4,192,256]{2,1,0:T(8,128)(2,1)S(1)} %pad_maximum_fusion.2.refs_3_), channel_id=1, source_target_pairs={{0,8},{8,16},{16,24},{24,0},{1,9},{9,17},{17,25},{25,1},{2,10},{10... | collective-permute-start | bytes 1179656 | tf_op jit(solution)/shard_map/ppermute | solution.py:18
  97.7 13.0 %collective-permute-start.21 = (bf16[4,192,256]{2,1,0:T(8,128)(2,1)S(1)}, bf16[4,192,256]{2,1,0:T(8,128)(2,1)S(1)}, u32[]{:S(2)}, u32[]{:S(2)}) collective-permute-start(bf16[4,192,256]{2,1,0:T(8,128)(2,1)S(1)} %collective-permute-done.17.refs_2_), channel_id=1, source_target_pairs={{0,8},{8,16},{16,24},{24,0},{1,9},{9,17},{17,25},{25,1},{2,10},{10... | collective-permute-start | bytes 1179656 | tf_op jit(solution)/shard_map/ppermute | solution.py:18
  97.8 13.0 %collective-permute-start.23 = (bf16[4,192,256]{2,1,0:T(8,128)(2,1)S(1)}, bf16[4,192,256]{2,1,0:T(8,128)(2,1)S(1)}, u32[]{:S(2)}, u32[]{:S(2)}) collective-permute-start(bf16[4,192,256]{2,1,0:T(8,128)(2,1)S(1)} %collective-permute-done.22.refs_5_), channel_id=1, source_target_pairs={{0,24},{8,0},{16,8},{24,16},{1,25},{9,1},{17,9},{25,17},{2,26},{10... | collective-permute-start | bytes 1179656 | tf_op jit(solution)/shard_map/ppermute | solution.py:18
  103.6 7.1 %collective-permute-start.19 = (bf16[2,192,256]{2,1,0:T(8,128)(2,1)S(1)}, bf16[2,192,256]{2,1,0:T(8,128)(2,1)S(1)}, u32[]{:S(2)}, u32[]{:S(2)}) collective-permute-start(bf16[2,192,256]{2,1,0:T(8,128)(2,1)S(1)} %slice.46), channel_id=1, source_target_pairs={{0,32},{32,64},{64,96},{96,128},{128,160},{160,192},{192,224},{224... | collective-permute-start | bytes 589832 | tf_op jit(solution)/shard_map/ppermute | solution.py:18
  103.7 13.1 %copy-start.2 = (bf16[1024,256]{1,0:T(8,128)(2,1)S(1)}, bf16[1024,256]{1,0:T(8,128)(2,1)}, u32[]{:S(2)}) copy-start(bf16[1024,256]{1,0:T(8,128)(2,1)} %cond_ref.1) | copy-start | bytes 1572868
  103.7 7.0 %collective-permute-start.20 = (bf16[2,192,256]{2,1,0:T(8,128)(2,1)S(1)}, bf16[2,192,256]{2,1,0:T(8,128)(2,1)S(1)}, u32[]{:S(2)}, u32[]{:S(2)}) collective-permute-start(bf16[2,192,256]{2,1,0:T(8,128)(2,1)S(1)} %slice.47), channel_id=1, source_target_pairs={{0,224},{32,0},{64,32},{96,64},{128,96},{160,128},{192,160},{224,1... | collective-permute-start | bytes 589832 | tf_op jit(solution)/shard_map/ppermute | solution.py:18
  112.0 2.0 %collective-permute-start.25 = (f32[48,256]{1,0:T(8,128)S(1)}, f32[48,256]{1,0:T(8,128)S(1)}, u32[]{:S(2)}, u32[]{:S(2)}) collective-permute-start(f32[48,256]{1,0:T(8,128)S(1)} %get-tuple-element.38), channel_id=1, source_target_pairs={{0,1},{1,0},{2,3},{3,2},{4,5},{5,4},{6,7},{7,6},{8,9},{9,8},{10,11... | collective-permute-start | bytes 147464 | tf_op jit(solution)/shard_map/ppermute | solution.py:192
  112.1 4.6 %collective-permute-start.26 = (f32[48,256]{1,0:T(8,128)S(1)}, f32[48,256]{1,0:T(8,128)S(1)}, u32[]{:S(2)}, u32[]{:S(2)}) collective-permute-start(f32[48,256]{1,0:T(8,128)S(1)} %get-tuple-element.39), channel_id=1, source_target_pairs={{0,2},{1,3},{2,0},{3,1},{4,6},{5,7},{6,4},{7,5},{8,10},{9,11},{10,... | collective-permute-start | bytes 147464 | tf_op jit(solution)/shard_map/ppermute | solution.py:192
  112.7 4.1 %collective-permute-start.27 = (f32[48,256]{1,0:T(8,128)S(1)}, f32[48,256]{1,0:T(8,128)S(1)}, u32[]{:S(2)}, u32[]{:S(2)}) collective-permute-start(f32[48,256]{1,0:T(8,128)S(1)} %get-tuple-element.40), channel_id=1, source_target_pairs={{0,3},{1,2},{2,1},{3,0},{4,7},{5,6},{6,5},{7,4},{8,11},{9,10},{10,... | collective-permute-start | bytes 147464 | tf_op jit(solution)/shard_map/ppermute | solution.py:192
